TPU v7x, 32 devices: a whole 2x2x4 slice. The times are simulated.
32 devices in a mesh: th: 4 (over z), ph: 8 (over y, x, core).
Axes of the slice: x: 2, y: 2, z: 4, core: 2. Of those that a mesh axis runs over, the one named last changes fastest.
Arguments:
- state: float32 [8, 96, 192, 256], P(None, 'th', 'ph'), may hold values from -1 to 7.5, as said below
- cotangent: float32 [8, 96, 192, 256], P(None, 'th', 'ph'), may hold values from -6 to 6
Outputs:
- sensitivity: float32 [8, 96, 192, 256], P(None, 'th', 'ph')
Inputs may be any that keep to these rules, and one draw needn't show every extreme that they name: `state`: component 0 is density in 0.5 to 2, components 1 to 3 momenta and 5 to 7 magnetic face fields in -1 to 1, component 4 total energy, which exceeds the kinetic energy by 2 or more.
All inputs are finite; a program needn't handle non-finite values.
Results may differ from a plain program's by a relative error of at most 0.0003.
Values sent between devices are 32-bit elements; how exact they have to be, the bound alone decides.
No kernel may reach another device: no remote copies, remote signals or barrier semaphores. Data moves between devices by JAX's collectives and lax.ppermute only.
A program may use at most 512 MiB of HBM per device.

v0:
```python
import math

import jax
import jax.numpy as jnp
from jax import lax
from jax.sharding import PartitionSpec as P

GAMMA = 5.0 / 3.0
R_INNER = 1.0
R_OUTER = 3.0
COURANT = 0.4
SPEED_BOUND = 5.0
PRESSURE_SOFT = 0.05
THETA_CUT = 0.1


def from_behind(block, axis, distance):
    devices = range(lax.axis_size(axis))
    route = [((i - distance) % len(devices), i) for i in devices]
    return lax.ppermute(block, axis, route)


def padded_2(value, sides, width, wrap):
    for axis, dim in sides:
        size, length = (lax.axis_size(axis), value.shape[dim])
        up = [(i, (i + 1) % size) for i in range(size if wrap else size - 1)]
        down = [(j, i) for i, j in up]
        last = lax.slice_in_dim(value, length - width, length, axis=dim)
        first = lax.slice_in_dim(value, 0, width, axis=dim)
        before = lax.ppermute(last, axis, up)
        after = lax.ppermute(first, axis, down)
        value = jnp.concatenate([before, value, after], axis=dim)
    return value


def lower_part(values, dim_index):
    return lax.slice_in_dim(values, 0, values.shape[dim_index] - 1, axis=dim_index)


def upper_part(values, dim_index):
    return lax.slice_in_dim(values, 1, values.shape[dim_index], axis=dim_index)


def time_step(total_cols, rad_count):
    step_phi = 2.0 * math.pi / total_cols
    step_radius = (R_OUTER - R_INNER) / rad_count
    return COURANT * min(step_radius, R_INNER * math.sin(THETA_CUT) * step_phi) / SPEED_BOUND


def section_rate(padded, row_start, total_rows, total_cols):
    row_count = padded.shape[1] - 4
    col_count = padded.shape[2] - 4
    rad_count = padded.shape[3]
    step_theta = (math.pi - 2.0 * THETA_CUT) / total_rows
    step_phi = 2.0 * math.pi / total_cols
    step_radius = (R_OUTER - R_INNER) / rad_count
    grid_vals = jnp.pad(padded, ((0, 0), (0, 0), (0, 0), (2, 2)), mode="edge")
    face_rows = row_start + jnp.arange(row_count + 4, dtype=jnp.int32) - 2
    keep_mask = jnp.where((face_rows != 0) & (face_rows != total_rows), 1.0, 0.0).astype(
        jnp.float32
    )
    polar_faces = grid_vals[6] * keep_mask[:, None, None]
    density = grid_vals[0, :-1, :-1, :-1]
    momentum = grid_vals[1:4, :-1, :-1, :-1]
    energy = grid_vals[4, :-1, :-1, :-1]
    b_radial = 0.5 * (grid_vals[5, :-1, :-1, :-1] + grid_vals[5, :-1, :-1, 1:])
    b_polar = 0.5 * (polar_faces[:-1, :-1, :-1] + polar_faces[1:, :-1, :-1])
    b_azimuth = 0.5 * (grid_vals[7, :-1, :-1, :-1] + grid_vals[7, :-1, 1:, :-1])
    magnet = jnp.stack([b_radial, b_polar, b_azimuth])
    velocity = momentum / density
    field_square = jnp.sum(magnet * magnet, 0)
    pressure = (GAMMA - 1.0) * (energy - 0.5 * jnp.sum(momentum * velocity, 0) - 0.5 * field_square)
    total_p = pressure + 0.5 * field_square
    sound_sq = (
        GAMMA * jnp.sqrt(pressure * pressure + PRESSURE_SOFT * PRESSURE_SOFT) + field_square
    ) / density
    vel_dot_field = jnp.sum(velocity * magnet, 0)
    conserved = jnp.concatenate([density[None], momentum, energy[None]], 0)

    def face_flux(normal):
        dim_index = (3, 1, 2)[normal]
        normal_vel = velocity[normal]
        normal_field = magnet[normal]
        pieces = [density * normal_vel]
        for component in range(3):
            addend = momentum[component] * normal_vel - magnet[component] * normal_field
            if component == normal:
                addend = addend + total_p
            pieces.append(addend)
        pieces.append((energy + total_p) * normal_vel - normal_field * vel_dot_field)
        flux_vals = jnp.stack(pieces)
        speed_sq = normal_vel * normal_vel + sound_sq
        viscosity = jnp.sqrt(
            0.5 * (lower_part(speed_sq, dim_index - 1) + upper_part(speed_sq, dim_index - 1))
        )
        return 0.5 * (
            lower_part(flux_vals, dim_index) + upper_part(flux_vals, dim_index)
        ) - 0.5 * viscosity * (upper_part(conserved, dim_index) - lower_part(conserved, dim_index))

    flux_radial = face_flux(0)
    flux_polar = face_flux(1)
    flux_azimuth = face_flux(2)
    jrow, kcol, irad = (row_count, col_count, rad_count)
    row_pos = (row_start + jnp.arange(row_count, dtype=jnp.int32)).astype(jnp.float32)
    theta_low = (THETA_CUT + row_pos * step_theta)[:, None, None]
    theta_high = theta_low + step_theta
    theta_mid = theta_low + 0.5 * step_theta
    radius_low = (R_INNER + jnp.arange(rad_count, dtype=jnp.float32) * step_radius)[None, None, :]
    radius_high = radius_low + step_radius
    radius_mid = radius_low + 0.5 * step_radius
    sine_low = jnp.sin(theta_low)
    sine_high = jnp.sin(theta_high)
    cos_diff = jnp.cos(theta_low) - jnp.cos(theta_high)
    shell_area = 0.5 * (radius_high * radius_high - radius_low * radius_low)
    volume = (radius_high**3 - radius_low**3) / 3.0 * cos_diff * step_phi
    area_rad_low = radius_low * radius_low * cos_diff * step_phi
    area_rad_high = radius_high * radius_high * cos_diff * step_phi
    area_pol_low = sine_low * shell_area * step_phi
    area_pol_high = sine_high * shell_area * step_phi
    area_azim = shell_area * step_theta
    net_flow = (
        area_rad_high * flux_radial[:, 2 : jrow + 2, 2 : kcol + 2, 2 : irad + 2]
        - area_rad_low * flux_radial[:, 2 : jrow + 2, 2 : kcol + 2, 1 : irad + 1]
        + area_pol_high * flux_polar[:, 2 : jrow + 2, 2 : kcol + 2, 2 : irad + 2]
        - area_pol_low * flux_polar[:, 1 : jrow + 1, 2 : kcol + 2, 2 : irad + 2]
        + area_azim
        * (
            flux_azimuth[:, 2 : jrow + 2, 2 : kcol + 2, 2 : irad + 2]
            - flux_azimuth[:, 2 : jrow + 2, 1 : kcol + 1, 2 : irad + 2]
        )
    )

    def interior(values):
        return values[..., 2 : jrow + 2, 2 : kcol + 2, 2 : irad + 2]

    rho_in = interior(density)
    vel_in = interior(velocity)
    mag_in = interior(magnet)
    press_in = interior(total_p)
    cotan_mid = jnp.cos(theta_mid) / jnp.sin(theta_mid)
    source_rad = (
        rho_in * (vel_in[1] ** 2 + vel_in[2] ** 2)
        - (mag_in[1] ** 2 + mag_in[2] ** 2)
        + 2.0 * press_in
    ) / radius_mid
    source_pol = (
        (rho_in * vel_in[2] ** 2 - mag_in[2] ** 2 + press_in) * cotan_mid
        - rho_in * vel_in[0] * vel_in[1]
        + mag_in[0] * mag_in[1]
    ) / radius_mid
    source_azim = (
        -(
            rho_in * vel_in[0] * vel_in[2]
            - mag_in[0] * mag_in[2]
            + cotan_mid * (rho_in * vel_in[1] * vel_in[2] - mag_in[1] * mag_in[2])
        )
        / radius_mid
    )
    zeroes = jnp.zeros_like(source_rad)
    hydro = -net_flow / volume + jnp.stack([zeroes, source_rad, source_pol, source_azim, zeroes])
    e_radial = velocity[2] * magnet[1] - velocity[1] * magnet[2]
    e_polar = velocity[0] * magnet[2] - velocity[2] * magnet[0]
    e_azimuth = velocity[1] * magnet[0] - velocity[0] * magnet[1]
    edge_radial = 0.25 * (
        e_radial[:-1, :-1] + e_radial[1:, :-1] + e_radial[:-1, 1:] + e_radial[1:, 1:]
    )
    edge_polar = 0.25 * (
        e_polar[:, :-1, :-1] + e_polar[:, 1:, :-1] + e_polar[:, :-1, 1:] + e_polar[:, 1:, 1:]
    )
    edge_azimuth = 0.25 * (
        e_azimuth[:-1, :, :-1]
        + e_azimuth[1:, :, :-1]
        + e_azimuth[:-1, :, 1:]
        + e_azimuth[1:, :, 1:]
    )
    azim_at_low = edge_azimuth[1 : jrow + 1, 2 : kcol + 2, 1 : irad + 1]
    azim_high_theta = edge_azimuth[2 : jrow + 2, 2 : kcol + 2, 1 : irad + 1]
    azim_high_radius = edge_azimuth[1 : jrow + 1, 2 : kcol + 2, 2 : irad + 2]
    polar_at_low = edge_polar[2 : jrow + 2, 1 : kcol + 1, 1 : irad + 1]
    polar_high_phi = edge_polar[2 : jrow + 2, 2 : kcol + 2, 1 : irad + 1]
    polar_high_radius = edge_polar[2 : jrow + 2, 1 : kcol + 1, 2 : irad + 2]
    radial_at_low = edge_radial[1 : jrow + 1, 1 : kcol + 1, 2 : irad + 2]
    radial_high_phi = edge_radial[1 : jrow + 1, 2 : kcol + 2, 2 : irad + 2]
    radial_high_theta = edge_radial[2 : jrow + 2, 1 : kcol + 1, 2 : irad + 2]
    circ_radial = radius_low * step_phi * (
        azim_high_theta * sine_high - azim_at_low * sine_low
    ) - radius_low * step_theta * (polar_high_phi - polar_at_low)
    rate_radial = -circ_radial / area_rad_low
    circ_polar = step_radius * (radial_high_phi - radial_at_low) - step_phi * sine_low * (
        radius_high * azim_high_radius - radius_low * azim_at_low
    )
    keep_inner = keep_mask[2 : jrow + 2][:, None, None]
    rate_polar = -circ_polar * keep_inner / jnp.where(keep_inner > 0.5, area_pol_low, 1.0)
    circ_azim = step_theta * (
        radius_high * polar_high_radius - radius_low * polar_at_low
    ) - step_radius * (radial_high_theta - radial_at_low)
    rate_azim = -circ_azim / area_azim
    return jnp.concatenate([hydro, jnp.stack([rate_radial, rate_polar, rate_azim])], 0)


def advance(padded, row_start, total_rows, total_cols):
    rate = section_rate(padded, row_start, total_rows, total_cols)
    delta = time_step(total_cols, padded.shape[3])
    return padded[:, 2:-2, 2:-2] + delta * rate


def pole_ghosts(received, width):
    flip_signs = jnp.array([1.0, 1.0, -1.0, -1.0, 1.0, 1.0, -1.0, -1.0], jnp.float32)[
        :, None, None, None
    ]
    first_rows = received[:, : width + 2]
    last_rows = received[:, width + 2 :]
    cells_low = first_rows[:, width - 1 :: -1]
    face_low = first_rows[6:7, width + 1 : 1 : -1]
    cells_high = last_rows[:, ::-1]
    face_high = jnp.concatenate(
        [last_rows[6:7, width - 1 : width], last_rows[6:7, width - 1 : 0 : -1]], 1
    )
    low_ghost = jnp.concatenate([cells_low[:6], face_low, cells_low[7:]], 0) * flip_signs
    high_ghost = jnp.concatenate([cells_high[:6], face_high, cells_high[7:]], 0) * flip_signs
    return (low_ghost, high_ghost)


def pole_payload(full_pad, width):
    inner_count = full_pad.shape[1] - 2 * width
    return jnp.concatenate(
        [full_pad[:, width : 2 * width + 2], full_pad[:, inner_count : inner_count + width]], 1
    )


def place_poles(full_pad, received, width, at_bottom, at_top):
    low_ghost, high_ghost = pole_ghosts(received, width)
    full_pad = full_pad.at[:, :width].set(jnp.where(at_bottom, low_ghost, full_pad[:, :width]))
    return full_pad.at[:, -width:].set(jnp.where(at_top, high_ghost, full_pad[:, -width:]))


def across_pole(payload):
    return from_behind(payload, "ph", lax.axis_size("ph") // 2)


def fill_poles(full_pad, width, at_bottom, at_top):
    received = across_pole(pole_payload(full_pad, width))
    return place_poles(full_pad, received, width, at_bottom, at_top)


def surround(grid_vals, width, at_bottom, at_top):
    side_pad = padded_2(grid_vals, (("ph", 2),), width, True)
    full_pad = padded_2(side_pad, (("th", 1),), width, False)
    return fill_poles(full_pad, width, at_bottom, at_top)


def pole_transpose(cot_full, width, at_bottom, at_top):
    recv_shape = (cot_full.shape[0], 2 * width + 2, cot_full.shape[2], cot_full.shape[3])
    blank_full = jnp.zeros_like(cot_full)
    blank_recv = jnp.zeros(recv_shape, cot_full.dtype)
    _, pull_place = jax.vjp(
        lambda full_pad, received: place_poles(full_pad, received, width, at_bottom, at_top),
        blank_full,
        blank_recv,
    )
    cot_kept, cot_recv = pull_place(cot_full)
    returned = across_pole(cot_recv)
    _, pull_take = jax.vjp(lambda full_pad: pole_payload(full_pad, width), blank_full)
    return cot_kept + pull_take(returned)[0]


def fold_rows(cot_full, width):
    inner_count = cot_full.shape[1] - 2 * width
    edges_both = jnp.concatenate([cot_full[:, :width], cot_full[:, inner_count + width :]], 1)
    arrived = padded_2(edges_both, (("th", 1),), width, False)
    middle = cot_full[:, width : inner_count + width]
    middle = middle.at[:, :width].add(arrived[:, :width])
    return middle.at[:, inner_count - width :].add(arrived[:, 3 * width :])


def fold_columns(cot_side, width):
    inner_count = cot_side.shape[2] - 2 * width
    edges_both = jnp.concatenate([cot_side[:, :, :width], cot_side[:, :, inner_count + width :]], 2)
    arrived = padded_2(edges_both, (("ph", 2),), width, True)
    middle = cot_side[:, :, width : inner_count + width]
    middle = middle.at[:, :, :width].add(arrived[:, :, :width])
    return middle.at[:, :, inner_count - width :].add(arrived[:, :, 3 * width :])


def unsurround(cot_full, width, at_bottom, at_top):
    cot_kept = pole_transpose(cot_full, width, at_bottom, at_top)
    return fold_columns(fold_rows(cot_kept, width), width)


def shards(state, cotangent):
    row_count = state.shape[1]
    col_count = state.shape[2]
    total_rows = row_count * lax.axis_size("th")
    total_cols = col_count * lax.axis_size("ph")
    position = lax.axis_index("th")
    first_row = position * row_count
    at_bottom = position == 0
    at_top = position == lax.axis_size("th") - 1
    half_cot = 0.5 * cotangent

    def section_at(start):
        return lambda padded: advance(padded, start, total_rows, total_cols)

    padded_zero = surround(state, 2, at_bottom, at_top)
    moved_one, pull_first = jax.vjp(section_at(first_row), padded_zero)
    padded_one = surround(moved_one, 2, at_bottom, at_top)
    _, pull_second = jax.vjp(section_at(first_row), padded_one)
    cot_one = unsurround(pull_second(half_cot)[0], 2, at_bottom, at_top)
    return half_cot + unsurround(pull_first(cot_one)[0], 2, at_bottom, at_top)


def solution(mesh):
    placed = (P(None, "th", "ph", None), P(None, "th", "ph", None))
    return jax.shard_map(
        shards, mesh=mesh, in_specs=placed, out_specs=P(None, "th", "ph", None), check_vma=False
    )
```

profile of v0, /device:TPU:0, one launch (start us, length us, event | category | flops | bytes accessed | tf_op | source)
XLA Modules:
  0.0 1044.1 jit_solution(209531099116584600)
XLA Ops:
  78.7 13.2 %pad_maximum_fusion = f32[8,28,28,260]{3,2,1,0:T(8,128)} fusion(f32[8,28,28,2]{3,2,1,0:T(8,128)} %reshape.963, f32[8,28,28,256]{3,2,1,0:T(8,128)} %fusion.299, f32[8,28,28,2]{3,2,1,0:T(8,128)} %reshape.962), kind=kLoop, calls=%fused_computation | loop fusion | flops 3261440 | bytes 13045760 | tf_op jit(solution)/shard_map/jvp(jit(_pad))/concatenate | solution.py:57
  154.8 11.7 %fusion.13 = f32[5,27,27,258]{3,2,1,0:T(8,128)} fusion(f32[5,27,27,259]{3,2,1,0:T(8,128)} %get-tuple-element.315, f32[27,27,258]{2,1,0:T(8,128)} %broadcast_multiply_fusion.10, f32[8,28,28,256]{3,2,1,0:T(8,128)} %fusion.299, f32[8,28,28,2]{3,2,1,0:T(8,128)} %reshape.962, f32[8,28,28,260]{3,2,1,0:T(8,128)S(1)} %copy-done), kind=kLoop, calls=%fused_computation.43 | loop fusion | flops 5642460 | bytes 22271592 | tf_op jit(solution)/shard_map/jvp()/sub | solution.py:96
  188.6 22.3 %fusion.370 = (f32[5,24,24,256]{3,2,1,0:T(8,128)}, f32[5,24,24,256]{3,2,1,0:T(8,128)}, f32[5,24,24,256]{3,2,1,0:T(8,128)}, f32[5,24,24,256]{3,2,1,0:T(8,128)}, f...) fusion(f32[24,256]{1,0:T(8,128)} %get-tuple-element.600, ...), kind=kLoop, calls=%fused_computation.916 | loop fusion | flops 15482880 | bytes 44360704 | tf_op jit(solution)/shard_map/transpose(jvp())/neg | solution.py:128
  217.6 9.3 collective-permute-done.5
  251.1 8.9 collective-permute-done.9
  283.9 13.1 %pad_maximum_fusion.1 = f32[8,28,28,260]{3,2,1,0:T(8,128)} fusion(f32[8,28,28,2]{3,2,1,0:T(8,128)} %reshape.965, f32[8,28,28,256]{3,2,1,0:T(8,128)} %fusion.298, f32[8,28,28,2]{3,2,1,0:T(8,128)} %reshape.964), kind=kLoop, calls=%fused_computation.1 | loop fusion | flops 3261440 | bytes 13045760 | tf_op jit(solution)/shard_map/jvp(jit(_pad))/concatenate | solution.py:57
  302.7 11.2 %fusion.165 = (f32[1,27,27,259]{3,2,1,0:T(8,128)}, f32[1,27,27,259]{3,2,1,0:T(8,128)S(1)}, f32[1,27,27,259]{3,2,1,0:T(8,128)}, f32[1,27,27,259]{3,2,1,0:T(8,128)...) fusion(f32[26,27,258]{2,1,0:T(8,128)} %add_multiply_fusion.5, f32[8,28,28,260]{3,2,1,0:T(8,128)} %pad_maximum_fusion.1, ...), kind=kLoop, calls=%fused_computation.394 | loop fusion | flops 3020976 | bytes 10511856 | tf_op jit(solution)/shard_map/transpose(jvp())/broadcast_in_dim | solution.py:163
  360.9 9.7 fusion.366
  372.5 15.2 %fusion.22 = (f32[5,26,27,259]{3,2,1,0:T(8,128)}, f32[26,27,259]{2,1,0:T(8,128)}, f32[5,26,27,259]{3,2,1,0:T(8,128)}, f32[5,26,27,259]{3,2,1,0:T(8,128)}) fusion(f32[5,24,24,256]{3,2,1,0:T(8,128)} %get-tuple-element.475, f32[5,24,24,256]{3,2,1,0:T(8,128)} %get-tuple-element.472, f32[8,28,28,260]{3,2,1,0:T(8,128)} %pad_maximum_fusion.1, ...), kind=kLoop, calls=%fused_computation.124 | loop fusion | flops 7090902 | bytes 25534584 | tf_op jit(solution)/shard_map/transpose(jvp())/mul | solution.py:96
  391.6 15.5 %fusion.19 = (f32[5,27,27,258]{3,2,1,0:T(8,128)S(1)}, f32[27,27,258]{2,1,0:T(8,128)}, f32[5,27,27,258]{3,2,1,0:T(8,128)}, f32[5,27,27,258]{3,2,1,0:T(8,128)}) fusion(f32[5,24,24,256]{3,2,1,0:T(8,128)} %get-tuple-element.474, f32[5,24,24,256]{3,2,1,0:T(8,128)} %get-tuple-element.473, f32[8,28,28,256]{3,2,1,0:T(8,128)S(1)} %bitcast.1247, ...), kind=kLoop, calls=%fused_computation.119 | loop fusion | flops 8275608 | bytes 28922160 | tf_op jit(solution)/shard_map/transpose(jvp())/mul | solution.py:96
  417.9 14.8 %pad_add_fusion.19 = f32[5,27,27,259]{3,2,1,0:T(8,128)} fusion(f32[5,27,27,258]{3,2,1,0:T(8,128)} %get-tuple-element.416, f32[5,27,27,258]{3,2,1,0:T(8,128)S(1)} %bitcast.1249, f32[5,26,27,259]{3,2,1,0:T(8,128)} %get-tuple-element.420, f32[5,26,27,259]{3,2,1,0:T(8,128)} %get-tuple-element.419, f32[5,27,26,259]{3,2,1,0:T(8,128)} %get-tuple-element.286, ...), kind=kLoop, calls=%fused_computation.49 | loop fusion | flops 4720275 | bytes 25844940 | tf_op jit(solution)/shard_map/transpose(jvp())/add_any | solution.py:41
  432.7 18.1 %fusion.89 = (f32[1,27,27,259]{3,2,1,0:T(8,128)}, f32[27,27,259]{2,1,0:T(8,128)}, f32[27,27,259]{2,1,0:T(8,128)}, f32[27,27,259]{2,1,0:T(8,128)}, f32[27,27,259]...) fusion(f32[5,27,27,258]{3,2,1,0:T(8,128)} %get-tuple-element.41, ...), kind=kLoop, calls=%fused_computation.260 | loop fusion | flops 7363629 | bytes 47228436 | tf_op jit(solution)/shard_map/transpose(jvp())/broadcast_in_dim | solution.py:65
  462.5 10.6 %fusion.161 = (f32[1,27,27,259]{3,2,1,0:T(8,128)}, f32[27,27,259]{2,1,0:T(8,128)}, f32[27,27,259]{2,1,0:T(8,128)}) fusion(f32[1,27,27,259]{3,2,1,0:T(8,128)} %copy-done.63, f32[1,27,27,259]{3,2,1,0:T(8,128)} %copy-done.62, f32[1,27,27,259]{3,2,1,0:T(8,128)} %get-tuple-element.253, f32[27,27,259]{2,1,0:T(8,128)} %get-tuple-element.252, ...), kind=kLoop, calls=%fused_computation.386 | loop fusion | flops 3209787 | bytes 15692292 | tf_op jit(solution)/shard_map/transpose(jvp())/broadcast_in_dim | solution.py:82
  483.1 12.4 %fusion.164 = (f32[27,27,259]{2,1,0:T(8,128)}, f32[1,27,27,259]{3,2,1,0:T(8,128)}, f32[1,27,27,259]{3,2,1,0:T(8,128)}, f32[1,27,27,259]{3,2,1,0:T(8,128)}) fusion(f32[1,27,27,259]{3,2,1,0:T(8,128)S(1)} %copy-done.20, f32[1,27,27,259]{3,2,1,0:T(8,128)S(1)} %copy-done.24, f32[27,27,259]{2,1,0:T(8,128)} %get-tuple-element.580, ...), kind=kLoop, calls=%fused_computation.393 | loop fusion | flops 6230763 | bytes 13539484 | tf_op jit(solution)/shard_map/transpose(jvp())/add_any | solution.py:90
  495.6 12.2 %fusion.151 = (f32[1,27,27,259]{3,2,1,0:T(8,128)}, f32[27,27,259]{2,1,0:T(8,128)}, f32[1,27,27,259]{3,2,1,0:T(8,128)}, f32[1,27,27,259]{3,2,1,0:T(8,128)}, f32[1...) fusion(f32[1,27,27,259]{3,2,1,0:T(8,128)} %get-tuple-element.267, f32[1,27,27,259]{3,2,1,0:T(8,128)} %get-tuple-element.254, ...), kind=kLoop, calls=%fused_computation.369 | loop fusion | flops 5097897 | bytes 19468512 | tf_op jit(solution)/shard_map/transpose(jvp())/broadcast_in_dim | solution.py:82
  524.1 10.2 add_add_fusion.3
  540.1 16.8 %fusion.27 = (f32[3,27,27,259]{3,2,1,0:T(8,128)}, f32[3,27,27,259]{3,2,1,0:T(8,128)}) fusion(f32[5,27,27,259]{3,2,1,0:T(8,128)} %pad_add_fusion.19, f32[3,27,27,259]{3,2,1,0:T(8,128)S(1)} %copy-done.7, f32[1,27,27,259]{3,2,1,0:T(8,128)} %get-tuple-element.526, f32[1,27,27,259]{3,2,1,0:T(8,128)} %get-tuple-element.529, ...), kind=kLoop, calls=%fused_computation.131 | loop fusion | flops 15860124 | bytes 31223988 | tf_op jit(solution)/shard_map/transpose(jvp())/add_any | solution.py:70
  591.0 10.0 fusion
  610.8 30.0 %collective-permute-done.10 = f32[8,6,28,256]{3,0,2,1:T(8,128)S(1)} collective-permute-done((f32[8,6,28,256]{3,0,2,1:T(8,128)S(1)}, f32[8,6,28,256]{3,0,2,1:T(8,128)S(1)}, u32[]{:S(2)}, u32[]{:S(2)}) %collective-permute-start.10) | collective-permute-done | bytes 1376288 | tf_op jit(solution)/shard_map/ppermute | solution.py:20
  706.4 11.3 %fusion.232 = (f32[1,27,27,259]{3,2,1,0:T(8,128)}, f32[1,27,27,259]{3,2,1,0:T(8,128)}, f32[1,27,27,259]{3,2,1,0:T(8,128)}, f32[1,27,27,259]{3,2,1,0:T(8,128)}) fusion(f32[1,27,27,259]{3,2,1,0:T(8,128)S(1)} %copy-done.9, f32[26,27,258]{2,1,0:T(8,128)} %add_multiply_fusion.3, f32[27,26,258]{2,1,0:T(8,128)} %copy-done.79, ...), kind=kLoop, calls=%fused_computation.531 | loop fusion | flops 2832165 | bytes 6680728 | tf_op jit(solution)/shard_map/transpose(jvp())/broadcast_in_dim | solution.py:163
  723.6 15.0 %fusion.343 = (f32[5,27,26,259]{3,2,1,0:T(8,128)}, f32[5,27,26,259]{3,2,1,0:T(8,128)}, f32[5,27,26,259]{3,2,1,0:T(8,128)}, f32[27,26,259]{2,1,0:T(8,128)S(1)}) fusion(f32[5,24,24,256]{3,2,1,0:T(8,128)} %get-tuple-element.247, f32[5,24,24,256]{3,2,1,0:T(8,128)S(1)} %copy-done.84, f32[27,26,259]{2,1,0:T(8,128)S(1)} %copy-done.75, ...), kind=kLoop, calls=%fused_computation.909 | loop fusion | flops 7090902 | bytes 25534584 | tf_op jit(solution)/shard_map/transpose(jvp())/neg | solution.py:98
  740.8 13.5 %fusion.23 = (f32[5,26,27,259]{3,2,1,0:T(8,128)}, f32[26,27,259]{2,1,0:T(8,128)}, f32[5,26,27,259]{3,2,1,0:T(8,128)}, f32[5,26,27,259]{3,2,1,0:T(8,128)}) fusion(f32[5,24,24,256]{3,2,1,0:T(8,128)} %get-tuple-element.471, f32[5,24,24,256]{3,2,1,0:T(8,128)S(1)} %copy-done.81, f32[8,28,28,260]{3,2,1,0:T(8,128)} %pad_maximum_fusion, ...), kind=kLoop, calls=%fused_computation.125 | loop fusion | flops 7090902 | bytes 25534584 | tf_op jit(solution)/shard_map/transpose(jvp())/mul | solution.py:96
  757.4 16.9 %fusion.21 = (f32[5,27,27,258]{3,2,1,0:T(8,128)S(1)}, f32[27,27,258]{2,1,0:T(8,128)}, f32[5,27,27,258]{3,2,1,0:T(8,128)}, f32[5,27,27,258]{3,2,1,0:T(8,128)}) fusion(f32[5,24,24,256]{3,2,1,0:T(8,128)} %get-tuple-element.470, f32[5,24,24,256]{3,2,1,0:T(8,128)} %get-tuple-element.469, f32[8,28,28,256]{3,2,1,0:T(8,128)} %fusion.299, ...), kind=kLoop, calls=%fused_computation.121 | loop fusion | flops 8275608 | bytes 28922160 | tf_op jit(solution)/shard_map/transpose(jvp())/mul | solution.py:96
  784.9 16.7 %pad_add_fusion.16 = f32[5,27,27,259]{3,2,1,0:T(8,128)} fusion(f32[5,27,27,258]{3,2,1,0:T(8,128)} %get-tuple-element.406, f32[5,27,27,258]{3,2,1,0:T(8,128)} %get-tuple-element.405, f32[5,26,27,259]{3,2,1,0:T(8,128)} %get-tuple-element.410, f32[5,26,27,259]{3,2,1,0:T(8,128)} %get-tuple-element.409, f32[5,27,26,259]{3,2,1,0:T(8,128)} %get-tuple-element.239, ...), kind=kLoop, calls=%fused_computation.44 | loop fusion | flops 4720275 | bytes 25844940 | tf_op jit(solution)/shard_map/transpose(jvp())/add_any | solution.py:41
  801.6 18.0 %fusion.78 = (f32[1,27,27,259]{3,2,1,0:T(8,128)}, f32[27,27,259]{2,1,0:T(8,128)}, f32[27,27,259]{2,1,0:T(8,128)}, f32[27,27,259]{2,1,0:T(8,128)}, f32[27,27,259]...) fusion(f32[5,27,27,258]{3,2,1,0:T(8,128)} %get-tuple-element.40, ...), kind=kLoop, calls=%fused_computation.238 | loop fusion | flops 7363629 | bytes 47228436 | tf_op jit(solution)/shard_map/transpose(jvp())/broadcast_in_dim | solution.py:65
  830.8 10.4 fusion.129
  845.4 12.0 %multiply_bitcast_fusion.3 = (f32[1,27,27,259]{3,2,1,0:T(8,128)}, f32[1,27,27,259]{3,2,1,0:T(8,128)}, f32[1,27,27,259]{3,2,1,0:T(8,128)}, f32[27,27,259]{2,1,0:T(8,128)}) fusion(f32[27,27,259]{2,1,0:T(8,128)} %get-tuple-element.310, f32[26,27,258]{2,1,0:T(8,128)} %add_multiply_fusion.3, f32[26,26,259]{2,1,0:T(8,128)} %copy-done.67, ...), kind=kLoop, calls=%fused_computation.557 | loop fusion | flops 5097897 | bytes 11998216 | tf_op jit(solution)/shard_map/transpose(jvp())/broadcast_in_dim | solution.py:163
  857.5 12.2 %fusion.119 = (f32[1,27,27,259]{3,2,1,0:T(8,128)}, f32[27,27,259]{2,1,0:T(8,128)}, f32[1,27,27,259]{3,2,1,0:T(8,128)}, f32[1,27,27,259]{3,2,1,0:T(8,128)}, f32[1...) fusion(f32[1,27,27,259]{3,2,1,0:T(8,128)} %get-tuple-element.227, f32[1,27,27,259]{3,2,1,0:T(8,128)} %get-tuple-element.214, ...), kind=kLoop, calls=%fused_computation.316 | loop fusion | flops 5097897 | bytes 19468512 | tf_op jit(solution)/shard_map/transpose(jvp())/broadcast_in_dim | solution.py:82
  884.9 12.3 %add_add_fusion.2 = f32[3,27,27,259]{3,2,1,0:T(8,128)} fusion(f32[1,27,27,259]{3,2,1,0:T(8,128)} %get-tuple-element.556, f32[1,27,27,259]{3,2,1,0:T(8,128)} %get-tuple-element.566, f32[1,27,27,259]{3,2,1,0:T(8,128)} %get-tuple-element.567, f32[1,27,27,259]{3,2,1,0:T(8,128)} %get-tuple-element.565, f32[1,27,27,259]{3,2,1,0:T(8,128)} %get-tuple-element.429, ...), kind=kLoop, calls=%fused_computation.68 | loop fusion | flops 14727258 | bytes 24426792 | tf_op jit(solution)/shard_map/transpose(jvp())/add_any | solution.py:71
  905.4 16.0 %fusion.25 = (f32[3,27,27,259]{3,2,1,0:T(8,128)}, f32[3,27,27,259]{3,2,1,0:T(8,128)}) fusion(f32[5,27,27,259]{3,2,1,0:T(8,128)} %pad_add_fusion.16, f32[1,27,27,259]{3,2,1,0:T(8,128)} %get-tuple-element.508, f32[1,27,27,259]{3,2,1,0:T(8,128)} %get-tuple-element.511, f32[1,27,27,259]{3,2,1,0:T(8,128)} %get-tuple-element.513, ...), kind=kLoop, calls=%fused_computation.128 | loop fusion | flops 16426557 | bytes 28958256 | tf_op jit(solution)/shard_map/transpose(jvp())/add_any | solution.py:70
  955.5 9.8 fusion.1
  974.1 32.1 %collective-permute-done.15 = f32[8,6,28,256]{3,0,2,1:T(8,128)S(1)} collective-permute-done((f32[8,6,28,256]{3,0,2,1:T(8,128)S(1)}, f32[8,6,28,256]{3,0,2,1:T(8,128)S(1)}, u32[]{:S(2)}, u32[]{:S(2)}) %collective-permute-start.15) | collective-permute-done | bytes 1376288 | tf_op jit(solution)/shard_map/ppermute | solution.py:20
  (698 shorter events, 579.5 us)
Async XLA Ops:
  2.2 10.3 collective-permute-start
  2.8 11.4 %collective-permute-start.1 = (f32[8,24,2,256]{3,1,2,0:T(8,128)S(1)}, f32[8,24,2,256]{3,1,2,0:T(8,128)S(1)}, u32[]{:S(2)}, u32[]{:S(2)}) collective-permute-start(f32[8,24,2,256]{3,1,2,0:T(8,128)S(1)} %copy.2567), channel_id=1, source_target_pairs={{1,0},{2,1},{3,2},{4,3},{5,4},{6,5},{7,6},{0,7},{9,8},{10,9},{11,1... | collective-permute-start | bytes 1179656 | tf_op jit(solution)/shard_map/ppermute | solution.py:31
  5.7 332.0 %copy-start.145 = (f32[256]{0:T(256)}, f32[256]{0:T(256)S(1)}, u32[]{:S(2)}) copy-start(f32[256]{0:T(256)S(1)} %fusion.320) | copy-start | bytes 3076
  5.8 327.8 %copy-start.152 = (f32[24]{0:T(128)}, f32[24]{0:T(128)S(1)}, u32[]{:S(2)}) copy-start(f32[24]{0:T(128)S(1)} %get-tuple-element.602) | copy-start | bytes 292
  5.9 179.1 %copy-start.175 = (f32[24]{0:T(128)}, f32[24]{0:T(128)S(1)}, u32[]{:S(2)}) copy-start(f32[24]{0:T(128)S(1)} %get-tuple-element.604) | copy-start | bytes 292
  5.9 179.1 %copy-start.178 = (f32[24]{0:T(128)}, f32[24]{0:T(128)S(1)}, u32[]{:S(2)}) copy-start(f32[24]{0:T(128)S(1)} %get-tuple-element.605) | copy-start | bytes 292
  6.0 179.0 %copy-start.160 = (f32[256]{0:T(256)}, f32[256]{0:T(256)S(1)}, u32[]{:S(2)}) copy-start(f32[256]{0:T(256)S(1)} %get-tuple-element.612) | copy-start | bytes 3076
  6.0 229.0 %copy-start.147 = (f32[256]{0:T(256)}, f32[256]{0:T(256)S(1)}, u32[]{:S(2)}) copy-start(f32[256]{0:T(256)S(1)} %get-tuple-element.613) | copy-start | bytes 3076
  6.0 179.0 %copy-start.154 = (f32[256]{0:T(256)}, f32[256]{0:T(256)S(1)}, u32[]{:S(2)}) copy-start(f32[256]{0:T(256)S(1)} %get-tuple-element.608) | copy-start | bytes 3076
  6.0 179.0 %copy-start.157 = (f32[256]{0:T(256)}, f32[256]{0:T(256)S(1)}, u32[]{:S(2)}) copy-start(f32[256]{0:T(256)S(1)} %get-tuple-element.609) | copy-start | bytes 3076
  6.1 178.9 %copy-start.163 = (f32[256]{0:T(256)}, f32[256]{0:T(256)S(1)}, u32[]{:S(2)}) copy-start(f32[256]{0:T(256)S(1)} %get-tuple-element.611) | copy-start | bytes 3076
  6.1 178.9 %copy-start.169 = (f32[256]{0:T(256)}, f32[256]{0:T(256)S(1)}, u32[]{:S(2)}) copy-start(f32[256]{0:T(256)S(1)} %get-tuple-element.610) | copy-start | bytes 3076
  6.8 176.5 %copy-start.135 = (f32[24,256]{1,0:T(8,128)}, f32[24,256]{1,0:T(8,128)S(1)}, u32[]{:S(2)}) copy-start(f32[24,256]{1,0:T(8,128)S(1)} %get-tuple-element.591) | copy-start | bytes 73732
  19.2 34.0 %collective-permute-start.4 = (f32[8,6,28,256]{3,0,2,1:T(8,128)}, f32[8,6,28,256]{3,0,2,1:T(8,128)}, u32[]{:S(2)}, u32[]{:S(2)}) collective-permute-start(f32[8,6,28,256]{3,0,2,1:T(8,128)} %pad_maximum_fusion.8), channel_id=1, source_target_pairs={{4,0},{5,1},{6,2},{7,3},{0,4},{1,5},{2,6},{3,7},{12,8},{13,9},{14,... | collective-permute-start | bytes 4128776 | tf_op jit(solution)/shard_map/ppermute | solution.py:20
  23.6 161.4 %copy-start.138 = (f32[24,256]{1,0:T(8,128)}, f32[24,256]{1,0:T(8,128)S(1)}, u32[]{:S(2)}) copy-start(f32[24,256]{1,0:T(8,128)S(1)} %get-tuple-element.599) | copy-start | bytes 73732
  23.6 13.0 %collective-permute-start.2 = (f32[8,2,28,256]{3,0,2,1:T(8,128)S(1)}, f32[8,2,28,256]{3,0,2,1:T(8,128)S(1)}, u32[]{:S(2)}, u32[]{:S(2)}) collective-permute-start(f32[8,2,28,256]{3,0,2,1:T(8,128)S(1)} %copy.2490), channel_id=1, source_target_pairs={{0,8},{8,16},{16,24},{1,9},{9,17},{17,25},{2,10},{10,18},{18,26},{... | collective-permute-start | bytes 1376264 | tf_op jit(solution)/shard_map/ppermute | solution.py:30
  27.4 13.9 %collective-permute-start.3 = (f32[8,2,28,256]{3,0,2,1:T(8,128)S(1)}, f32[8,2,28,256]{3,0,2,1:T(8,128)S(1)}, u32[]{:S(2)}, u32[]{:S(2)}) collective-permute-start(f32[8,2,28,256]{3,0,2,1:T(8,128)S(1)} %copy.2491), channel_id=1, source_target_pairs={{8,0},{16,8},{24,16},{9,1},{17,9},{25,17},{10,2},{18,10},{26,18},{... | collective-permute-start | bytes 1376264 | tf_op jit(solution)/shard_map/ppermute | solution.py:31
  214.8 12.1 %collective-permute-start.5 = (f32[8,24,2,256]{3,1,2,0:T(8,128)S(1)}, f32[8,24,2,256]{3,1,2,0:T(8,128)S(1)}, u32[]{:S(2)}, u32[]{:S(2)}) collective-permute-start(f32[8,24,2,256]{3,1,2,0:T(8,128)S(1)} %copy.2505), channel_id=1, source_target_pairs={{0,1},{1,2},{2,3},{3,4},{4,5},{5,6},{6,7},{7,0},{8,9},{9,10},{10,1... | collective-permute-start | bytes 1179656 | tf_op jit(solution)/shard_map/ppermute | solution.py:30
  215.0 12.1 %collective-permute-start.6 = (f32[8,24,2,256]{3,1,2,0:T(8,128)S(1)}, f32[8,24,2,256]{3,1,2,0:T(8,128)S(1)}, u32[]{:S(2)}, u32[]{:S(2)}) collective-permute-start(f32[8,24,2,256]{3,1,2,0:T(8,128)S(1)} %copy.2506), channel_id=1, source_target_pairs={{1,0},{2,1},{3,2},{4,3},{5,4},{6,5},{7,6},{0,7},{9,8},{10,9},{11,1... | collective-permute-start | bytes 1179656 | tf_op jit(solution)/shard_map/ppermute | solution.py:31
  228.7 31.3 %collective-permute-start.9 = (f32[8,6,28,256]{3,0,2,1:T(8,128)S(1)}, f32[8,6,28,256]{3,0,2,1:T(8,128)S(1)}, u32[]{:S(2)}, u32[]{:S(2)}) collective-permute-start(f32[8,6,28,256]{3,0,2,1:T(8,128)S(1)} %pad_maximum_fusion.9), channel_id=1, source_target_pairs={{4,0},{5,1},{6,2},{7,3},{0,4},{1,5},{2,6},{3,7},{12,8},{13,9},{14,... | collective-permute-start | bytes 4128776 | tf_op jit(solution)/shard_map/ppermute | solution.py:20
  228.7 13.8 %collective-permute-start.7 = (f32[8,2,28,256]{3,0,2,1:T(8,128)S(1)}, f32[8,2,28,256]{3,0,2,1:T(8,128)S(1)}, u32[]{:S(2)}, u32[]{:S(2)}) collective-permute-start(f32[8,2,28,256]{3,0,2,1:T(8,128)S(1)} %copy.2509), channel_id=1, source_target_pairs={{0,8},{8,16},{16,24},{1,9},{9,17},{17,25},{2,10},{10,18},{18,26},{... | collective-permute-start | bytes 1376264 | tf_op jit(solution)/shard_map/ppermute | solution.py:30
  233.7 13.3 %collective-permute-start.8 = (f32[8,2,28,256]{3,0,2,1:T(8,128)S(1)}, f32[8,2,28,256]{3,0,2,1:T(8,128)S(1)}, u32[]{:S(2)}, u32[]{:S(2)}) collective-permute-start(f32[8,2,28,256]{3,0,2,1:T(8,128)S(1)} %copy.2510), channel_id=1, source_target_pairs={{8,0},{16,8},{24,16},{9,1},{17,9},{25,17},{10,2},{18,10},{26,18},{... | collective-permute-start | bytes 1376264 | tf_op jit(solution)/shard_map/ppermute | solution.py:31
  609.4 31.3 %collective-permute-start.10 = (f32[8,6,28,256]{3,0,2,1:T(8,128)S(1)}, f32[8,6,28,256]{3,0,2,1:T(8,128)S(1)}, u32[]{:S(2)}, u32[]{:S(2)}) collective-permute-start(f32[8,6,28,256]{3,0,2,1:T(8,128)S(1)} %copy.2528), channel_id=1, source_target_pairs={{4,0},{5,1},{6,2},{7,3},{0,4},{1,5},{2,6},{3,7},{12,8},{13,9},{14,... | collective-permute-start | bytes 4128776 | tf_op jit(solution)/shard_map/ppermute | solution.py:20
  645.4 11.4 %collective-permute-start.11 = (f32[8,2,28,256]{3,0,2,1:T(8,128)S(1)}, f32[8,2,28,256]{3,0,2,1:T(8,128)S(1)}, u32[]{:S(2)}, u32[]{:S(2)}) collective-permute-start(f32[8,2,28,256]{3,0,2,1:T(8,128)S(1)} %copy.2531), channel_id=1, source_target_pairs={{0,8},{8,16},{16,24},{1,9},{9,17},{17,25},{2,10},{10,18},{18,26},{... | collective-permute-start | bytes 1376264 | tf_op jit(solution)/shard_map/ppermute | solution.py:30
  649.3 11.9 %collective-permute-start.12 = (f32[8,2,28,256]{3,0,2,1:T(8,128)S(1)}, f32[8,2,28,256]{3,0,2,1:T(8,128)S(1)}, u32[]{:S(2)}, u32[]{:S(2)}) collective-permute-start(f32[8,2,28,256]{3,0,2,1:T(8,128)S(1)} %copy.2533), channel_id=1, source_target_pairs={{8,0},{16,8},{24,16},{9,1},{17,9},{25,17},{10,2},{18,10},{26,18},{... | collective-permute-start | bytes 1376264 | tf_op jit(solution)/shard_map/ppermute | solution.py:31
  661.8 10.6 %collective-permute-start.13 = (f32[8,24,2,256]{3,1,2,0:T(8,128)S(1)}, f32[8,24,2,256]{3,1,2,0:T(8,128)S(1)}, u32[]{:S(2)}, u32[]{:S(2)}) collective-permute-start(f32[8,24,2,256]{3,1,2,0:T(8,128)S(1)} %copy.2535), channel_id=1, source_target_pairs={{0,1},{1,2},{2,3},{3,4},{4,5},{5,6},{6,7},{7,0},{8,9},{9,10},{10,1... | collective-permute-start | bytes 1179656 | tf_op jit(solution)/shard_map/ppermute | solution.py:30
  661.9 11.0 %collective-permute-start.14 = (f32[8,24,2,256]{3,1,2,0:T(8,128)S(1)}, f32[8,24,2,256]{3,1,2,0:T(8,128)S(1)}, u32[]{:S(2)}, u32[]{:S(2)}) collective-permute-start(f32[8,24,2,256]{3,1,2,0:T(8,128)S(1)} %copy.2537), channel_id=1, source_target_pairs={{1,0},{2,1},{3,2},{4,3},{5,4},{6,5},{7,6},{0,7},{9,8},{10,9},{11,1... | collective-permute-start | bytes 1179656 | tf_op jit(solution)/shard_map/ppermute | solution.py:31
  973.7 32.5 %collective-permute-start.15 = (f32[8,6,28,256]{3,0,2,1:T(8,128)S(1)}, f32[8,6,28,256]{3,0,2,1:T(8,128)S(1)}, u32[]{:S(2)}, u32[]{:S(2)}) collective-permute-start(f32[8,6,28,256]{3,0,2,1:T(8,128)S(1)} %copy.2543), channel_id=1, source_target_pairs={{4,0},{5,1},{6,2},{7,3},{0,4},{1,5},{2,6},{3,7},{12,8},{13,9},{14,... | collective-permute-start | bytes 4128776 | tf_op jit(solution)/shard_map/ppermute | solution.py:20
  1010.9 12.9 %collective-permute-start.16 = (f32[8,2,28,256]{3,0,2,1:T(8,128)S(1)}, f32[8,2,28,256]{3,0,2,1:T(8,128)S(1)}, u32[]{:S(2)}, u32[]{:S(2)}) collective-permute-start(f32[8,2,28,256]{3,0,2,1:T(8,128)S(1)} %copy.2546), channel_id=1, source_target_pairs={{0,8},{8,16},{16,24},{1,9},{9,17},{17,25},{2,10},{10,18},{18,26},{... | collective-permute-start | bytes 1376264 | tf_op jit(solution)/shard_map/ppermute | solution.py:30
  1014.6 13.6 %collective-permute-start.17 = (f32[8,2,28,256]{3,0,2,1:T(8,128)S(1)}, f32[8,2,28,256]{3,0,2,1:T(8,128)S(1)}, u32[]{:S(2)}, u32[]{:S(2)}) collective-permute-start(f32[8,2,28,256]{3,0,2,1:T(8,128)S(1)} %copy.2548), channel_id=1, source_target_pairs={{8,0},{16,8},{24,16},{9,1},{17,9},{25,17},{10,2},{18,10},{26,18},{... | collective-permute-start | bytes 1376264 | tf_op jit(solution)/shard_map/ppermute | solution.py:31
  1028.8 11.1 %collective-permute-start.18 = (f32[8,24,2,256]{3,1,2,0:T(8,128)S(1)}, f32[8,24,2,256]{3,1,2,0:T(8,128)S(1)}, u32[]{:S(2)}, u32[]{:S(2)}) collective-permute-start(f32[8,24,2,256]{3,1,2,0:T(8,128)S(1)} %copy.2550), channel_id=1, source_target_pairs={{0,1},{1,2},{2,3},{3,4},{4,5},{5,6},{6,7},{7,0},{8,9},{9,10},{10,1... | collective-permute-start | bytes 1179656 | tf_op jit(solution)/shard_map/ppermute | solution.py:30
  1028.9 11.5 %collective-permute-start.19 = (f32[8,24,2,256]{3,1,2,0:T(8,128)S(1)}, f32[8,24,2,256]{3,1,2,0:T(8,128)S(1)}, u32[]{:S(2)}, u32[]{:S(2)}) collective-permute-start(f32[8,24,2,256]{3,1,2,0:T(8,128)S(1)} %copy.2552), channel_id=1, source_target_pairs={{1,0},{2,1},{3,2},{4,3},{5,4},{6,5},{7,6},{0,7},{9,8},{10,9},{11,1... | collective-permute-start | bytes 1179656 | tf_op jit(solution)/shard_map/ppermute | solution.py:31
  (193 other events, 1773.2 us)
where the time goes:
time: 1050 us; the launch traced here: 1040 us
  other arithmetic  758 us (72%)
  waiting for transfers between devices  140 us (13%)
  local copies, waits for them, and re-layouts  106 us (10%)
  starting transfers between devices  37.3 us (4%)
    ppermute x4, waiting for transfers between devices, from_behind(): return lax.ppermute(block, axis, route)  78.9 us
    mul x4, other arithmetic, face_flux(): 0.5 * (lower_part(flux_vals, dim_index) + upper_part(flux_vals, dim_index))  61.1 us
    broadcast_in_dim x6, other arithmetic, face_flux(): normal_vel = velocity[normal]  58.8 us
    broadcast_in_dim x5, other arithmetic, section_rate(): e_azimuth = velocity[1] * magnet[0] - velocity[0] * magnet[1]  48.5 us
    ppermute x8, waiting for transfers between devices, padded_2(): before = lax.ppermute(last, axis, up)  42.3 us
    mul x8, other arithmetic, face_flux(): addend = momentum[component] * normal_vel - magnet[component] * normal_field  39.4 us
    unnamed x423, local copies, waits for them, and re-layouts  37.3 us
    broadcast_in_dim x2, other arithmetic, section_rate(): energy = grid_vals[4, :-1, :-1, :-1]  36.1 us
  transfers between devices with their start and end apart: 20, of which 17 were waited for; matrix products, arithmetic and copies ran while one was open for 3% of the time, Pallas kernels for 0%

commit v1 on v0

v1 whole, which is shorter than its diff:
```python
import functools
import math

import jax
import jax.numpy as jnp
import numpy as np
from jax import lax
from jax.experimental import pallas as pl
from jax.experimental.pallas import tpu as pltpu
from jax.sharding import PartitionSpec as P

GAMMA = 5.0 / 3.0
R_INNER = 1.0
R_OUTER = 3.0
COURANT = 0.4
SPEED_BOUND = 5.0
PRESSURE_SOFT = 0.05
THETA_CUT = 0.1

G1 = GAMMA - 1.0
LANES = 128
PAD = 16
FLIPS = (1.0, 1.0, -1.0, -1.0, 1.0, 1.0, -1.0, -1.0)
SH, SL, AZ, COT, AK, KEEP, N_ROW = 0, 1, 2, 3, 4, 5, 6
INV_V, R_HI2, K_V, INV_MID, INV_LO, LO, HI, INV_SHELL, HALF_HI2, HALF_KV, HALF_LO2, TOP, OPEN = range(13)


class Grid:
    def __init__(self, rows, cols, rads, total_rows, total_cols):
        self.rows, self.cols, self.rads = rows, cols, rads
        self.width = cols + 8
        self.tiles = self.width // 8
        self.slots = PAD + (rows + 4) * self.width + PAD
        self.dth = (math.pi - 2.0 * THETA_CUT) / total_rows
        self.dph = 2.0 * math.pi / total_cols
        self.dr = (R_OUTER - R_INNER) / rads
        self.dt = COURANT * min(self.dr, R_INNER * math.sin(THETA_CUT) * self.dph) / SPEED_BOUND
        self.total_rows = total_rows

    def at(self, j, k):
        return PAD + (j + 2) * self.width + k

    def row_table(self):
        j = np.arange(-2, self.total_rows + 3, dtype=np.float64)
        low = THETA_CUT + j * self.dth
        high, mid = low + self.dth, low + 0.5 * self.dth
        drop = np.cos(low) - np.cos(high)
        keep = np.where((j == 0) | (j == self.total_rows), 0.0, 1.0)
        safe = np.where(np.abs(np.sin(low)) < 1e-6, 1.0, np.sin(low))
        table = np.zeros((len(j), N_ROW))
        table[:, SH] = np.sin(high) / drop
        table[:, SL] = np.sin(low) / drop
        table[:, AZ] = self.dth / (drop * self.dph)
        table[:, COT] = np.cos(mid) / np.sin(mid)
        table[:, AK] = keep / (safe * self.dph)
        table[:, KEEP] = keep
        return table.astype(np.float32)

    def radial_planes(self):
        i = np.arange(self.rads, dtype=np.float64)
        low = R_INNER + i * self.dr
        high, mid = low + self.dr, low + 0.5 * self.dr
        vol = (high**3 - low**3) / 3.0
        shell = 0.5 * (high**2 - low**2)
        top = np.where(i == self.rads - 1, 2.0, 1.0)
        planes = [None] * 13
        planes[INV_V] = 1.0 / vol
        planes[R_HI2] = high**2
        planes[K_V] = shell / vol
        planes[INV_MID] = 1.0 / mid
        planes[INV_LO] = 1.0 / low
        planes[LO] = low
        planes[HI] = high
        planes[INV_SHELL] = 1.0 / shell
        planes[HALF_HI2] = 0.5 * self.dt * high**2
        planes[HALF_KV] = 0.5 * self.dt * shell / vol
        planes[HALF_LO2] = 0.5 * self.dt * low**2
        planes[TOP] = top
        planes[OPEN] = 2.0 - top
        stack = np.stack(planes).astype(np.float32).reshape(13, 2, 1, LANES)
        return np.broadcast_to(stack, (13, 2, 8, LANES)).copy()


def lane_index():
    return lax.broadcasted_iota(jnp.int32, (2, 8, LANES), 2)


def next_r(x, last=None):
    turned = pltpu.roll(x, LANES - 1, 2)
    end = x[1:2] if last is None else last
    return jnp.where(lane_index() == LANES - 1, jnp.concatenate([turned[1:2], end], 0), turned)


def prev_r(x, first):
    turned = pltpu.roll(x, 1, 2)
    return jnp.where(lane_index() == 0, jnp.concatenate([first, turned[0:1]], 0), turned)


def split(x):
    return jnp.stack([x[:, :LANES], x[:, LANES:]])


def load(ref, field, slot):
    return ref[field, :, pl.ds(slot, 8), :]


def put(ref, field, slot, value):
    ref[field, :, pl.ds(slot, 8), :] = value


def put_line(ref, field, slot, line):
    ref[field, 0, pl.ds(slot, 1), :] = line[:, :LANES]
    ref[field, 1, pl.ds(slot, 1), :] = line[:, LANES:]


def get_line(ref, field, slot):
    return jnp.concatenate([ref[field, 0, pl.ds(slot, 1), :], ref[field, 1, pl.ds(slot, 1), :]], 1)


def fill_state(g, us, row_ref, own, phlo, phhi, thlo, thhi):
    rows, cols = g.rows, g.cols

    def keep(j):
        return row_ref[(j + 2) * N_ROW + KEEP]

    def ends(j, fetch):
        for c in range(8):
            scale = keep(j) if c == 6 else None
            for which, k in ((0, -1), (1, cols)):
                line = fetch(c, which)
                put_line(us, c, g.at(j, k), line if scale is None else line * scale)
        put_line(us, 7, g.at(j, cols + 1), fetch(7, 2))

    def body_row(j, tile_of):
        for c in range(8):
            for t in range(cols // 8):
                x = split(tile_of(c, t))
                if c == 6:
                    x = x * keep(j)
                put(us, c, g.at(j, t * 8), x)
                if t == 0:
                    put(us, c, g.at(j, cols), x)

    for c in range(8):
        put(us, c, g.at(-1, -8), split(thlo[c, 0:8, :]))
    body_row(-1, lambda c, t: thlo[c, t * 8 : t * 8 + 8, :])
    ends(-1, lambda c, w: thlo[9, (c, 9 + c, 18)[w] : (c, 9 + c, 18)[w] + 1, :])

    def step(j, carry):
        body_row(j, lambda c, t: own[c, j, t * 8 : t * 8 + 8, :])
        ends(j, lambda c, w: (phlo[c, pl.ds(j, 1), :], phhi[c, pl.ds(j, 1), :], phhi[8, pl.ds(j, 1), :])[w])
        return carry

    lax.fori_loop(0, rows, step, 0)
    body_row(rows, lambda c, t: thhi[c, t * 8 : t * 8 + 8, :])
    ends(rows, lambda c, w: thhi[9, (c, 9 + c, 18)[w] : (c, 9 + c, 18)[w] + 1, :])
    far = keep(rows + 1)
    for t in range(g.tiles):
        x = split(thhi[8, t * 8 : t * 8 + 8, :]) if t < cols // 8 else jnp.zeros((2, 8, LANES), jnp.float32)
        put(us, 6, g.at(rows + 1, t * 8), x * far)
    put_line(us, 6, g.at(rows + 1, -1), thhi[9, 8:9, :] * far)
    put_line(us, 6, g.at(rows + 1, cols), thhi[9, 17:18, :] * far)


def cell_values(g, us, p):
    rho, m0, m1, m2, energy, u5, u6, u7 = [load(us, c, p) for c in range(8)]
    b0 = 0.5 * (u5 + next_r(u5))
    b1 = 0.5 * (u6 + load(us, 6, p + g.width))
    b2 = 0.5 * (u7 + load(us, 7, p + 1))
    q = 1.0 / rho
    v0, v1, v2 = m0 * q, m1 * q, m2 * q
    square = b0 * b0 + b1 * b1 + b2 * b2
    pressure = G1 * (energy - 0.5 * (m0 * v0 + m1 * v1 + m2 * v2) - 0.5 * square)
    total = pressure + 0.5 * square
    soft = pressure * pressure + PRESSURE_SOFT * PRESSURE_SOFT
    inv_soft = lax.rsqrt(soft)
    c2 = (GAMMA * (soft * inv_soft) + square) * q
    return (m0, m1, m2), (v0, v1, v2), (b0, b1, b2), u5, q, pressure, total, energy + total, inv_soft, c2


def forward_kernel(g, row_ref, own, phlo, phhi, thlo, thhi, rc, out, us, cf, gf, ff):
    fill_state(g, us, row_ref, own, phlo, phhi, thlo, thhi)
    w = g.width

    def cells(n, carry):
        p = pl.multiple_of(g.at(-1, -8) + n * 8, 8)
        m, v, b, u5, q, pressure, total, h, inv_soft, c2 = cell_values(g, us, p)
        put(cf, 0, p, m[0] * v[0] - b[0] * b[0] + total)
        put(cf, 1, p, m[0] * v[1] - b[0] * b[1])
        put(cf, 2, p, m[0] * v[2] - b[0] * b[2])
        put(cf, 3, p, m[1] * v[1] - b[1] * b[1] + total)
        put(cf, 4, p, m[1] * v[2] - b[1] * b[2])
        put(cf, 5, p, m[2] * v[2] - b[2] * b[2] + total)
        vb = v[0] * b[0] + v[1] * b[1] + v[2] * b[2]
        for d in range(3):
            put(cf, 6 + d, p, h * v[d] - b[d] * vb)
            put(cf, 9 + d, p, v[d] * v[d] + c2)
        put(cf, 12, p, v[2] * b[1] - v[1] * b[2])
        put(cf, 13, p, v[0] * b[2] - v[2] * b[0])
        put(cf, 14, p, v[1] * b[0] - v[0] * b[1])
        m, v, b = [[x[0:1] for x in y] for y in (m, v, b)]
        bg = u5[0:1]
        gain = (1.0 - 0.5 * GAMMA) * (bg * bg - b[0] * b[0])
        vbg = vb[0:1] + v[0] * (bg - b[0])
        ghost = (
            m[0] * v[0] - bg * bg + total[0:1] + gain,
            m[0] * v[1] - bg * b[1],
            m[0] * v[2] - bg * b[2],
            (h[0:1] + gain) * v[0] - bg * vbg,
            v[0] * b[2] - v[2] * bg,
            v[1] * bg - v[0] * b[1],
        )
        for f, x in enumerate(ghost):
            gf[f, pl.ds(p, 8), :] = x[0]
        return carry

    lax.fori_loop(0, (g.rows + 2) * g.tiles + 1, cells, 0)

    index = ((0, 1, 2), (1, 3, 4), (2, 4, 5))

    def face(d, p, shift):
        fluxes = [load(us, 1 + d, p)] + [load(cf, index[d][c], p) for c in range(3)] + [load(cf, 6 + d, p)]
        speed = load(cf, 9 + d, p)
        state = [load(us, c, p) for c in range(5)]
        if shift is None:
            other = [next_r(x) for x in fluxes]
            speed2 = next_r(speed)
            state2 = [other[0] if c == 1 else next_r(state[c]) for c in range(5)]
        else:
            r = p + shift
            other = [load(us, 1 + d, r)] + [load(cf, index[d][c], r) for c in range(3)] + [load(cf, 6 + d, r)]
            speed2 = load(cf, 9 + d, r)
            state2 = [load(us, c, r) for c in range(5)]
        total = 0.5 * (speed + speed2)
        half = 0.5 * (total * lax.rsqrt(total))
        return fluxes, [0.5 * (fluxes[c] + other[c]) - half * (state2[c] - state[c]) for c in range(5)]

    def faces(n, carry):
        p = pl.multiple_of(g.at(-1, 0) + n * 8, 8)
        for d, shift, base in ((1, w, 0), (2, 1, 5)):
            _, flux = face(d, p, shift)
            for c in range(5):
                put(ff, base + c, p, flux[c])
        return carry

    lax.fori_loop(0, (g.rows + 1) * g.tiles, faces, 0)

    own_tiles = g.cols // 8

    def combine(n, carry):
        j = n // own_tiles
        t = n - j * own_tiles
        p = pl.multiple_of(g.at(j, t * 8), 8)
        row = (j + 2) * N_ROW
        sh, sl, az, cot, ak, keep = [row_ref[row + i] for i in range(N_ROW)]
        cells_here, flux_r = face(0, p, None)
        ghost = [load(us, 1, p)[0:1]] + [gf[f, pl.ds(p, 8), :][None] for f in range(4)]
        inv_v, kv = rc[INV_V], rc[K_V]
        rates = []
        for c in range(5):
            high = rc[R_HI2] * flux_r[c]
            first = 0.5 * rc[HALF_LO2][0:1] * (2.0 / g.dt) * (ghost[c] + cells_here[c][0:1])
            low = prev_r(high, first)
            th = sh * load(ff, c, p) - sl * load(ff, c, p - w)
            ph = az * (load(ff, 5 + c, p) - load(ff, 5 + c, p - 1))
            rates.append(-(inv_v * (high - low) + kv * (th + ph)))
        tt = [load(cf, f, p) for f in range(1, 6)]
        mid = rc[INV_MID]
        rates[1] = rates[1] + (tt[2] + tt[4]) * mid
        rates[2] = rates[2] + (cot * tt[4] - tt[0]) * mid
        rates[3] = rates[3] - (tt[1] + cot * tt[3]) * mid
        ep, ept = load(cf, 14, p), load(cf, 14, p + w)
        x0 = load(cf, 14, p - w) + ep
        x1 = ep + ept
        g_here = gf[5, pl.ds(p, 8), :][None]
        x0m = prev_r(x0, gf[5, pl.ds(p - w, 8), :][None] + g_here)
        x1m = prev_r(x1, g_here + gf[5, pl.ds(p + w, 8), :][None])
        z0 = 0.25 * (x0 + x0m)
        zr = 0.25 * (next_r(x0) + x0)
        z1 = 0.25 * (x1 + x1m)
        et = load(cf, 13, p)
        y0 = load(cf, 13, p - 1) + et
        y1 = et + load(cf, 13, p + 1)
        g_here = gf[4, pl.ds(p, 8), :][None]
        y0m = prev_r(y0, gf[4, pl.ds(p - 1, 8), :][None] + g_here)
        y1m = prev_r(y1, g_here + gf[4, pl.ds(p + 1, 8), :][None])
        p0 = 0.25 * (y0 + y0m)
        pr = 0.25 * (next_r(y0) + y0)
        p1 = 0.25 * (y1 + y1m)
        er, era, erb = load(cf, 12, p), load(cf, 12, p - 1), load(cf, 12, p - w)
        r0 = 0.25 * (er + era + erb + load(cf, 12, p - w - 1))
        r1 = 0.25 * (load(cf, 12, p + 1) + er + load(cf, 12, p - w + 1) + erb)
        rt = 0.25 * (load(cf, 12, p + w) + load(cf, 12, p + w - 1) + er + era)
        lo, hi, shell = rc[LO], rc[HI], rc[INV_SHELL]
        rates.append(-rc[INV_LO] * (sh * z1 - sl * z0 - az * (p1 - p0)))
        rates.append(-shell * (g.dr * ak * (r1 - r0) - keep * (hi * zr - lo * z0)))
        rates.append(shell * ((g.dr / g.dth) * (rt - r0) - (hi * pr - lo * p0)))
        for c in range(8):
            new = own[c, j, pl.ds(pl.multiple_of(t * 8, 8), 8), :] + g.dt * jnp.concatenate([rates[c][0], rates[c][1]], 1)
            out[c, j, pl.ds(pl.multiple_of(t * 8, 8), 8), :] = new
        return carry

    lax.fori_loop(0, g.rows * own_tiles, combine, 0)


def adjoint_kernel(
    g, row_ref, own, phlo, phhi, thlo, thhi, cot_ref, rc, out, gphlo, gphhi, gthlo, gthhi, us, cs, cf, ef, zf, ft, fp
):
    fill_state(g, us, row_ref, own, phlo, phhi, thlo, thhi)
    w, rows, cols = g.width, g.rows, g.cols
    zero = jnp.zeros((2, 8, LANES), jnp.float32)

    def clear(n, carry):
        p = pl.multiple_of(n * 8, 8)
        for c in range(8):
            put(cs, c, p, zero)
        return carry

    lax.fori_loop(0, g.slots // 8, clear, 0)

    def take(j, carry):
        for c in range(8):
            for t in range(cols // 8):
                put(cs, c, g.at(j, t * 8), split(cot_ref[c, j, t * 8 : t * 8 + 8, :]))
        return carry

    lax.fori_loop(0, rows, take, 0)

    def cells(n, carry):
        p = pl.multiple_of(g.at(-1, -8) + n * 8, 8)
        m, v, b, u5, q, pressure, total, h, inv_soft, c2 = cell_values(g, us, p)
        for d in range(3):
            put(cf, d, p, v[d])
            put(cf, 3 + d, p, b[d])
            put(cf, 6 + d, p, v[d] * v[d] + c2)
        put(cf, 9, p, h)
        put(cf, 10, p, q)
        put(cf, 11, p, GAMMA * q * (pressure * inv_soft))
        put(cf, 12, p, c2 * q)
        return carry

    lax.fori_loop(0, (rows + 2) * g.tiles + 1, cells, 0)

    none = jnp.zeros((1, 8, LANES), jnp.float32)

    def edges(n, carry):
        p = pl.multiple_of(g.at(-1, -8) + n * 8, 8)
        j = (n + g.tiles - 1) // g.tiles - 2
        row = (j + 2) * N_ROW
        sl, az, ak, keep = [row_ref[row + i] for i in (SL, AZ, AK, KEEP)]
        sh_below = row_ref[jnp.maximum(row - N_ROW, 0) + SH]
        shell, lo, hi = rc[INV_SHELL], rc[LO], rc[HI]
        c5, c6, c7 = load(cs, 5, p), load(cs, 6, p), load(cs, 7, p)
        rb = ak * (c6 - load(cs, 6, p - 1)) + (1.0 / g.dth) * (load(cs, 7, p - w) - c7)
        put(ef, 0, p, (0.25 * g.dt * g.dr) * shell * rb)
        q6 = keep * c6 * shell
        zb = rc[INV_LO] * (sl * c5 - sh_below * load(cs, 5, p - w)) + prev_r(hi * q6, none) - lo * q6
        q7 = c7 * shell
        hq7 = hi * q7
        pb = rc[INV_LO] * az * (load(cs, 5, p - 1) - c5) + lo * q7 - prev_r(hq7, none)
        zl = 2.0 * hi[1:2] * q6[1:2]
        plast = -2.0 * hq7[1:2]
        put(ef, 1, p, (0.25 * g.dt) * (zb + next_r(zb, zl)))
        put(ef, 2, p, (0.25 * g.dt) * (pb + next_r(pb, plast)))
        zf[0, pl.ds(p, 8), :] = (0.25 * g.dt) * zb[0]
        zf[1, pl.ds(p, 8), :] = (0.25 * g.dt) * pb[0]
        return carry

    lax.fori_loop(0, (rows + 3) * g.tiles + 1, edges, 0)

    for f in range(11):
        for t in range(g.tiles):
            put(ft, f, t * 8, zero)
        for t in range(2):
            put(fp, f, t * 8, zero)

    def face_pull(halves, state, state2, speed, speed2, closed=None):
        total = 0.5 * (speed + speed2)
        inv = lax.rsqrt(total)
        a = total * inv
        if closed is not None:
            a = a * closed
        dot = halves[0] * (state2[0] - state[0])
        for c in range(1, 5):
            dot = dot + halves[c] * (state2[c] - state[c])
        return halves + [a * x for x in halves] + [-0.25 * inv * dot]

    def pull(n, carry):
        p = pl.multiple_of(g.at(-1, -8) + n * 8, 8)
        j = n // g.tiles - 1
        slot = pl.multiple_of(lax.rem(n + g.tiles - 1, g.tiles) * 8, 8)
        row = (j + 2) * N_ROW
        sh, az, cot = [row_ref[row + i] for i in (SH, AZ, COT)]
        sl_above = row_ref[row + N_ROW + SL]
        state = [load(us, c, p) for c in range(5)]
        cc = [load(cs, c, p) for c in range(5)]
        kd = rc[HALF_KV]
        sides = []
        up = kd * sl_above
        down = kd * sh
        pw = pl.multiple_of(p + jnp.where(n > (rows + 1) * g.tiles, 0, w), 8)
        high = face_pull(
            [up * load(cs, c, pw) - down * cc[c] for c in range(5)],
            state,
            [load(us, c, pw) for c in range(5)],
            load(cf, 7, p),
            load(cf, 7, pw),
        )
        low = [load(ft, f, slot) for f in range(11)]
        for f in range(11):
            put(ft, f, slot, high[f])
        sides.append((high, low))
        kaz = kd * az
        high_p = face_pull(
            [kaz * (load(cs, c, p + 1) - cc[c]) for c in range(5)],
            state,
            [load(us, c, p + 1) for c in range(5)],
            load(cf, 8, p),
            load(cf, 8, p + 1),
        )
        for f in range(11):
            put(fp, f, 8, high_p[f])
        per_volume = [rc[INV_V] * x for x in cc]
        half_hi = rc[HALF_HI2]
        speed = load(cf, 6, p)
        high_r = face_pull(
            [half_hi * (next_r(x, none) - x) for x in per_volume],
            state,
            [next_r(x) for x in state],
            speed,
            next_r(speed),
            rc[OPEN],
        )
        first = [rc[HALF_LO2][0:1] * x[0:1] for x in per_volume]
        low_r = [prev_r(high_r[f], first[f] if f < 5 else none) for f in range(11)]
        low_p = [load(fp, f, 7) for f in range(11)]
        for f in range(11):
            fp[f, :, 7:8, :] = fp[f, :, 15:16, :]
        sides.append((high_p, low_p))
        ft_, fp_ = [[hi_[c] + lo_[c] for c in range(5)] for hi_, lo_ in sides]
        fr_ = [rc[TOP] * high_r[c] + low_r[c] for c in range(5)]
        both = [(high_r, low_r)] + sides
        ub = []
        for c in range(5):
            ub.append(
                cc[c]
                + (both[0][0][5 + c] - both[0][1][5 + c])
                + (both[1][0][5 + c] - both[1][1][5 + c])
                + (both[2][0][5 + c] - both[2][1][5 + c])
            )
        sb = [hi_[10] + lo_[10] for hi_, lo_ in both]
        mid = rc[INV_MID] * g.dt
        w1, w2, w3 = cc[1] * mid, cc[2] * mid, cc[3] * mid
        s00, s11 = fr_[1], ft_[2] + w1
        s22 = fp_[3] + w1 + cot * w2
        s01 = fr_[2] + ft_[1] - w2
        s02 = fr_[3] + fp_[1] - w3
        s12 = ft_[3] + fp_[2] - cot * w3
        e0 = load(ef, 0, p) + load(ef, 0, p + 1) + load(ef, 0, p + w) + load(ef, 0, p + w + 1)
        e2 = load(ef, 1, p) + load(ef, 1, p + w)
        e1 = load(ef, 2, p) + load(ef, 2, p + 1)
        v = [load(cf, d, p) for d in range(3)]
        b = [load(cf, 3 + d, p) for d in range(3)]
        h, q = load(cf, 9, p), load(cf, 10, p)
        gg = (fr_[4], ft_[4], fp_[4])
        flow = v[0] * gg[0] + v[1] * gg[1] + v[2] * gg[2]
        beta = b[0] * gg[0] + b[1] * gg[1] + b[2] * gg[2]
        vb = v[0] * b[0] + v[1] * b[1] + v[2] * b[2]
        d00, d11, d22 = s00 + s00, s11 + s11, s22 + s22
        sv = (
            d00 * v[0] + s01 * v[1] + s02 * v[2],
            s01 * v[0] + d11 * v[1] + s12 * v[2],
            s02 * v[0] + s12 * v[1] + d22 * v[2],
        )
        sbm = (
            d00 * b[0] + s01 * b[1] + s02 * b[2],
            s01 * b[0] + d11 * b[1] + s12 * b[2],
            s02 * b[0] + s12 * b[1] + d22 * b[2],
        )
        c2b = sb[0] + sb[1] + sb[2]
        ptb = s00 + s11 + s22 + flow
        pb = c2b * load(cf, 11, p) + ptb
        pg = G1 * pb
        bbb = 2.0 * (c2b * q) + ptb - pg
        bxe = (b[1] * e2 - b[2] * e1, b[2] * e0 - b[0] * e2, b[0] * e1 - b[1] * e0)
        exv = (e1 * v[2] - e2 * v[1], e2 * v[0] - e0 * v[2], e0 * v[1] - e1 * v[0])
        rho_bar = ub[0] - c2b * load(cf, 12, p)
        m_bar, b_bar = [], []
        for d in range(3):
            vbar = h * gg[d] - beta * b[d] + 2.0 * (v[d] * sb[d]) - bxe[d]
            turn = q * vbar - pg * v[d]
            f0 = (fr_[0], ft_[0], fp_[0])[d]
            m_bar.append(ub[1 + d] + f0 + sv[d] + turn)
            rho_bar = rho_bar - v[d] * (0.5 * sv[d] + turn + 0.5 * (pg * v[d]))
            b_bar.append(b[d] * bbb - sbm[d] - vb * gg[d] - beta * v[d] - exv[d])
        e_bar = ub[4] + flow + pg

        first_lane = lax.broadcasted_iota(jnp.int32, (1, 8, LANES), 2) == 0
        v, b = [[x[0:1] for x in y] for y in (v, b)]
        q, h = q[0:1], h[0:1]
        bg = load(us, 5, p)[0:1]
        h = h + (1.0 - 0.5 * GAMMA) * (bg * bg - b[0] * b[0])
        vbg = vb[0:1] + v[0] * (bg - b[0])
        s00, s01, s02, g0 = first[1], first[2], first[3], first[4]
        e2 = (zf[0, pl.ds(p, 8), :] + zf[0, pl.ds(p + w, 8), :])[None]
        e1 = (zf[1, pl.ds(p, 8), :] + zf[1, pl.ds(p + 1, 8), :])[None]
        flow = v[0] * g0
        beta = bg * g0
        pb = s00 + flow
        pg = G1 * pb
        bbb = pb - pg
        d00 = s00 + s00
        sv = (d00 * v[0] + s01 * v[1] + s02 * v[2], s01 * v[0], s02 * v[0])
        sbm = (d00 * bg + s01 * b[1] + s02 * b[2], s01 * bg, s02 * bg)
        vbar = (
            h * g0 - beta * bg - (b[1] * e2 - b[2] * e1),
            bg * e2 - beta * b[1],
            -(beta * b[2]) - bg * e1,
        )
        exv = (e1 * v[2] - e2 * v[1], e2 * v[0], -(e1 * v[0]))
        more = [None] * 8
        rho_more = none
        for d in range(3):
            turn = q * vbar[d] - pg * v[d]
            more[1 + d] = sv[d] + turn + (first[0] if d == 0 else 0.0)
            rho_more = rho_more - v[d] * (0.5 * sv[d] + turn + 0.5 * (pg * v[d]))
            bd = bg if d == 0 else b[d]
            more[5 + d] = bd * bbb - sbm[d] - beta * v[d] - exv[d]
        more[5] = more[5] - vbg * g0
        more[0] = rho_more
        more[4] = flow + pg

        def with_first(x, extra):
            return x + jnp.concatenate([jnp.where(first_lane, extra, 0.0), none], 0)

        put(us, 0, p, with_first(rho_bar, more[0]))
        for d in range(3):
            put(us, 1 + d, p, with_first(m_bar[d], more[1 + d]))
        put(us, 4, p, with_first(e_bar, more[4]))
        put(us, 5, p, load(cs, 5, p) + 0.5 * (rc[TOP] * b_bar[0] + prev_r(b_bar[0], 2.0 * more[5])))
        put(us, 6, p, with_first(b_bar[1], more[6]))
        put(us, 7, p, with_first(b_bar[2], more[7]))
        return carry

    lax.fori_loop(0, (rows + 2) * g.tiles + 1, pull, 0)

    def keep_of(j):
        return 0.5 * row_ref[(j + 2) * N_ROW + KEEP]

    def tile6(j, p):
        return keep_of(j) * (load(us, 6, p) + load(us, 6, p - w))

    def tile7(p):
        return 0.5 * (load(us, 7, p) + load(us, 7, p - 1))

    def join(x):
        return jnp.concatenate([x[0], x[1]], 1)

    def line_of(c, j, k):
        p = g.at(j, k)
        if c < 6:
            return get_line(us, c, p)
        if c == 6:
            here = get_line(us, 6, p)
            if isinstance(j, int) and j == -1:
                return keep_of(j) * here
            return keep_of(j) * (here + get_line(us, 6, p - w))
        here = get_line(us, 7, p)
        return 0.5 * here if k == -1 else 0.5 * (here + get_line(us, 7, p - 1))

    def give(j, carry):
        for t in range(cols // 8):
            p = g.at(j, t * 8)
            at = (j, slice(t * 8, t * 8 + 8))
            for c in range(6):
                out[(c,) + at] = join(load(us, c, p))
            out[(6,) + at] = join(load(cs, 6, p) + tile6(j, p))
            out[(7,) + at] = join(load(cs, 7, p) + tile7(p))
        for c in range(8):
            gphlo[c, pl.ds(j, 1), :] = line_of(c, j, -1)
            gphhi[c, pl.ds(j, 1), :] = line_of(c, j, cols)
        gphhi[8, pl.ds(j, 1), :] = 0.5 * get_line(us, 7, g.at(j, cols))
        return carry

    lax.fori_loop(0, rows, give, 0)

    for ref, j in ((gthlo, -1), (gthhi, rows)):
        for t in range(cols // 8):
            p = g.at(j, t * 8)
            at = slice(t * 8, t * 8 + 8)
            for c in range(6):
                ref[c, at] = join(load(us, c, p))
            ref[6, at] = join(keep_of(j) * load(us, 6, p) if j < 0 else tile6(j, p))
            ref[7, at] = join(tile7(p))
            ref[8, at] = jnp.zeros((8, 2 * LANES), jnp.float32) if j < 0 else join(keep_of(j + 1) * load(us, 6, p))
        ref[9] = jnp.zeros((cols, 2 * LANES), jnp.float32)
        for k, base in ((-1, 0), (cols, 9)):
            for c in range(8):
                ref[9, base + c : base + c + 1] = line_of(c, j, k)
            if j > 0:
                ref[9, base + 8 : base + 9] = keep_of(j + 1) * get_line(us, 6, g.at(j, k))
        ref[9, 18:19] = 0.5 * get_line(us, 7, g.at(j, cols))


def call(kernel, outs, scratch, n_in, flops, interpret=False):
    vmem = pl.BlockSpec(memory_space=pltpu.VMEM)
    return pl.pallas_call(
        kernel,
        out_shape=[jax.ShapeDtypeStruct(s, jnp.float32) for s in outs],
        in_specs=[pl.BlockSpec(memory_space=pltpu.SMEM)] + [vmem] * n_in,
        out_specs=[vmem] * len(outs),
        scratch_shapes=[pltpu.VMEM(s, jnp.float32) for s in scratch],
        compiler_params=pltpu.CompilerParams(vmem_limit_bytes=62 << 20),
        cost_estimate=pl.CostEstimate(flops=flops, bytes_accessed=16 << 20, transcendentals=0),
        interpret=interpret,
    )


def forward(g, table, own, halos, planes, interpret=False):
    n = g.slots
    shape = (8, g.rows, g.cols, g.rads)
    scratch = [(8, 2, n, LANES), (15, 2, n, LANES), (6, n, LANES), (10, 2, n, LANES)]
    run = call(functools.partial(forward_kernel, g), [shape], scratch, 6, 10**8, interpret)
    return run(table, own, *halos, planes)[0]


def adjoint(g, table, own, halos, cot, planes, interpret=False):
    n = g.slots
    shape = (8, g.rows, g.cols, g.rads)
    outs = [shape, (8, g.rows, g.rads), (9, g.rows, g.rads), (10, g.cols, g.rads), (10, g.cols, g.rads)]
    scratch = [
        (8, 2, n, LANES),
        (8, 2, n, LANES),
        (13, 2, n, LANES),
        (3, 2, n, LANES),
        (2, n, LANES),
        (11, 2, g.width, LANES),
        (11, 2, 16, LANES),
    ]
    run = call(functools.partial(adjoint_kernel, g), outs, scratch, 7, 3 * 10**8, interpret)
    return run(table, own, *halos, cot, planes)


class Place:
    def __init__(self):
        self.n_th, self.n_ph = lax.axis_size("th"), lax.axis_size("ph")
        n_th, n_ph = self.n_th, self.n_ph
        half = n_ph // 2
        self.th, self.ph = lax.axis_index("th"), lax.axis_index("ph")
        self.at_bottom, self.at_top = self.th == 0, self.th == n_th - 1
        self.near = self.ph < half
        self.right = [(i, (i + 1) % n_ph) for i in range(n_ph)]
        self.left = [(j, i) for i, j in self.right]
        self.round = []
        for t in range(n_th):
            for p in range(half):
                self.round.append((t * n_ph + p, (t + 1) * n_ph + p if t < n_th - 1 else t * n_ph + p + half))
                self.round.append((t * n_ph + p + half, (t - 1) * n_ph + p + half if t > 0 else p))
        self.back = [(j, i) for i, j in self.round]

    def polar_exchange(self, low, high):
        ahead = lax.ppermute(jnp.where(self.near, high, low), ("th", "ph"), self.round)
        behind = lax.ppermute(jnp.where(self.near, low, high), ("th", "ph"), self.back)
        return jnp.where(self.near, ahead, behind), jnp.where(self.near, behind, ahead)


def flipped(rows, signs=FLIPS):
    return rows * jnp.array(signs, jnp.float32).reshape((-1,) + (1,) * (rows.ndim - 1))


def halos_of(place, state):
    rows, cols, rads = state.shape[1:]
    last = state[:, :, cols - 1]
    first = jnp.concatenate([state[:, :, 0], state[7:8, :, 1]], 0)
    phlo = lax.ppermute(last, "ph", place.right)
    phhi = lax.ppermute(first, "ph", place.left)

    def row_set(j, jface):
        plane = [phlo[:, j], phlo[6:7, jface], phhi[:8, j], phhi[6:7, jface], phhi[8:9, j], jnp.zeros((cols - 19, rads), jnp.float32)]
        return jnp.concatenate([state[:, j], state[6:7, jface], jnp.concatenate(plane, 0)[None]], 0)

    def corner_signs(s):
        return np.array(s + s + (-1.0,) + (1.0,) * (cols - 19), np.float32)[:, None]

    nine = FLIPS + (-1.0,)
    low = row_set(0, 1)
    high = row_set(rows - 1, rows - 1)

    def across(pack, bottom):
        body, plane = flipped(pack[:9], nine), pack[9] * corner_signs(nine)
        if bottom:
            body = jnp.concatenate([body[:6], body[8:9], body[7:]], 0)
            plane = jnp.concatenate([plane[:6], plane[8:9], plane[7:15], plane[17:18], plane[16:]], 0)
        return jnp.concatenate([body, plane[None]], 0)

    low = jnp.where(place.at_bottom, across(row_set(0, 2), True), low)
    high = jnp.where(place.at_top, across(high, False), high)
    thlo, thhi = place.polar_exchange(low, high)
    return phlo, phhi, thlo, thhi


def fold(place, parts):
    cot, gphlo, gphhi, gthlo, gthhi = parts
    rows, cols = cot.shape[1:3]
    body = gthlo[:9]
    plane = gthlo[9]
    body_b = jnp.concatenate([flipped(body[:6], FLIPS[:6]), 0.0 * body[6:7], -body[7:8], -body[6:7]], 0)
    signs6 = np.array(FLIPS[:6], np.float32)[:, None]

    def corner_b(x):
        return [x[:6] * signs6, 0.0 * x[6:7], -x[7:8], -x[6:7]]

    plane_b = jnp.concatenate(corner_b(plane[:9]) + corner_b(plane[9:18]) + [-plane[18:19], plane[19:]], 0)
    low = jnp.where(place.at_bottom, jnp.concatenate([body_b, plane_b[None]], 0), gthlo)
    body, plane = gthhi[:9], gthhi[9]
    body_t = jnp.concatenate([flipped(body[:6], FLIPS[:6]), -body[8:9], -body[7:8], 0.0 * body[8:9]], 0)

    def corner_t(x):
        return [x[:6] * signs6, -x[8:9], -x[7:8], 0.0 * x[8:9]]

    plane_t = jnp.concatenate(corner_t(plane[:9]) + corner_t(plane[9:18]) + [-plane[18:19], plane[19:]], 0)
    high = jnp.where(place.at_top, jnp.concatenate([body_t, plane_t[None]], 0), gthhi)
    from_low, from_high = place.polar_exchange(low, high)

    one = jnp.where(place.at_bottom, 0.0, 1.0)
    for got, j in ((from_low, 0), (from_high, rows - 1)):
        cot = cot.at[:, j].add(got[:8])
        plane = got[9]
        gphlo = gphlo.at[:, j].add(plane[:8])
        gphhi = gphhi.at[:, j].add(jnp.concatenate([plane[9:17], plane[18:19]], 0))
    for jface, share in ((1, one), (2, 1.0 - one)):
        cot = cot.at[6, jface].add(share * from_low[8])
        gphlo = gphlo.at[6, jface].add(share * from_low[9, 8])
        gphhi = gphhi.at[6, jface].add(share * from_low[9, 17])
    from_right = lax.ppermute(gphlo, "ph", place.left)
    from_left = lax.ppermute(gphhi, "ph", place.right)
    cot = cot.at[:, :, cols - 1].add(from_right)
    cot = cot.at[:, :, 0].add(from_left[:8])
    return cot.at[7, :, 1].add(from_left[8])


def shards(state, cotangent):
    place = Place()
    _, rows, cols, rads = state.shape
    g = Grid(rows, cols, rads, rows * place.n_th, cols * place.n_ph)
    table = lax.dynamic_slice_in_dim(jnp.asarray(g.row_table()), place.th * rows, rows + 5, 0).reshape(-1)
    planes = jnp.asarray(g.radial_planes())
    half_cot = 0.5 * cotangent
    halos_zero = halos_of(place, state)
    moved = forward(g, table, state, halos_zero, planes)
    halos_one = halos_of(place, moved)
    cot_one = fold(place, adjoint(g, table, moved, halos_one, half_cot, planes))
    last = fold(place, adjoint(g, table, state, halos_zero, cot_one, planes))
    return half_cot + last


def solution(mesh):
    placed = (P(None, "th", "ph", None), P(None, "th", "ph", None))
    return jax.shard_map(
        shards, mesh=mesh, in_specs=placed, out_specs=P(None, "th", "ph", None), check_vma=False
    )
```

time: 1050 us -> 334 us (0.32)
  other arithmetic: 758 us -> 52.8 us
  Pallas kernels: 0 us -> 169 us
  waiting for transfers between devices: 140 us -> 30.1 us
  local copies, waits for them, and re-layouts: 106 us -> 62.5 us
  starting transfers between devices: 37.3 us -> 16.1 us
    broadcast_in_dim x25 -> x0, other arithmetic: 193 us -> none  [the longest x6 58.8 us: face_flux(): normal_vel = velocity[normal]]
    mul x55 -> x8, other arithmetic: 181 us -> 3.44 us  [the longest x2 1.64 us: corner_b(): return [x[:6] * signs6, 0.0 * x[6:7], -x[7:8], -x[6:7]]]
    pallas_call x0 -> x3, Pallas kernels: none -> 169 us  [the longest x2 135 us: adjoint(): return run(table, own, *halos, cot, planes)]
    add_any x26 -> x0, other arithmetic: 157 us -> none  [the longest x2 32.9 us: section_rate(): velocity = momentum / density]
    ppermute x20 -> x16, waiting for transfers between devices: 140 us -> 30.1 us  [the longest x2 10 us: fold(): from_left = lax.ppermute(gphhi, 'ph', place.right)]
    neg x4, other arithmetic: 54 us -> 3.2 us  [fold(): -plane[18:19]]
    unnamed x423 -> x19, local copies, waits for them, and re-layouts: 37.3 us -> 0.2 us
    concatenate x10 -> x2, other arithmetic: 36 us -> 0.04 us  [halos_of(): first = jnp.concatenate([state[:, :, 0], state[7:8, :, 1]], 0)]
  transfers between devices with their start and end apart: 20 -> 16, of which waited for: 17 -> 11; matrix products, arithmetic and copies ran while one was open for 3% -> 12% of each run, Pallas kernels for 0% -> 0%
where the time goes in v1:
time: 334 us; the launch traced here: 331 us
  Pallas kernels  169 us (51%)
  local copies, waits for them, and re-layouts  62.5 us (19%)
  other arithmetic  52.8 us (16%)
  waiting for transfers between devices  30.1 us (9%)
  starting transfers between devices  16.1 us (5%)
    pallas_call x2, Pallas kernels, adjoint(): return run(table, own, *halos, cot, planes)  135 us
    pallas_call x1, Pallas kernels, forward(): return run(table, own, *halos, planes)[0]  33.6 us
    scatter-add x2, local copies, waits for them, and re-layouts, fold(): cot = cot.at[6, jface].add(share * from_low[8])  14.5 us
    unnamed x14, other arithmetic  11 us
    ppermute x2, waiting for transfers between devices, fold(): from_left = lax.ppermute(gphhi, 'ph', place.right)  10 us
    pallas_call x5, local copies, waits for them, and re-layouts, adjoint(): return run(table, own, *halos, cot, planes)  9.16 us
    scatter-add x1, local copies, waits for them, and re-layouts, fold(): cot = cot.at[:, :, 0].add(from_left[:8])  7.25 us
    ppermute x4, starting transfers between devices, polar_exchange(): lax.ppermute(jnp.where(self.near, high, low), ('th', 'ph'), self.round)  6.85 us
  transfers between devices with their start and end apart: 16, of which 11 were waited for; matrix products, arithmetic and copies ran while one was open for 12% of the time, Pallas kernels for 0%

profile of v1, /device:TPU:0, one launch (start us, length us, event | category | flops | bytes accessed | tf_op | source)
XLA Modules:
  0.0 331.1 jit_solution(17237234875023377019)
XLA Ops:
  0.0 2.2 fusion.37
  3.2 3.4 %collective-permute-start.1 = (f32[9,24,256]{2,1,0:T(8,128)S(1)}, f32[9,24,256]{2,1,0:T(8,128)S(1)}, u32[]{:S(2)}, u32[]{:S(2)}) collective-permute-start(f32[9,24,256]{2,1,0:T(8,128)S(1)} %pad_maximum_fusion), channel_id=1, source_target_pairs={{1,0},{2,1},{3,2},{4,3},{5,4},{6,5},{7,6},{0,7},{9,8},{10,9},{11,1... | collective-permute-start | bytes 663560 | tf_op jit(solution)/shard_map/ppermute | solution.py:676
  9.4 3.8 %collective-permute-done = f32[8,24,256]{2,0,1:T(8,128)S(1)} collective-permute-done((f32[8,24,256]{2,0,1:T(8,128)S(1)}, f32[8,24,256]{2,0,1:T(8,128)S(1)}, u32[]{:S(2)}, u32[]{:S(2)}) %collective-permute-start) | collective-permute-done | bytes 196640 | tf_op jit(solution)/shard_map/ppermute | solution.py:675
  19.1 2.0 collective-permute-done.2
  23.5 33.6 %shard_map.172.own = f32[8,24,24,256]{3,2,1,0:T(8,128)} custom-call(f32[174]{0:T(256)} %reshape.1611.row_ref, f32[8,24,24,256]{3,2,1,0:T(8,128)} %own.3, f32[8,24,256]{2,1,0:T(8,128)} %copy.96.phlo, f32[9,24,256]{2,1,0:T(8,128)} %copy-done, f32[10,24,256]{2,1,0:T(8,128)} %get-tuple-element.410.thlo, f32[10,24,256]{2,1,0:T(8,128)} %get-tuple-element.409.thhi, ...), custom_call_target="tpu_custom_call" | custom-call | flops 100000000 | bytes 16777216 | tf_op jit(solution)/shard_map/pallas_call | solution.py:624
  59.0 2.2 fusion.36
  62.5 2.7 collective-permute-start.5
  65.1 2.1 collective-permute-done.4
  69.6 1.6 collective-permute-start.6
  71.6 5.4 %copy_multiply_fusion = f32[8,24,24,256]{3,0,2,1:T(8,128)S(1)} fusion(f32[8,24,24,256]{3,2,1,0:T(8,128)} %param.79), kind=kLoop, calls=%fused_computation | loop fusion | flops 1179648 | bytes 9437184 | tf_op jit(solution)/shard_map/mul | solution.py:748
  77.0 3.6 %copy.81.cot_ref = f32[8,24,24,256]{3,2,1,0:T(8,128)} copy(f32[8,24,24,256]{3,0,2,1:T(8,128)S(1)} %copy_multiply_fusion) | data formatting | bytes 9437184 | tf_op jit(solution)/shard_map/mul | solution.py:748
  82.2 67.7 %shard_map.173 = (f32[8,24,24,256]{3,2,1,0:T(8,128)}, f32[8,24,256]{2,1,0:T(8,128)}, f32[9,24,256]{2,1,0:T(8,128)}, f32[10,24,256]{2,1,0:T(8,128)}, f32[10,24,256]{2,1,0:T(8,128)}) custom-call(f32[174]{0:T(256)} %reshape.1611.row_ref, f32[8,24,24,256]{3,2,1,0:T(8,128)} %shard_map.172.own, f32[8,24,256]{2,1,0:T(8,128)} %copy.80.phlo, ...), custom_call_target="tpu_custom_call" | custom-call | flops 300000000 | bytes 16777216 | tf_op jit(solution)/shard_map/pallas_call | solution.py:641
  160.4 1.7 collective-permute-start.8
  164.5 5.1 %copy.82 = f32[8,24,24,256]{3,2,0,1:T(8,128)} copy(f32[8,24,24,256]{3,2,1,0:T(8,128)} %get-tuple-element.375) | data formatting | bytes 9437184 | tf_op jit(solution)/shard_map/pallas_call | solution.py:641
  171.9 1.7 fusion.12
  173.6 1.7 fusion.9
  177.9 7.3 %copy.89 = f32[8,24,24,256]{3,0,1,2:T(8,128)} copy(f32[8,24,24,256]{3,2,1,0:T(8,128)} %fusion.19) | data formatting | bytes 9437184 | tf_op jit(solution)/shard_map/scatter-add | solution.py:732
  187.6 7.3 %collective-permute-done.11 = f32[9,24,256]{2,0,1:T(8,128)S(1)} collective-permute-done((f32[9,24,256]{2,0,1:T(8,128)S(1)}, f32[9,24,256]{2,0,1:T(8,128)S(1)}, u32[]{:S(2)}, u32[]{:S(2)}) %collective-permute-start.11) | collective-permute-done | bytes 221216 | tf_op jit(solution)/shard_map/ppermute | solution.py:736
  196.6 7.2 %copy.95 = f32[8,24,24,256]{3,2,1,0:T(8,128)} copy(f32[8,24,24,256]{3,0,1,2:T(8,128)} %fusion.7) | data formatting | bytes 9437184 | tf_op jit(solution)/shard_map/scatter-add | solution.py:738
  204.8 1.7 scatter-add.124.cot_ref
  206.5 67.7 %shard_map.174 = (f32[8,24,24,256]{3,2,1,0:T(8,128)}, f32[8,24,256]{2,1,0:T(8,128)}, f32[9,24,256]{2,1,0:T(8,128)}, f32[10,24,256]{2,1,0:T(8,128)}, f32[10,24,256]{2,1,0:T(8,128)}) custom-call(f32[174]{0:T(256)} %reshape.1611.row_ref, f32[8,24,24,256]{3,2,1,0:T(8,128)} %own.3, f32[8,24,256]{2,1,0:T(8,128)} %copy.96.phlo, f32[9,24,256]{2,1,0:T(8,128)} %copy-done, ...), custom_call_target="tpu_custom_call" | custom-call | flops 300000000 | bytes 16777216 | tf_op jit(solution)/shard_map/pallas_call | solution.py:641
  284.7 1.8 collective-permute-start.12
  288.8 2.1 collective-permute-done.12
  291.0 1.8 collective-permute-done.13
  292.9 1.6 fusion.5
  298.8 7.2 %copy.102 = f32[8,24,24,256]{3,0,2,1:T(8,128)} copy(f32[8,24,24,256]{3,2,1,0:T(8,128)} %fusion.16) | data formatting | bytes 9437184 | tf_op jit(solution)/shard_map/scatter-add | solution.py:732
  308.8 4.2 %collective-permute-done.14 = f32[8,24,256]{2,0,1:T(8,128)S(1)} collective-permute-done((f32[8,24,256]{2,0,1:T(8,128)S(1)}, f32[8,24,256]{2,0,1:T(8,128)S(1)}, u32[]{:S(2)}, u32[]{:S(2)}) %collective-permute-start.14) | collective-permute-done | bytes 196640 | tf_op jit(solution)/shard_map/ppermute | solution.py:735
  313.7 2.7 collective-permute-done.15
  316.4 1.7 fusion.1
  319.0 1.7 scatter-add.149
  320.7 6.8 %fusion.35 = f32[8,24,24,256]{3,0,2,1:T(8,128)S(1)} fusion(f32[8,24,24,256]{3,0,2,1:T(8,128)} %scatter-add.149, f32[8,24,24,256]{3,2,1,0:T(8,128)} %param.79), kind=kLoop, calls=%fused_computation.224 | loop fusion | flops 2359296 | bytes 14155776 | tf_op jit(solution)/shard_map/add | solution.py:754
  327.5 3.6 %copy.108 = f32[8,24,24,256]{3,2,1,0:T(8,128)} copy(f32[8,24,24,256]{3,0,2,1:T(8,128)S(1)} %fusion.35) | data formatting | bytes 9437184 | tf_op jit(solution)/shard_map/add | solution.py:754
  (176 shorter events, 63.5 us)
Async XLA Ops:
  0.0 14.3 %copy-start.2 = (f32[24]{0:T(128)S(1)}, f32[24]{0:T(128)}, u32[]{:S(2)}) copy-start(f32[24]{0:T(128)} %constant.753) | copy-start | bytes 292
  3.2 10.0 %collective-permute-start.1 = (f32[9,24,256]{2,1,0:T(8,128)S(1)}, f32[9,24,256]{2,1,0:T(8,128)S(1)}, u32[]{:S(2)}, u32[]{:S(2)}) collective-permute-start(f32[9,24,256]{2,1,0:T(8,128)S(1)} %pad_maximum_fusion), channel_id=1, source_target_pairs={{1,0},{2,1},{3,2},{4,3},{5,4},{6,5},{7,6},{0,7},{9,8},{10,9},{11,1... | collective-permute-start | bytes 663560 | tf_op jit(solution)/shard_map/ppermute | solution.py:676
  6.7 6.5 %collective-permute-start = (f32[8,24,256]{2,0,1:T(8,128)S(1)}, f32[8,24,256]{2,0,1:T(8,128)S(1)}, u32[]{:S(2)}, u32[]{:S(2)}) collective-permute-start(f32[8,24,256]{2,0,1:T(8,128)S(1)} %bitcast.373), channel_id=1, source_target_pairs={{0,1},{1,2},{2,3},{3,4},{4,5},{5,6},{6,7},{7,0},{8,9},{9,10},{10,1... | collective-permute-start | bytes 589832 | tf_op jit(solution)/shard_map/ppermute | solution.py:675
  13.2 10.4 %copy-start = (f32[9,24,256]{2,1,0:T(8,128)}, f32[9,24,256]{2,1,0:T(8,128)S(1)}, u32[]{:S(2)}) copy-start(f32[9,24,256]{2,1,0:T(8,128)S(1)} %collective-permute-done.1.phhi) | copy-start | bytes 663556
  14.9 6.2 %collective-permute-start.2 = (f32[10,24,256]{2,1,0:T(8,128)S(1)}, f32[10,24,256]{2,1,0:T(8,128)S(1)}, u32[]{:S(2)}, u32[]{:S(2)}) collective-permute-start(f32[10,24,256]{2,1,0:T(8,128)S(1)} %broadcast_select_fusion.19), channel_id=1, source_target_pairs={{0,8},{4,0},{1,9},{5,1},{2,10},{6,2},{3,11},{7,3},{8,16},{12,4},{9... | collective-permute-start | bytes 737288 | tf_op jit(solution)/shard_map/ppermute | solution.py:662
  16.5 6.2 %collective-permute-start.3 = (f32[10,24,256]{2,1,0:T(8,128)S(1)}, f32[10,24,256]{2,1,0:T(8,128)S(1)}, u32[]{:S(2)}, u32[]{:S(2)}) collective-permute-start(f32[10,24,256]{2,1,0:T(8,128)S(1)} %broadcast_select_fusion.18), channel_id=1, source_target_pairs={{8,0},{0,4},{9,1},{1,5},{10,2},{2,6},{11,3},{3,7},{16,8},{4,12},{1... | collective-permute-start | bytes 737288 | tf_op jit(solution)/shard_map/ppermute | solution.py:663
  23.5 37.7 %copy-start.4 = (f32[9]{0:T(128)S(1)}, f32[9]{0:T(128)}, u32[]{:S(2)}) copy-start(f32[9]{0:T(128)} %constant.749.clone) | copy-start | bytes 112
  61.2 6.0 %collective-permute-start.4 = (f32[8,24,256]{2,0,1:T(8,128)S(1)}, f32[8,24,256]{2,0,1:T(8,128)S(1)}, u32[]{:S(2)}, u32[]{:S(2)}) collective-permute-start(f32[8,24,256]{2,0,1:T(8,128)S(1)} %bitcast.374), channel_id=1, source_target_pairs={{0,1},{1,2},{2,3},{3,4},{4,5},{5,6},{6,7},{7,0},{8,9},{9,10},{10,1... | collective-permute-start | bytes 589832 | tf_op jit(solution)/shard_map/ppermute | solution.py:675
  62.5 6.1 %collective-permute-start.5 = (f32[9,24,256]{2,1,0:T(8,128)S(1)}, f32[9,24,256]{2,1,0:T(8,128)S(1)}, u32[]{:S(2)}, u32[]{:S(2)}) collective-permute-start(f32[9,24,256]{2,1,0:T(8,128)S(1)} %pad_maximum_fusion.1), channel_id=1, source_target_pairs={{1,0},{2,1},{3,2},{4,3},{5,4},{6,5},{7,6},{0,7},{9,8},{10,9},{11,1... | collective-permute-start | bytes 663560 | tf_op jit(solution)/shard_map/ppermute | solution.py:676
  68.6 8.4 %copy-start.1 = (f32[9,24,256]{2,1,0:T(8,128)}, f32[9,24,256]{2,1,0:T(8,128)S(1)}, u32[]{:S(2)}) copy-start(f32[9,24,256]{2,1,0:T(8,128)S(1)} %collective-permute-done.5.phhi) | copy-start | bytes 663556
  69.6 11.8 %collective-permute-start.6 = (f32[10,24,256]{2,1,0:T(8,128)S(1)}, f32[10,24,256]{2,1,0:T(8,128)S(1)}, u32[]{:S(2)}, u32[]{:S(2)}) collective-permute-start(f32[10,24,256]{2,1,0:T(8,128)S(1)} %broadcast_select_fusion.15), channel_id=1, source_target_pairs={{0,8},{4,0},{1,9},{5,1},{2,10},{6,2},{3,11},{7,3},{8,16},{12,4},{9... | collective-permute-start | bytes 737288 | tf_op jit(solution)/shard_map/ppermute | solution.py:662
  71.2 10.2 %collective-permute-start.7 = (f32[10,24,256]{2,1,0:T(8,128)S(1)}, f32[10,24,256]{2,1,0:T(8,128)S(1)}, u32[]{:S(2)}, u32[]{:S(2)}) collective-permute-start(f32[10,24,256]{2,1,0:T(8,128)S(1)} %broadcast_select_fusion.14), channel_id=1, source_target_pairs={{8,0},{0,4},{9,1},{1,5},{10,2},{2,6},{11,3},{3,7},{16,8},{4,12},{1... | collective-permute-start | bytes 737288 | tf_op jit(solution)/shard_map/ppermute | solution.py:663
  82.2 69.1 %copy-start.3 = (f32[6]{0:T(128)S(1)}, f32[6]{0:T(128)}, u32[]{:S(2)}) copy-start(f32[6]{0:T(128)} %constant.751.clone) | copy-start | bytes 76
  160.4 9.2 %collective-permute-start.8 = (f32[10,24,256]{2,1,0:T(8,128)S(1)}, f32[10,24,256]{2,1,0:T(8,128)S(1)}, u32[]{:S(2)}, u32[]{:S(2)}) collective-permute-start(f32[10,24,256]{2,1,0:T(8,128)S(1)} %get-tuple-element.402), channel_id=1, source_target_pairs={{0,8},{4,0},{1,9},{5,1},{2,10},{6,2},{3,11},{7,3},{8,16},{12,4},{9... | collective-permute-start | bytes 737288 | tf_op jit(solution)/shard_map/ppermute | solution.py:662
  162.2 8.6 %collective-permute-start.9 = (f32[10,24,256]{2,1,0:T(8,128)S(1)}, f32[10,24,256]{2,1,0:T(8,128)S(1)}, u32[]{:S(2)}, u32[]{:S(2)}) collective-permute-start(f32[10,24,256]{2,1,0:T(8,128)S(1)} %get-tuple-element.401), channel_id=1, source_target_pairs={{8,0},{0,4},{9,1},{1,5},{10,2},{2,6},{11,3},{3,7},{16,8},{4,12},{1... | collective-permute-start | bytes 737288 | tf_op jit(solution)/shard_map/ppermute | solution.py:663
  171.1 15.7 %collective-permute-start.10 = (f32[8,24,256]{2,0,1:T(8,128)S(1)}, f32[8,24,256]{2,0,1:T(8,128)S(1)}, u32[]{:S(2)}, u32[]{:S(2)}) collective-permute-start(f32[8,24,256]{2,0,1:T(8,128)S(1)} %scatter-add.111), channel_id=1, source_target_pairs={{1,0},{2,1},{3,2},{4,3},{5,4},{6,5},{7,6},{0,7},{9,8},{10,9},{11,1... | collective-permute-start | bytes 589832 | tf_op jit(solution)/shard_map/ppermute | solution.py:735
  186.8 8.2 %collective-permute-start.11 = (f32[9,24,256]{2,0,1:T(8,128)S(1)}, f32[9,24,256]{2,0,1:T(8,128)S(1)}, u32[]{:S(2)}, u32[]{:S(2)}) collective-permute-start(f32[9,24,256]{2,0,1:T(8,128)S(1)} %scatter-add.120), channel_id=1, source_target_pairs={{0,1},{1,2},{2,3},{3,4},{4,5},{5,6},{6,7},{7,0},{8,9},{9,10},{10,1... | collective-permute-start | bytes 663560 | tf_op jit(solution)/shard_map/ppermute | solution.py:736
  284.7 6.2 %collective-permute-start.12 = (f32[10,24,256]{2,1,0:T(8,128)S(1)}, f32[10,24,256]{2,1,0:T(8,128)S(1)}, u32[]{:S(2)}, u32[]{:S(2)}) collective-permute-start(f32[10,24,256]{2,1,0:T(8,128)S(1)} %get-tuple-element.400), channel_id=1, source_target_pairs={{0,8},{4,0},{1,9},{5,1},{2,10},{6,2},{3,11},{7,3},{8,16},{12,4},{9... | collective-permute-start | bytes 737288 | tf_op jit(solution)/shard_map/ppermute | solution.py:662
  286.6 6.2 %collective-permute-start.13 = (f32[10,24,256]{2,1,0:T(8,128)S(1)}, f32[10,24,256]{2,1,0:T(8,128)S(1)}, u32[]{:S(2)}, u32[]{:S(2)}) collective-permute-start(f32[10,24,256]{2,1,0:T(8,128)S(1)} %get-tuple-element.399), channel_id=1, source_target_pairs={{8,0},{0,4},{9,1},{1,5},{10,2},{2,6},{11,3},{3,7},{16,8},{4,12},{1... | collective-permute-start | bytes 737288 | tf_op jit(solution)/shard_map/ppermute | solution.py:663
  307.9 5.0 %collective-permute-start.14 = (f32[8,24,256]{2,0,1:T(8,128)S(1)}, f32[8,24,256]{2,0,1:T(8,128)S(1)}, u32[]{:S(2)}, u32[]{:S(2)}) collective-permute-start(f32[8,24,256]{2,0,1:T(8,128)S(1)} %scatter-add.136), channel_id=1, source_target_pairs={{1,0},{2,1},{3,2},{4,3},{5,4},{6,5},{7,6},{0,7},{9,8},{10,9},{11,1... | collective-permute-start | bytes 589832 | tf_op jit(solution)/shard_map/ppermute | solution.py:735
  308.0 8.4 %collective-permute-start.15 = (f32[9,24,256]{2,0,1:T(8,128)S(1)}, f32[9,24,256]{2,0,1:T(8,128)S(1)}, u32[]{:S(2)}, u32[]{:S(2)}) collective-permute-start(f32[9,24,256]{2,0,1:T(8,128)S(1)} %scatter-add.145), channel_id=1, source_target_pairs={{0,1},{1,2},{2,3},{3,4},{4,5},{5,6},{6,7},{7,0},{8,9},{9,10},{10,1... | collective-permute-start | bytes 663560 | tf_op jit(solution)/shard_map/ppermute | solution.py:736

commit v2 on v1

v2 whole, which is shorter than its diff:
```python
import functools
import math

import jax
import jax.numpy as jnp
import numpy as np
from jax import lax
from jax.experimental import pallas as pl
from jax.experimental.pallas import tpu as pltpu
from jax.sharding import PartitionSpec as P

GAMMA = 5.0 / 3.0
R_INNER = 1.0
R_OUTER = 3.0
COURANT = 0.4
SPEED_BOUND = 5.0
PRESSURE_SOFT = 0.05
THETA_CUT = 0.1

G1 = GAMMA - 1.0
LANES = 128
PAD = 32
FACE_SLOTS, PULL_SLOTS = 16, 16
FLIPS = (1.0, 1.0, -1.0, -1.0, 1.0, 1.0, -1.0, -1.0)
SH, SL, AZ, COT, AK, KEEP, N_ROW = 0, 1, 2, 3, 4, 5, 6
BOTTOM, TOP_END, NEAR = 0, 1, 2
INV_V, R_HI2, K_V, INV_MID, INV_LO, LO, HI, INV_SHELL, HALF_HI2, HALF_KV, HALF_LO2, TOP, OPEN = range(13)


class Grid:
    def __init__(self, rows, cols, rads, total_rows, total_cols):
        self.rows, self.cols, self.rads = rows, cols, rads
        self.width = cols + 8
        self.tiles = self.width // 8
        self.slots = PAD + (rows + 4) * self.width + PAD
        self.dth = (math.pi - 2.0 * THETA_CUT) / total_rows
        self.dph = 2.0 * math.pi / total_cols
        self.dr = (R_OUTER - R_INNER) / rads
        self.dt = COURANT * min(self.dr, R_INNER * math.sin(THETA_CUT) * self.dph) / SPEED_BOUND
        self.total_rows = total_rows

    def at(self, j, k):
        return PAD + (j + 2) * self.width + k

    def row_table(self):
        j = np.arange(-2, self.total_rows + 3, dtype=np.float64)
        low = THETA_CUT + j * self.dth
        high, mid = low + self.dth, low + 0.5 * self.dth
        drop = np.cos(low) - np.cos(high)
        keep = np.where((j == 0) | (j == self.total_rows), 0.0, 1.0)
        safe = np.where(np.abs(np.sin(low)) < 1e-6, 1.0, np.sin(low))
        table = np.zeros((len(j), N_ROW))
        table[:, SH] = np.sin(high) / drop
        table[:, SL] = np.sin(low) / drop
        table[:, AZ] = self.dth / (drop * self.dph)
        table[:, COT] = np.cos(mid) / np.sin(mid)
        table[:, AK] = keep / (safe * self.dph)
        table[:, KEEP] = keep
        return table.astype(np.float32)

    @property
    def flags(self):
        return (self.rows + 5) * N_ROW

    def radial_planes(self):
        i = np.arange(self.rads, dtype=np.float64)
        low = R_INNER + i * self.dr
        high, mid = low + self.dr, low + 0.5 * self.dr
        vol = (high**3 - low**3) / 3.0
        shell = 0.5 * (high**2 - low**2)
        top = np.where(i == self.rads - 1, 2.0, 1.0)
        planes = [None] * 13
        planes[INV_V] = 1.0 / vol
        planes[R_HI2] = high**2
        planes[K_V] = shell / vol
        planes[INV_MID] = 1.0 / mid
        planes[INV_LO] = 1.0 / low
        planes[LO] = low
        planes[HI] = high
        planes[INV_SHELL] = 1.0 / shell
        planes[HALF_HI2] = 0.5 * self.dt * high**2
        planes[HALF_KV] = 0.5 * self.dt * shell / vol
        planes[HALF_LO2] = 0.5 * self.dt * low**2
        planes[TOP] = top
        planes[OPEN] = 2.0 - top
        stack = np.stack(planes).astype(np.float32).reshape(13, 2, 1, LANES)
        return np.broadcast_to(stack, (13, 2, 8, LANES)).copy()


def lane_index(x):
    return lax.broadcasted_iota(jnp.int32, x.shape, 2)


def next_r(x, last=None):
    turned = pltpu.roll(x, LANES - 1, 2)
    end = x[1:2] if last is None else last
    return jnp.where(lane_index(x) == LANES - 1, jnp.concatenate([turned[1:2], end], 0), turned)


def prev_r(x, first):
    turned = pltpu.roll(x, 1, 2)
    return jnp.where(lane_index(x) == 0, jnp.concatenate([first, turned[0:1]], 0), turned)


def split(x):
    return jnp.stack([x[:, :LANES], x[:, LANES:]])


def load(ref, field, slot, size=8):
    return ref[field, :, pl.ds(slot, size), :]


def put(ref, field, slot, value):
    ref[field, :, pl.ds(slot, value.shape[1]), :] = value


def loader(size):
    return lambda ref, field, slot: load(ref, field, slot, size)


def planes_of(rc, size):
    return lambda i: jnp.concatenate([rc[i]] * (size // 8), 1)


def put_line(ref, field, slot, line):
    ref[field, 0, pl.ds(slot, 1), :] = line[:, :LANES]
    ref[field, 1, pl.ds(slot, 1), :] = line[:, LANES:]


def get_line(ref, field, slot):
    return jnp.concatenate([ref[field, 0, pl.ds(slot, 1), :], ref[field, 1, pl.ds(slot, 1), :]], 1)


def picker(g, row_ref, ahead, behind):
    near = row_ref[g.flags + NEAR] > 0.5

    def low(*at):
        return jnp.where(near, ahead[at], behind[at])

    def high(*at):
        return jnp.where(near, behind[at], ahead[at])

    return low, high


def row_copies(g, hbm, ref, sem):
    for j in range(g.rows):
        for h in range(2):
            yield pltpu.make_async_copy(
                hbm.at[:, j, :, pl.ds(h * LANES, LANES)], ref.at[:, h, pl.ds(g.at(j, 0), g.cols), :], sem.at[j, h]
            )


def fill_state(g, us, row_ref, own, sem, phlo, phhi, ahead, behind):
    rows, cols = g.rows, g.cols
    low, high = picker(g, row_ref, ahead, behind)
    calm = [jnp.full((2, 8, LANES), 1.0 if c == 0 else 0.0, jnp.float32) for c in range(8)]

    def keep(j):
        return row_ref[(j + 2) * N_ROW + KEEP]

    def ends(j, fetch):
        for c in range(8):
            scale = keep(j) if c == 6 else None
            for which, k in ((0, -1), (1, cols)):
                line = fetch(c, which)
                put_line(us, c, g.at(j, k), line if scale is None else line * scale)
        put_line(us, 7, g.at(j, cols + 1), fetch(7, 2))

    def body_row(j, side):
        for c in range(8):
            for t in range(cols // 8):
                x = split(side(c, slice(t * 8, t * 8 + 8)))
                put(us, c, g.at(j, t * 8), x * keep(j) if c == 6 else x)
            put(us, c, g.at(j, cols), calm[c])

    for c in range(8):
        put(us, c, g.at(-1, -8), calm[c])
    body_row(-1, low)
    ends(-1, lambda c, w: low(9, slice((c, 9 + c, 18)[w], (c, 9 + c, 18)[w] + 1)))

    def step(j, carry):
        for c in range(8):
            put(us, c, g.at(j, cols), calm[c])
        ends(j, lambda c, w: (phlo[c, pl.ds(j, 1), :], phhi[c, pl.ds(j, 1), :], phhi[8, pl.ds(j, 1), :])[w])
        return carry

    lax.fori_loop(0, rows, step, 0)
    body_row(rows, high)
    ends(rows, lambda c, w: high(9, slice((c, 9 + c, 18)[w], (c, 9 + c, 18)[w] + 1)))
    far = keep(rows + 1)
    for t in range(g.tiles):
        x = split(high(8, slice(t * 8, t * 8 + 8))) if t < cols // 8 else calm[1]
        put(us, 6, g.at(rows + 1, t * 8), x * far)
    put_line(us, 6, g.at(rows + 1, -1), high(9, slice(8, 9)) * far)
    put_line(us, 6, g.at(rows + 1, cols), high(9, slice(17, 18)) * far)
    for copy in row_copies(g, own, us, sem):
        copy.wait()
    for t in range(cols // 8):
        put(us, 6, g.at(0, t * 8), load(us, 6, g.at(0, t * 8)) * keep(0))


def cell_values(g, us, p, size):
    load = loader(size)
    rho, m0, m1, m2, energy, u5, u6, u7 = [load(us, c, p) for c in range(8)]
    b0 = 0.5 * (u5 + next_r(u5))
    b1 = 0.5 * (u6 + load(us, 6, p + g.width))
    b2 = 0.5 * (u7 + load(us, 7, p + 1))
    q = 1.0 / rho
    v0, v1, v2 = m0 * q, m1 * q, m2 * q
    square = b0 * b0 + b1 * b1 + b2 * b2
    pressure = G1 * (energy - 0.5 * (m0 * v0 + m1 * v1 + m2 * v2) - 0.5 * square)
    total = pressure + 0.5 * square
    soft = pressure * pressure + PRESSURE_SOFT * PRESSURE_SOFT
    inv_soft = lax.rsqrt(soft)
    c2 = (GAMMA * (soft * inv_soft) + square) * q
    return (m0, m1, m2), (v0, v1, v2), (b0, b1, b2), u5, q, pressure, total, energy + total, inv_soft, c2


def forward_kernel(
    g, row_ref, own, phlo, phhi, ahead, behind, rc, out, last_col, first_col, us, cf, gf, ff, stage, sem, sem_out
):
    for copy in row_copies(g, own, us, sem):
        copy.start()
    fill_state(g, us, row_ref, own, sem, phlo, phhi, ahead, behind)
    w = g.width
    wide = g.cols

    def cells(n, carry):
        p = pl.multiple_of(g.at(-1, -8) + n * wide, 8)
        m, v, b, u5, q, pressure, total, h, inv_soft, c2 = cell_values(g, us, p, wide)
        put(cf, 0, p, m[0] * v[0] - b[0] * b[0] + total)
        put(cf, 1, p, m[0] * v[1] - b[0] * b[1])
        put(cf, 2, p, m[0] * v[2] - b[0] * b[2])
        put(cf, 3, p, m[1] * v[1] - b[1] * b[1] + total)
        put(cf, 4, p, m[1] * v[2] - b[1] * b[2])
        put(cf, 5, p, m[2] * v[2] - b[2] * b[2] + total)
        vb = v[0] * b[0] + v[1] * b[1] + v[2] * b[2]
        for d in range(3):
            put(cf, 6 + d, p, h * v[d] - b[d] * vb)
            put(cf, 9 + d, p, v[d] * v[d] + c2)
        put(cf, 12, p, v[2] * b[1] - v[1] * b[2])
        put(cf, 13, p, v[0] * b[2] - v[2] * b[0])
        put(cf, 14, p, v[1] * b[0] - v[0] * b[1])
        m, v, b = [[x[0:1] for x in y] for y in (m, v, b)]
        bg = u5[0:1]
        gain = (1.0 - 0.5 * GAMMA) * (bg * bg - b[0] * b[0])
        vbg = vb[0:1] + v[0] * (bg - b[0])
        ghost = (
            m[0] * v[0] - bg * bg + total[0:1] + gain,
            m[0] * v[1] - bg * b[1],
            m[0] * v[2] - bg * b[2],
            (h[0:1] + gain) * v[0] - bg * vbg,
            v[0] * b[2] - v[2] * bg,
            v[1] * bg - v[0] * b[1],
        )
        for f, x in enumerate(ghost):
            gf[f, pl.ds(p, wide), :] = x[0]
        return carry

    lax.fori_loop(0, pl.cdiv((g.rows + 2) * g.width + 8, wide), cells, 0)

    index = ((0, 1, 2), (1, 3, 4), (2, 4, 5))

    def face(d, p, shift, size):
        load = loader(size)
        fluxes = [load(us, 1 + d, p)] + [load(cf, index[d][c], p) for c in range(3)] + [load(cf, 6 + d, p)]
        speed = load(cf, 9 + d, p)
        state = [load(us, c, p) for c in range(5)]
        if shift is None:
            other = [next_r(x) for x in fluxes]
            speed2 = next_r(speed)
            state2 = [other[0] if c == 1 else next_r(state[c]) for c in range(5)]
        else:
            r = p + shift
            other = [load(us, 1 + d, r)] + [load(cf, index[d][c], r) for c in range(3)] + [load(cf, 6 + d, r)]
            speed2 = load(cf, 9 + d, r)
            state2 = [load(us, c, r) for c in range(5)]
        total = 0.5 * (speed + speed2)
        half = 0.5 * (total * lax.rsqrt(total))
        return fluxes, [0.5 * (fluxes[c] + other[c]) - half * (state2[c] - state[c]) for c in range(5)]

    def faces(n, carry):
        p = pl.multiple_of(g.at(-1, 0) + n * FACE_SLOTS, 8)
        for d, shift, base in ((1, w, 0), (2, 1, 5)):
            _, flux = face(d, p, shift, FACE_SLOTS)
            for c in range(5):
                put(ff, base + c, p, flux[c])
        return carry

    lax.fori_loop(0, (g.rows + 1) * g.width // FACE_SLOTS, faces, 0)

    size = g.cols
    load = loader(size)
    plane = planes_of(rc, size)

    def leave(j):
        return pltpu.make_async_copy(stage.at[:, j], out.at[:, j], sem_out.at[j])

    def combine(j, carry):
        p = pl.multiple_of(g.at(j, 0), 8)
        row = (j + 2) * N_ROW
        sh, sl, az, cot, ak, keep = [row_ref[row + i] for i in range(N_ROW)]
        cells_here, flux_r = face(0, p, None, size)
        ghost = [load(us, 1, p)[0:1]] + [gf[f, pl.ds(p, size), :][None] for f in range(4)]
        inv_v, kv = plane(INV_V), plane(K_V)
        rates = []
        for c in range(5):
            high = plane(R_HI2) * flux_r[c]
            first = 0.5 * plane(HALF_LO2)[0:1] * (2.0 / g.dt) * (ghost[c] + cells_here[c][0:1])
            low = prev_r(high, first)
            th = sh * load(ff, c, p) - sl * load(ff, c, p - w)
            ph = az * (load(ff, 5 + c, p) - load(ff, 5 + c, p - 1))
            rates.append(-(inv_v * (high - low) + kv * (th + ph)))
        tt = [load(cf, f, p) for f in range(1, 6)]
        mid = plane(INV_MID)
        rates[1] = rates[1] + (tt[2] + tt[4]) * mid
        rates[2] = rates[2] + (cot * tt[4] - tt[0]) * mid
        rates[3] = rates[3] - (tt[1] + cot * tt[3]) * mid
        ep, ept = load(cf, 14, p), load(cf, 14, p + w)
        x0 = load(cf, 14, p - w) + ep
        x1 = ep + ept
        g_here = gf[5, pl.ds(p, size), :][None]
        x0m = prev_r(x0, gf[5, pl.ds(p - w, size), :][None] + g_here)
        x1m = prev_r(x1, g_here + gf[5, pl.ds(p + w, size), :][None])
        z0 = 0.25 * (x0 + x0m)
        zr = 0.25 * (next_r(x0) + x0)
        z1 = 0.25 * (x1 + x1m)
        et = load(cf, 13, p)
        y0 = load(cf, 13, p - 1) + et
        y1 = et + load(cf, 13, p + 1)
        g_here = gf[4, pl.ds(p, size), :][None]
        y0m = prev_r(y0, gf[4, pl.ds(p - 1, size), :][None] + g_here)
        y1m = prev_r(y1, g_here + gf[4, pl.ds(p + 1, size), :][None])
        p0 = 0.25 * (y0 + y0m)
        pr = 0.25 * (next_r(y0) + y0)
        p1 = 0.25 * (y1 + y1m)
        er, era, erb = load(cf, 12, p), load(cf, 12, p - 1), load(cf, 12, p - w)
        r0 = 0.25 * (er + era + erb + load(cf, 12, p - w - 1))
        r1 = 0.25 * (load(cf, 12, p + 1) + er + load(cf, 12, p - w + 1) + erb)
        rt = 0.25 * (load(cf, 12, p + w) + load(cf, 12, p + w - 1) + er + era)
        lo, hi, shell = plane(LO), plane(HI), plane(INV_SHELL)
        rates.append(-plane(INV_LO) * (sh * z1 - sl * z0 - az * (p1 - p0)))
        rates.append(-shell * (g.dr * ak * (r1 - r0) - keep * (hi * zr - lo * z0)))
        rates.append(shell * ((g.dr / g.dth) * (rt - r0) - (hi * pr - lo * p0)))
        for c in range(8):
            new = load(us, c, p) + g.dt * rates[c]
            stage[c, j] = jnp.concatenate([new[0], new[1]], 1)
        leave(j).start()
        for c in range(8):
            last_col[c, pl.ds(j, 1), :] = stage[c, j, g.cols - 1 : g.cols, :]
            first_col[c, pl.ds(j, 1), :] = stage[c, j, 0:1, :]
        first_col[8, pl.ds(j, 1), :] = stage[7, j, 1:2, :]
        return carry

    lax.fori_loop(0, g.rows, combine, 0)

    def settle(j, carry):
        leave(j).wait()
        return carry

    lax.fori_loop(0, g.rows, settle, 0)


def adjoint_kernel(g, received, row_ref, own, phlo, phhi, ahead, behind, cot, *refs):
    if received:
        back_ahead, back_behind, from_right, from_left = refs[:4]
        refs = refs[4:]
    rc, out, gphlo, gphhi, go_ahead, go_behind, us, cs, cf, ef, zf, ft, fp, stage, sem, sem_cot, sem_out = refs
    w, rows, cols = g.width, g.rows, g.cols
    load = loader(8)
    for copy in row_copies(g, own, us, sem):
        copy.start()
    for copy in row_copies(g, cot, cs, sem_cot):
        copy.start()
    zero = jnp.zeros((2, 8, LANES), jnp.float32)
    for j in (-2, -1, rows, rows + 1):
        for c in range(8):
            for t in range(g.tiles):
                put(cs, c, g.at(j, t * 8), zero)
    for c in range(8):
        put(cs, c, g.at(-2, -8), zero)

    def clear(j, carry):
        for c in range(8):
            put(cs, c, g.at(j, cols), zero)
        return carry

    lax.fori_loop(0, rows, clear, 0)
    fill_state(g, us, row_ref, own, sem, phlo, phhi, ahead, behind)
    for copy in row_copies(g, cot, cs, sem_cot):
        copy.wait()
    if received:
        low, high = picker(g, row_ref, back_ahead, back_behind)
        bottom = row_ref[g.flags + BOTTOM]

        def add_line(c, slot, line):
            put_line(cs, c, slot, get_line(cs, c, slot) + line)

        def columns(j, carry):
            for c in range(8):
                add_line(c, g.at(j, 0), from_left[c, pl.ds(j, 1), :])
                add_line(c, g.at(j, cols - 1), from_right[c, pl.ds(j, 1), :])
            add_line(7, g.at(j, 1), from_left[8, pl.ds(j, 1), :])
            return carry

        lax.fori_loop(0, rows, columns, 0)
        for t in range(cols // 8):
            at = slice(t * 8, t * 8 + 8)
            for c in range(8):
                p = g.at(0, t * 8)
                put(cs, c, p, load(cs, c, p) + split(low(c, at)))
                p = g.at(rows - 1, t * 8)
                put(cs, c, p, load(cs, c, p) + split(high(c, at)))
            for j, share in ((1, 1.0 - bottom), (2, bottom)):
                p = g.at(j, t * 8)
                put(cs, 6, p, load(cs, 6, p) + share * split(low(8, at)))

    def cells(n, carry):
        p = pl.multiple_of(g.at(-1, -8) + n * cols, 8)
        m, v, b, u5, q, pressure, total, h, inv_soft, c2 = cell_values(g, us, p, cols)
        for d in range(3):
            put(cf, d, p, v[d])
            put(cf, 3 + d, p, b[d])
            put(cf, 6 + d, p, v[d] * v[d] + c2)
        put(cf, 9, p, h)
        put(cf, 10, p, q)
        put(cf, 11, p, GAMMA * q * (pressure * inv_soft))
        put(cf, 12, p, c2 * q)
        return carry

    lax.fori_loop(0, pl.cdiv((rows + 2) * w + 8, cols), cells, 0)

    for f in range(3):
        put(ef, f, g.at(-1, -8), zero)
    for f in range(2):
        zf[f, pl.ds(g.at(-1, -8), 8), :] = zero[0]

    def edges(n, carry):
        load = loader(w)
        plane = planes_of(rc, w)
        none = jnp.zeros((1, w, LANES), jnp.float32)
        p = pl.multiple_of(g.at(-1, 0) + n * w, 8)
        j = n - 1
        row = (j + 2) * N_ROW
        sl, az, ak, keep = [row_ref[row + i] for i in (SL, AZ, AK, KEEP)]
        sh_below = row_ref[row - N_ROW + SH]
        shell, lo, hi = plane(INV_SHELL), plane(LO), plane(HI)
        c5, c6, c7 = load(cs, 5, p), load(cs, 6, p), load(cs, 7, p)
        rb = ak * (c6 - load(cs, 6, p - 1)) + (1.0 / g.dth) * (load(cs, 7, p - w) - c7)
        put(ef, 0, p, (0.25 * g.dt * g.dr) * shell * rb)
        q6 = keep * c6 * shell
        zb = plane(INV_LO) * (sl * c5 - sh_below * load(cs, 5, p - w)) + prev_r(hi * q6, none) - lo * q6
        q7 = c7 * shell
        hq7 = hi * q7
        pb = plane(INV_LO) * az * (load(cs, 5, p - 1) - c5) + lo * q7 - prev_r(hq7, none)
        zl = 2.0 * hi[1:2] * q6[1:2]
        plast = -2.0 * hq7[1:2]
        put(ef, 1, p, (0.25 * g.dt) * (zb + next_r(zb, zl)))
        put(ef, 2, p, (0.25 * g.dt) * (pb + next_r(pb, plast)))
        zf[0, pl.ds(p, w), :] = (0.25 * g.dt) * zb[0]
        zf[1, pl.ds(p, w), :] = (0.25 * g.dt) * pb[0]
        return carry

    lax.fori_loop(0, rows + 3, edges, 0)

    size = PULL_SLOTS
    load = loader(size)
    plane = planes_of(rc, size)
    none = jnp.zeros((1, size, LANES), jnp.float32)
    groups = w // size
    for f in range(11):
        for t in range(g.tiles):
            put(ft, f, t * 8, zero)
        put(fp, f, 0, zero)

    def face_pull(halves, state, state2, speed, speed2, closed=None):
        total = 0.5 * (speed + speed2)
        inv = lax.rsqrt(total)
        a = total * inv
        if closed is not None:
            a = a * closed
        dot = halves[0] * (state2[0] - state[0])
        for c in range(1, 5):
            dot = dot + halves[c] * (state2[c] - state[c])
        return halves + [a * x for x in halves] + [-0.25 * inv * dot]

    def pull(n, carry):
        p = pl.multiple_of(g.at(-1, -8) + n * size, 8)
        j = n // groups - 1
        slot = pl.multiple_of(lax.rem(n, groups) * size, 8)
        row = (j + 2) * N_ROW
        sh, az, cot = [row_ref[row + i] for i in (SH, AZ, COT)]
        sl_above = row_ref[row + N_ROW + SL]
        state = [load(us, c, p) for c in range(5)]
        cc = [load(cs, c, p) for c in range(5)]
        kd = plane(HALF_KV)
        sides = []
        up = kd * sl_above
        down = kd * sh
        pw = pl.multiple_of(p + jnp.where(n >= (rows + 1) * groups, 0, w), 8)
        high = face_pull(
            [up * load(cs, c, pw) - down * cc[c] for c in range(5)],
            state,
            [load(us, c, pw) for c in range(5)],
            load(cf, 7, p),
            load(cf, 7, pw),
        )
        low = [load(ft, f, slot) for f in range(11)]
        for f in range(11):
            put(ft, f, slot, high[f])
        sides.append((high, low))
        kaz = kd * az
        high_p = face_pull(
            [kaz * (load(cs, c, p + 1) - cc[c]) for c in range(5)],
            state,
            [load(us, c, p + 1) for c in range(5)],
            load(cf, 8, p),
            load(cf, 8, p + 1),
        )
        for f in range(11):
            put(fp, f, 8, high_p[f])
        per_volume = [plane(INV_V) * x for x in cc]
        half_hi = plane(HALF_HI2)
        speed = load(cf, 6, p)
        high_r = face_pull(
            [half_hi * (next_r(x, none) - x) for x in per_volume],
            state,
            [next_r(x) for x in state],
            speed,
            next_r(speed),
            plane(OPEN),
        )
        first = [plane(HALF_LO2)[0:1] * x[0:1] for x in per_volume]
        low_r = [prev_r(high_r[f], first[f] if f < 5 else none) for f in range(11)]
        low_p = [load(fp, f, 7) for f in range(11)]
        for f in range(11):
            fp[f, :, 7:8, :] = fp[f, :, size + 7 : size + 8, :]
        sides.append((high_p, low_p))
        ft_, fp_ = [[hi_[c] + lo_[c] for c in range(5)] for hi_, lo_ in sides]
        fr_ = [plane(TOP) * high_r[c] + low_r[c] for c in range(5)]
        both = [(high_r, low_r)] + sides
        ub = []
        for c in range(5):
            ub.append(
                cc[c]
                + (both[0][0][5 + c] - both[0][1][5 + c])
                + (both[1][0][5 + c] - both[1][1][5 + c])
                + (both[2][0][5 + c] - both[2][1][5 + c])
            )
        sb = [hi_[10] + lo_[10] for hi_, lo_ in both]
        mid = plane(INV_MID) * g.dt
        w1, w2, w3 = cc[1] * mid, cc[2] * mid, cc[3] * mid
        s00, s11 = fr_[1], ft_[2] + w1
        s22 = fp_[3] + w1 + cot * w2
        s01 = fr_[2] + ft_[1] - w2
        s02 = fr_[3] + fp_[1] - w3
        s12 = ft_[3] + fp_[2] - cot * w3
        e0 = load(ef, 0, p) + load(ef, 0, p + 1) + load(ef, 0, p + w) + load(ef, 0, p + w + 1)
        e2 = load(ef, 1, p) + load(ef, 1, p + w)
        e1 = load(ef, 2, p) + load(ef, 2, p + 1)
        v = [load(cf, d, p) for d in range(3)]
        b = [load(cf, 3 + d, p) for d in range(3)]
        h, q = load(cf, 9, p), load(cf, 10, p)
        gg = (fr_[4], ft_[4], fp_[4])
        flow = v[0] * gg[0] + v[1] * gg[1] + v[2] * gg[2]
        beta = b[0] * gg[0] + b[1] * gg[1] + b[2] * gg[2]
        vb = v[0] * b[0] + v[1] * b[1] + v[2] * b[2]
        d00, d11, d22 = s00 + s00, s11 + s11, s22 + s22
        sv = (
            d00 * v[0] + s01 * v[1] + s02 * v[2],
            s01 * v[0] + d11 * v[1] + s12 * v[2],
            s02 * v[0] + s12 * v[1] + d22 * v[2],
        )
        sbm = (
            d00 * b[0] + s01 * b[1] + s02 * b[2],
            s01 * b[0] + d11 * b[1] + s12 * b[2],
            s02 * b[0] + s12 * b[1] + d22 * b[2],
        )
        c2b = sb[0] + sb[1] + sb[2]
        ptb = s00 + s11 + s22 + flow
        pb = c2b * load(cf, 11, p) + ptb
        pg = G1 * pb
        bbb = 2.0 * (c2b * q) + ptb - pg
        bxe = (b[1] * e2 - b[2] * e1, b[2] * e0 - b[0] * e2, b[0] * e1 - b[1] * e0)
        exv = (e1 * v[2] - e2 * v[1], e2 * v[0] - e0 * v[2], e0 * v[1] - e1 * v[0])
        rho_bar = ub[0] - c2b * load(cf, 12, p)
        m_bar, b_bar = [], []
        for d in range(3):
            vbar = h * gg[d] - beta * b[d] + 2.0 * (v[d] * sb[d]) - bxe[d]
            turn = q * vbar - pg * v[d]
            f0 = (fr_[0], ft_[0], fp_[0])[d]
            m_bar.append(ub[1 + d] + f0 + sv[d] + turn)
            rho_bar = rho_bar - v[d] * (0.5 * sv[d] + turn + 0.5 * (pg * v[d]))
            b_bar.append(b[d] * bbb - sbm[d] - vb * gg[d] - beta * v[d] - exv[d])
        e_bar = ub[4] + flow + pg

        first_lane = lax.broadcasted_iota(jnp.int32, (1, size, LANES), 2) == 0
        v, b = [[x[0:1] for x in y] for y in (v, b)]
        q, h = q[0:1], h[0:1]
        bg = load(us, 5, p)[0:1]
        h = h + (1.0 - 0.5 * GAMMA) * (bg * bg - b[0] * b[0])
        vbg = vb[0:1] + v[0] * (bg - b[0])
        s00, s01, s02, g0 = first[1], first[2], first[3], first[4]
        e2 = (zf[0, pl.ds(p, size), :] + zf[0, pl.ds(p + w, size), :])[None]
        e1 = (zf[1, pl.ds(p, size), :] + zf[1, pl.ds(p + 1, size), :])[None]
        flow = v[0] * g0
        beta = bg * g0
        pb = s00 + flow
        pg = G1 * pb
        bbb = pb - pg
        d00 = s00 + s00
        sv = (d00 * v[0] + s01 * v[1] + s02 * v[2], s01 * v[0], s02 * v[0])
        sbm = (d00 * bg + s01 * b[1] + s02 * b[2], s01 * bg, s02 * bg)
        vbar = (
            h * g0 - beta * bg - (b[1] * e2 - b[2] * e1),
            bg * e2 - beta * b[1],
            -(beta * b[2]) - bg * e1,
        )
        exv = (e1 * v[2] - e2 * v[1], e2 * v[0], -(e1 * v[0]))
        more = [None] * 8
        rho_more = none
        for d in range(3):
            turn = q * vbar[d] - pg * v[d]
            more[1 + d] = sv[d] + turn + (first[0] if d == 0 else 0.0)
            rho_more = rho_more - v[d] * (0.5 * sv[d] + turn + 0.5 * (pg * v[d]))
            bd = bg if d == 0 else b[d]
            more[5 + d] = bd * bbb - sbm[d] - beta * v[d] - exv[d]
        more[5] = more[5] - vbg * g0
        more[0] = rho_more
        more[4] = flow + pg

        def with_first(x, extra):
            return x + jnp.concatenate([jnp.where(first_lane, extra, 0.0), none], 0)

        put(us, 0, p, with_first(rho_bar, more[0]))
        for d in range(3):
            put(us, 1 + d, p, with_first(m_bar[d], more[1 + d]))
        put(us, 4, p, with_first(e_bar, more[4]))
        put(us, 5, p, load(cs, 5, p) + 0.5 * (plane(TOP) * b_bar[0] + prev_r(b_bar[0], 2.0 * more[5])))
        put(us, 6, p, with_first(b_bar[1], more[6]))
        put(us, 7, p, with_first(b_bar[2], more[7]))
        return carry

    lax.fori_loop(0, (rows + 2) * groups + 1, pull, 0)
    load = loader(8)

    def keep_of(j):
        return 0.5 * row_ref[(j + 2) * N_ROW + KEEP]

    def tile6(j, p):
        return keep_of(j) * (load(us, 6, p) + load(us, 6, p - w))

    def tile7(p):
        return 0.5 * (load(us, 7, p) + load(us, 7, p - 1))

    def join(x):
        return jnp.concatenate([x[0], x[1]], 1)

    def line_of(c, j, k):
        p = g.at(j, k)
        if c < 6:
            return get_line(us, c, p)
        if c == 6:
            here = get_line(us, 6, p)
            if isinstance(j, int) and j == -1:
                return keep_of(j) * here
            return keep_of(j) * (here + get_line(us, 6, p - w))
        here = get_line(us, 7, p)
        return 0.5 * here if k == -1 else 0.5 * (here + get_line(us, 7, p - 1))

    def leave(j):
        return pltpu.make_async_copy(stage.at[:, j], out.at[:, j], sem_out.at[j])

    def give(j, carry):
        for t in range(cols // 8):
            p = g.at(j, t * 8)
            at = (j, slice(t * 8, t * 8 + 8))
            for c in range(6):
                stage[(c,) + at] = join(load(us, c, p))
            stage[(6,) + at] = join(load(cs, 6, p) + tile6(j, p))
            stage[(7,) + at] = join(load(cs, 7, p) + tile7(p))
        leave(j).start()
        for c in range(8):
            gphlo[c, pl.ds(j, 1), :] = line_of(c, j, -1)
            gphhi[c, pl.ds(j, 1), :] = line_of(c, j, cols)
        gphhi[8, pl.ds(j, 1), :] = 0.5 * get_line(us, 7, g.at(j, cols))
        return carry

    lax.fori_loop(0, rows, give, 0)

    bottom, top = row_ref[g.flags + BOTTOM], row_ref[g.flags + TOP_END]
    near = row_ref[g.flags + NEAR] > 0.5

    def toward_low(of):
        signs = [1.0 if f > 0 else 1.0 - 2.0 * bottom for f in FLIPS]
        face = of(6)
        return [of(c) * signs[c] for c in range(6)] + [face * (1.0 - bottom), of(7) * signs[7], face * -bottom]

    def toward_high(of, far):
        signs = [1.0 if f > 0 else 1.0 - 2.0 * top for f in FLIPS]
        face = of(6) * (1.0 - top) - far * top
        return [of(c) * signs[c] for c in range(6)] + [face, of(7) * signs[7], far * (1.0 - top)]

    def send(at, low_value, high_value):
        go_ahead[at] = jnp.where(near, high_value, low_value)
        go_behind[at] = jnp.where(near, low_value, high_value)

    for t in range(cols // 8):
        p0, p1 = g.at(-1, t * 8), g.at(rows, t * 8)

        def tile_low(c):
            if c == 6:
                return join(keep_of(-1) * load(us, 6, p0))
            return join(load(us, c, p0) if c < 6 else tile7(p0))

        def tile_high(c):
            return join(load(us, c, p1) if c < 6 else tile6(rows, p1) if c == 6 else tile7(p1))

        lows = toward_low(tile_low)
        highs = toward_high(tile_high, join(keep_of(rows + 1) * load(us, 6, p1)))
        for c in range(9):
            send((c, slice(t * 8, t * 8 + 8)), lows[c], highs[c])
    for k, base in ((-1, 0), (cols, 9)):
        lows = toward_low(lambda c: line_of(c, -1, k))
        highs = toward_high(lambda c: line_of(c, rows, k), keep_of(rows + 1) * get_line(us, 6, g.at(rows, k)))
        for c in range(9):
            send((9, slice(base + c, base + c + 1)), lows[c], highs[c])
    send(
        (9, slice(18, 19)),
        (0.5 - bottom) * get_line(us, 7, g.at(-1, cols)),
        (0.5 - top) * get_line(us, 7, g.at(rows, cols)),
    )

    def settle(j, carry):
        leave(j).wait()
        return carry

    lax.fori_loop(0, rows, settle, 0)


def pack_kernel(g, row_ref, state, phlo, phhi, go_ahead, go_behind, edge, sem):
    rows, cols = g.rows, g.cols
    copies = [
        pltpu.make_async_copy(state.at[:, pl.ds(j0, n)], edge.at[:, pl.ds(e0, n)], sem.at[i])
        for i, (j0, n, e0) in enumerate(((0, 3, 0), (rows - 1, 1, 3)))
    ]
    for copy in copies:
        copy.start()
    bottom, top = row_ref[g.flags + BOTTOM], row_ref[g.flags + TOP_END]
    near = row_ref[g.flags + NEAR] > 0.5

    def nine(of, low):
        pole = bottom if low else top
        signs = [1.0 if f > 0 else 1.0 - 2.0 * pole for f in FLIPS]
        j = 0 if low else rows - 1
        values = [of(c, j) * signs[c] for c in range(8)]
        if low:
            values[6] = of(6, 0) * (1.0 - bottom) - of(6, 2) * bottom
            return values + [of(6, 1)]
        return values + [-of(6, rows - 1)]

    def send(at, low_value, high_value):
        go_ahead[at] = jnp.where(near, high_value, low_value)
        go_behind[at] = jnp.where(near, low_value, high_value)

    for ref, base in ((phlo, 0), (phhi, 9)):
        of = lambda c, j: ref[c, j : j + 1, :]
        for c, (x, y) in enumerate(zip(nine(of, True), nine(of, False))):
            send((9, slice(base + c, base + c + 1)), x, y)
    send(
        (9, slice(18, 19)),
        (1.0 - 2.0 * bottom) * phhi[8, 0:1, :],
        (1.0 - 2.0 * top) * phhi[8, rows - 1 : rows, :],
    )
    for copy in copies:
        copy.wait()
    of = lambda c, j: edge[c, j if j < 3 else 3]
    for c, (x, y) in enumerate(zip(nine(of, True), nine(of, False))):
        send((c,), x, y)


def corner_kernel(g, row_ref, gphlo, gphhi, ahead, behind, to_left, to_right):
    low, high = picker(g, row_ref, ahead, behind)
    bottom = row_ref[g.flags + BOTTOM]
    for ref, got, base in ((to_left, gphlo, 0), (to_right, gphhi, 9)):
        ref[...] = got[...]
        for c in range(8):
            for side, j in ((low, 0), (high, g.rows - 1)):
                ref[c, j : j + 1, :] += side(9, slice(base + c, base + c + 1))
        for j, share in ((1, 1.0 - bottom), (2, bottom)):
            ref[6, j : j + 1, :] += share * low(9, slice(base + 8, base + 9))
    for side, j in ((low, 0), (high, g.rows - 1)):
        to_right[8, j : j + 1, :] += side(9, slice(18, 19))


def finish_kernel(g, block, row_ref, cot, part, ahead, behind, from_right, from_left, out):
    low, high = picker(g, row_ref, ahead, behind)
    bottom = row_ref[g.flags + BOTTOM]
    for c in range(8):
        for j in range(block):
            out[c, j] = 0.5 * (cot[c, j] + part[c, j])

    def columns(j, carry):
        for c in range(8):
            out[c, j, 0:1, :] += 0.5 * from_left[c, pl.ds(j, 1), :]
            out[c, j, g.cols - 1 : g.cols, :] += 0.5 * from_right[c, pl.ds(j, 1), :]
        out[7, j, 1:2, :] += 0.5 * from_left[8, pl.ds(j, 1), :]
        return carry

    lax.fori_loop(0, block, columns, 0)

    @pl.when(pl.program_id(0) == 0)
    def _():
        for c in range(8):
            out[c, 0] += 0.5 * low(c)
        out[6, 1] += (0.5 - 0.5 * bottom) * low(8)
        out[6, 2] += (0.5 * bottom) * low(8)

    @pl.when(pl.program_id(0) == pl.num_programs(0) - 1)
    def _():
        for c in range(8):
            out[c, block - 1] += 0.5 * high(c)


ANY = pl.BlockSpec(memory_space=pl.ANY)
VMEM = pl.BlockSpec(memory_space=pltpu.VMEM)
SMEM = pl.BlockSpec(memory_space=pltpu.SMEM)


def call(kernel, ins, outs, scratch, flops, limit, interpret=False):
    return pl.pallas_call(
        kernel,
        out_shape=[jax.ShapeDtypeStruct(s, jnp.float32) for _, s in outs],
        in_specs=[SMEM] + ins,
        out_specs=[s for s, _ in outs],
        scratch_shapes=scratch,
        compiler_params=pltpu.CompilerParams(vmem_limit_bytes=limit << 20),
        cost_estimate=pl.CostEstimate(flops=flops, bytes_accessed=16 << 20, transcendentals=0),
        interpret=interpret,
    )


def buffers(*shapes):
    return [pltpu.VMEM(s, jnp.float32) for s in shapes]


def forward(g, table, own, halos, planes, interpret=False):
    n = g.slots
    shape = (8, g.rows, g.cols, g.rads)
    scratch = buffers((8, 2, n, LANES), (15, 2, n, LANES), (6, n, LANES), (10, 2, n, LANES), shape)
    scratch += [pltpu.SemaphoreType.DMA((g.rows, 2)), pltpu.SemaphoreType.DMA((g.rows,))]
    outs = [(ANY, shape), (VMEM, (8, g.rows, g.rads)), (VMEM, (9, g.rows, g.rads))]
    run = call(functools.partial(forward_kernel, g), [ANY] + [VMEM] * 5, outs, scratch, 10**8, 58, interpret)
    return run(table, own, *halos, planes)


def adjoint(g, table, own, halos, cot, planes, received=(), interpret=False):
    n = g.slots
    shape = (8, g.rows, g.cols, g.rads)
    message = (10, g.cols, g.rads)
    outs = [(ANY, shape), (VMEM, (8, g.rows, g.rads)), (VMEM, (9, g.rows, g.rads)), (VMEM, message), (VMEM, message)]
    scratch = buffers(
        (8, 2, n, LANES),
        (8, 2, n, LANES),
        (13, 2, n, LANES),
        (3, 2, n, LANES),
        (2, n, LANES),
        (11, 2, g.width, LANES),
        (11, 2, 8 + PULL_SLOTS, LANES),
        shape,
    )
    rows_sem = pltpu.SemaphoreType.DMA((g.rows, 2))
    scratch += [rows_sem, rows_sem, pltpu.SemaphoreType.DMA((g.rows,))]
    ins = [ANY] + [VMEM] * 4 + [ANY] + [VMEM] * (len(received) + 1)
    run = call(functools.partial(adjoint_kernel, g, bool(received)), ins, outs, scratch, 3 * 10**8, 58, interpret)
    return run(table, own, *halos, cot, *received, planes)


def pack(g, table, state, phlo, phhi):
    message = (10, g.cols, g.rads)
    scratch = buffers((8, 4, g.cols, g.rads)) + [pltpu.SemaphoreType.DMA((2,))]
    run = call(functools.partial(pack_kernel, g), [ANY, VMEM, VMEM], [(VMEM, message)] * 2, scratch, 10**6, 16)
    return run(table, state, phlo, phhi)


def corners(g, table, gphlo, gphhi, ahead, behind):
    outs = [(VMEM, gphlo.shape), (VMEM, gphhi.shape)]
    run = call(functools.partial(corner_kernel, g), [VMEM] * 4, outs, [], 10**6, 16)
    return run(table, gphlo, gphhi, ahead, behind)


def finish(g, table, cot, part, ahead, behind, from_right, from_left):
    block = 8
    body = pl.BlockSpec((8, block, g.cols, g.rads), lambda n: (0, n, 0, 0))
    message = pl.BlockSpec((10, g.cols, g.rads), lambda n: (0, 0, 0))
    side = [pl.BlockSpec((m, block, g.rads), lambda n: (0, n, 0)) for m in (8, 9)]
    return pl.pallas_call(
        functools.partial(finish_kernel, g, block),
        grid=(g.rows // block,),
        out_shape=jax.ShapeDtypeStruct(cot.shape, jnp.float32),
        in_specs=[SMEM, body, body, message, message] + side,
        out_specs=body,
        compiler_params=pltpu.CompilerParams(vmem_limit_bytes=32 << 20),
        cost_estimate=pl.CostEstimate(flops=10**6, bytes_accessed=14 << 20, transcendentals=0),
    )(table, cot, part, ahead, behind, from_right, from_left)


class Place:
    def __init__(self):
        self.n_th, self.n_ph = lax.axis_size("th"), lax.axis_size("ph")
        n_th, n_ph = self.n_th, self.n_ph
        half = n_ph // 2
        self.th, self.ph = lax.axis_index("th"), lax.axis_index("ph")
        self.at_bottom, self.at_top = self.th == 0, self.th == n_th - 1
        self.near = self.ph < half
        self.right = [(i, (i + 1) % n_ph) for i in range(n_ph)]
        self.left = [(j, i) for i, j in self.right]
        self.round = []
        for t in range(n_th):
            for p in range(half):
                self.round.append((t * n_ph + p, (t + 1) * n_ph + p if t < n_th - 1 else t * n_ph + p + half))
                self.round.append((t * n_ph + p + half, (t - 1) * n_ph + p + half if t > 0 else p))
        self.back = [(j, i) for i, j in self.round]

    def polar(self, ahead, behind):
        both = ("th", "ph")
        return lax.ppermute(ahead, both, self.round), lax.ppermute(behind, both, self.back)

    def sideways(self, to_right, to_left):
        return lax.ppermute(to_right, "ph", self.right), lax.ppermute(to_left, "ph", self.left)


def shards(state, cotangent):
    place = Place()
    _, rows, cols, rads = state.shape
    g = Grid(rows, cols, rads, rows * place.n_th, cols * place.n_ph)
    flags = jnp.stack([place.at_bottom, place.at_top, place.near]).astype(jnp.float32)
    table = lax.dynamic_slice_in_dim(jnp.asarray(g.row_table()), place.th * rows, rows + 5, 0).reshape(-1)
    table = jnp.concatenate([table, flags])
    planes = jnp.asarray(g.radial_planes())

    def halos_of(value, last, first):
        phlo, phhi = place.sideways(last, first)
        return (phlo, phhi) + tuple(place.polar(*pack(g, table, value, phlo, phhi)))

    def give_back(parts):
        gphlo, gphhi, ahead, behind = parts
        ahead, behind = place.polar(ahead, behind)
        to_left, to_right = corners(g, table, gphlo, gphhi, ahead, behind)
        from_left, from_right = place.sideways(to_right, to_left)
        return ahead, behind, from_right, from_left

    first = jnp.concatenate([state[:, :, 0], state[7:8, :, 1]], 0)
    halos_zero = halos_of(state, state[:, :, cols - 1], first)
    moved, last, first = forward(g, table, state, halos_zero, planes)
    halos_one = halos_of(moved, last, first)
    part, *ghosts = adjoint(g, table, moved, halos_one, cotangent, planes)
    part, *ghosts = adjoint(g, table, state, halos_zero, part, planes, give_back(ghosts))
    return finish(g, table, cotangent, part, *give_back(ghosts))


def solution(mesh):
    placed = (P(None, "th", "ph", None), P(None, "th", "ph", None))
    return jax.shard_map(
        shards, mesh=mesh, in_specs=placed, out_specs=P(None, "th", "ph", None), check_vma=False
    )
```

time: 334 us -> 188 us (0.56)
  Pallas kernels: 169 us -> 103 us
  other arithmetic: 52.8 us -> 0.17 us
  local copies, waits for them, and re-layouts: 62.5 us -> 17.8 us
  waiting for transfers between devices: 30.1 us -> 48 us
    pallas_call x3 -> x8, Pallas kernels: 169 us -> 103 us  [the longest x2 77 us: adjoint(): return run(table, own, *halos, cot, *received, planes)]
    scatter-add x13 -> x0, local copies, waits for them, and re-layouts: 25.5 us -> none  [the longest x2 14.5 us: fold(): cot = cot.at[6, jface].add(share * from_low[8])]
    ppermute x16, waiting for transfers between devices: 30.1 us -> 48 us  [the longest x4 21.7 us: polar(): lax.ppermute(ahead, both, self.round)]
    scatter-add x20 -> x0, other arithmetic: 16.8 us -> none  [the longest x4 6.58 us: fold(): cot = cot.at[:, j].add(got[:8])]
    unnamed x19 -> x53, local copies, waits for them, and re-layouts: 0.2 us -> 13.8 us
    unnamed x14 -> x1, other arithmetic: 11 us -> 0.01 us
    pallas_call x5 -> x0, local copies, waits for them, and re-layouts: 9.16 us -> none  [adjoint(): return run(table, own, *halos, cot, planes)]
    mul x9 -> x0, other arithmetic: 8.82 us -> none  [the longest x1 5.37 us: shards(): half_cot = 0.5 * cotangent]
  transfers between devices with their start and end apart: 16 -> 16, of which waited for: 11 -> 14; matrix products, arithmetic and copies ran while one was open for 12% -> 1% of each run, Pallas kernels for 0% -> 0%
where the time goes in v2:
time: 188 us
  Pallas kernels  103 us (55%)
  waiting for transfers between devices  48 us (26%)
  starting transfers between devices  18 us (10%)
  local copies, waits for them, and re-layouts  17.8 us (9%)
    pallas_call x2, Pallas kernels, adjoint(): return run(table, own, *halos, cot, *received, planes)  77 us
    ppermute x4, waiting for transfers between devices, polar(): lax.ppermute(ahead, both, self.round)  21.7 us
    pallas_call x1, Pallas kernels, forward(): return run(table, own, *halos, planes)  20 us
    unnamed x53, local copies, waits for them, and re-layouts  13.8 us
    ppermute x4, waiting for transfers between devices, sideways(): lax.ppermute(to_right, 'ph', self.right)  9.99 us
    ppermute x4, waiting for transfers between devices, sideways(): lax.ppermute(to_left, 'ph', self.left)  9.93 us
    ppermute x4, starting transfers between devices, sideways(): lax.ppermute(to_left, 'ph', self.left)  8.55 us
    ppermute x4, starting transfers between devices, polar(): lax.ppermute(ahead, both, self.round)  6.92 us
  transfers between devices with their start and end apart: 16, of which 14 were waited for; matrix products, arithmetic and copies ran while one was open for 1% of the time, Pallas kernels for 0%

profile of v2, /device:TPU:0, one launch (start us, length us, event | category | flops | bytes accessed | tf_op | source)
XLA Modules:
  0.0 187.5 jit_solution(6637031843701693148)
XLA Ops:
  0.0 2.2 %fusion = (f32[8,24,1,256]{3,2,1,0:T(1,128)S(1)}, f32[8,24,1,256]{3,2,1,0:T(1,128)S(1)}) fusion(f32[8,24,24,256]{3,2,1,0:T(8,128)} %own.3), kind=kLoop, calls=%fused_computation.7 | loop fusion | bytes 786432 | tf_op jit(solution)/shard_map/slice | solution.py:954
  2.7 0.9 slice.11
  3.7 3.0 %collective-permute-start.1 = (f32[9,24,256]{2,1,0:T(8,128)S(1)}, f32[9,24,256]{2,1,0:T(8,128)S(1)}, u32[]{:S(2)}, u32[]{:S(2)}) collective-permute-start(f32[9,24,256]{2,1,0:T(8,128)S(1)} %pad_maximum_fusion), channel_id=1, source_target_pairs={{1,0},{2,1},{3,2},{4,3},{5,4},{6,5},{7,6},{0,7},{9,8},{10,9},{11,1... | collective-permute-start | bytes 663560 | tf_op jit(solution)/shard_map/ppermute | solution.py:931
  7.7 1.3 collective-permute-done.phlo
  8.9 1.2 collective-permute-done.1.phhi
  10.2 2.3 %copy-done = f32[8,24,24,256]{3,2,1,0:T(8,128)S(1)} copy-done((f32[8,24,24,256]{3,2,1,0:T(8,128)S(1)}, f32[8,24,24,256]{3,2,1,0:T(8,128)}, u32[]{:S(2)}) %copy-start) | copy-done | bytes 4718616
  13.2 2.3 %collective-permute-start.2 = (f32[10,24,256]{2,1,0:T(8,128)S(1)}, f32[10,24,256]{2,1,0:T(8,128)S(1)}, u32[]{:S(2)}, u32[]{:S(2)}) collective-permute-start(f32[10,24,256]{2,1,0:T(8,128)S(1)} %get-tuple-element.26), channel_id=1, source_target_pairs={{0,8},{4,0},{1,9},{5,1},{2,10},{6,2},{3,11},{7,3},{8,16},{12,4},{9... | collective-permute-start | bytes 737288 | tf_op jit(solution)/shard_map/ppermute | solution.py:928
  15.5 6.2 %collective-permute-done.2.ahead = f32[10,24,256]{2,1,0:T(8,128)S(1)} collective-permute-done((f32[10,24,256]{2,1,0:T(8,128)S(1)}, f32[10,24,256]{2,1,0:T(8,128)S(1)}, u32[]{:S(2)}, u32[]{:S(2)}) %collective-permute-start.2) | collective-permute-done | bytes 245792 | tf_op jit(solution)/shard_map/ppermute | solution.py:928
  21.8 2.4 %collective-permute-done.3.behind = f32[10,24,256]{2,1,0:T(8,128)S(1)} collective-permute-done((f32[10,24,256]{2,1,0:T(8,128)S(1)}, f32[10,24,256]{2,1,0:T(8,128)S(1)}, u32[]{:S(2)}, u32[]{:S(2)}) %collective-permute-start.3) | collective-permute-done | bytes 245792 | tf_op jit(solution)/shard_map/ppermute | solution.py:928
  24.9 20.0 %shard_map.47 = (f32[8,24,24,256]{3,2,1,0:T(8,128)}, f32[8,24,256]{2,1,0:T(8,128)}, f32[9,24,256]{2,1,0:T(8,128)}) custom-call(f32[177]{0:T(256)} %copy-done.13, f32[8,24,24,256]{3,2,1,0:T(8,128)} %own.3, f32[8,24,256]{2,1,0:T(8,128)} %copy-done.4, f32[9,24,256]{2,1,0:T(8,128)} %copy-done.3, f32[10,24,256]{2,1,0:T(8,128)} %copy-done.17, ...), custom_call_target="tpu_custom_call" | custom-call | flops 100000000 | bytes 16777216 | tf_op jit(solution)/shard_map/pallas_call | solution.py:855
  45.5 7.5 %collective-permute-done.4.phlo = f32[8,24,256]{2,1,0:T(8,128)S(1)} collective-permute-done((f32[8,24,256]{2,1,0:T(8,128)}, f32[8,24,256]{2,1,0:T(8,128)S(1)}, u32[]{:S(2)}, u32[]{:S(2)}) %collective-permute-start.4) | collective-permute-done | bytes 196640 | tf_op jit(solution)/shard_map/ppermute | solution.py:931
  53.0 2.5 %copy-done.1 = f32[8,24,24,256]{3,2,1,0:T(8,128)S(1)} copy-done((f32[8,24,24,256]{3,2,1,0:T(8,128)S(1)}, f32[8,24,24,256]{3,2,1,0:T(8,128)}, u32[]{:S(2)}) %copy-start.1) | copy-done | bytes 4718616
  56.8 1.6 collective-permute-start.6
  58.9 4.7 %collective-permute-done.6.ahead = f32[10,24,256]{2,1,0:T(8,128)S(1)} collective-permute-done((f32[10,24,256]{2,1,0:T(8,128)S(1)}, f32[10,24,256]{2,1,0:T(8,128)S(1)}, u32[]{:S(2)}, u32[]{:S(2)}) %collective-permute-start.6) | collective-permute-done | bytes 245792 | tf_op jit(solution)/shard_map/ppermute | solution.py:928
  63.6 1.3 collective-permute-done.7.behind
  65.6 38.1 %shard_map.49 = (f32[8,24,24,256]{3,2,1,0:T(8,128)}, f32[8,24,256]{2,1,0:T(8,128)}, f32[9,24,256]{2,1,0:T(8,128)}, f32[10,24,256]{2,1,0:T(8,128)}, f32[10,24,256]{2,1,0:T(8,128)}) custom-call(f32[177]{0:T(256)} %copy-done.13, f32[8,24,24,256]{3,2,1,0:T(8,128)} %get-tuple-element.28.state.own, f32[8,24,256]{2,1,0:T(8,128)} %copy-done.8, ...), custom_call_target="tpu_custom_call" | custom-call | flops 300000000 | bytes 16777216 | tf_op jit(solution)/shard_map/pallas_call | solution.py:877
  103.7 1.6 collective-permute-start.8
  105.8 4.4 %collective-permute-done.8.ahead.refs_0_ = f32[10,24,256]{2,1,0:T(8,128)S(1)} collective-permute-done((f32[10,24,256]{2,1,0:T(8,128)}, f32[10,24,256]{2,1,0:T(8,128)S(1)}, u32[]{:S(2)}, u32[]{:S(2)}) %collective-permute-start.8) | collective-permute-done | bytes 245792 | tf_op jit(solution)/shard_map/ppermute | solution.py:928
  110.2 1.6 collective-permute-done.9.behind.refs_1_
  111.7 1.0 copy-done.10
  114.4 2.6 %collective-permute-start.10 = (f32[8,24,256]{2,1,0:T(8,128)S(1)}, f32[8,24,256]{2,1,0:T(8,128)S(1)}, u32[]{:S(2)}, u32[]{:S(2)}) collective-permute-start(f32[8,24,256]{2,1,0:T(8,128)S(1)} %get-tuple-element.38), channel_id=1, source_target_pairs={{1,0},{2,1},{3,2},{4,3},{5,4},{6,5},{7,6},{0,7},{9,8},{10,9},{11,1... | collective-permute-start | bytes 589832 | tf_op jit(solution)/shard_map/ppermute | solution.py:931
  117.0 5.3 %collective-permute-done.10.refs_2_ = f32[8,24,256]{2,1,0:T(8,128)S(1)} collective-permute-done((f32[8,24,256]{2,1,0:T(8,128)S(1)}, f32[8,24,256]{2,1,0:T(8,128)S(1)}, u32[]{:S(2)}, u32[]{:S(2)}) %collective-permute-start.10) | collective-permute-done | bytes 196640 | tf_op jit(solution)/shard_map/ppermute | solution.py:931
  123.0 38.9 %shard_map.51 = (f32[8,24,24,256]{3,2,1,0:T(8,128)}, f32[8,24,256]{2,1,0:T(8,128)}, f32[9,24,256]{2,1,0:T(8,128)}, f32[10,24,256]{2,1,0:T(8,128)}, f32[10,24,256]{2,1,0:T(8,128)}) custom-call(f32[177]{0:T(256)} %copy-done.13, f32[8,24,24,256]{3,2,1,0:T(8,128)} %own.3, f32[8,24,256]{2,1,0:T(8,128)} %copy-done.4, f32[9,24,256]{2,1,0:T(8,128)} %copy-done.3, ...), custom_call_target="tpu_custom_call" | custom-call | flops 300000000 | bytes 16777216 | tf_op jit(solution)/shard_map/pallas_call | solution.py:877
  162.0 1.3 collective-permute-start.12
  164.1 6.4 %collective-permute-done.12.ahead = f32[10,24,256]{2,1,0:T(8,128)S(1)} collective-permute-done((f32[10,24,256]{2,1,0:T(8,128)}, f32[10,24,256]{2,1,0:T(8,128)S(1)}, u32[]{:S(2)}, u32[]{:S(2)}) %collective-permute-start.12) | collective-permute-done | bytes 245792 | tf_op jit(solution)/shard_map/ppermute | solution.py:928
  170.4 1.1 collective-permute-done.13.behind
  171.6 0.9 copy-done.9
  174.1 2.6 %collective-permute-start.14 = (f32[8,24,256]{2,1,0:T(8,128)S(1)}, f32[8,24,256]{2,1,0:T(8,128)S(1)}, u32[]{:S(2)}, u32[]{:S(2)}) collective-permute-start(f32[8,24,256]{2,1,0:T(8,128)S(1)} %get-tuple-element.45), channel_id=1, source_target_pairs={{1,0},{2,1},{3,2},{4,3},{5,4},{6,5},{7,6},{0,7},{9,8},{10,9},{11,1... | collective-permute-start | bytes 589832 | tf_op jit(solution)/shard_map/ppermute | solution.py:931
  176.7 3.4 %collective-permute-done.14.from_right = f32[8,24,256]{2,1,0:T(8,128)S(1)} collective-permute-done((f32[8,24,256]{2,1,0:T(8,128)S(1)}, f32[8,24,256]{2,1,0:T(8,128)S(1)}, u32[]{:S(2)}, u32[]{:S(2)}) %collective-permute-start.14) | collective-permute-done | bytes 196640 | tf_op jit(solution)/shard_map/ppermute | solution.py:931
  180.1 1.2 collective-permute-done.15.from_left
  181.4 2.3 %copy-done.2 = f32[8,24,24,256]{3,2,1,0:T(8,128)S(1)} copy-done((f32[8,24,24,256]{3,2,1,0:T(8,128)S(1)}, f32[8,24,24,256]{3,2,1,0:T(8,128)}, u32[]{:S(2)}) %copy-start.2) | copy-done | bytes 4718616
  183.7 3.8 %shard_map.53 = f32[8,24,24,256]{3,2,1,0:T(8,128)} custom-call(f32[177]{0:T(256)S(1)} %copy-done.16, f32[8,24,24,256]{3,2,1,0:T(8,128)S(1)} %bitcast.13, f32[8,24,24,256]{3,2,1,0:T(8,128)S(1)} %copy-done.2, f32[10,24,256]{2,1,0:T(8,128)S(1)} %collective-permute-done.12.ahead, f32[10,24,256]{2,1,0:T(8,128)S(1)} %collective-permute-done.13.behind, ...), custom_call_target="tpu_custom_call" | custom-call | flops 1000000 | bytes 14680064 | tf_op jit(solution)/shard_map/pallas_call | solution.py:898
  (69 shorter events, 11.2 us)
Async XLA Ops:
  2.2 6.7 %collective-permute-start = (f32[8,24,256]{2,1,0:T(8,128)S(1)}, f32[8,24,256]{2,1,0:T(8,128)S(1)}, u32[]{:S(2)}, u32[]{:S(2)}) collective-permute-start(f32[8,24,256]{2,1,0:T(8,128)S(1)} %bitcast.15), channel_id=1, source_target_pairs={{0,1},{1,2},{2,3},{3,4},{4,5},{5,6},{6,7},{7,0},{8,9},{9,10},{10,1... | collective-permute-start | bytes 589832 | tf_op jit(solution)/shard_map/ppermute | solution.py:931
  3.7 6.5 %collective-permute-start.1 = (f32[9,24,256]{2,1,0:T(8,128)S(1)}, f32[9,24,256]{2,1,0:T(8,128)S(1)}, u32[]{:S(2)}, u32[]{:S(2)}) collective-permute-start(f32[9,24,256]{2,1,0:T(8,128)S(1)} %pad_maximum_fusion), channel_id=1, source_target_pairs={{1,0},{2,1},{3,2},{4,3},{5,4},{6,5},{7,6},{0,7},{9,8},{10,9},{11,1... | collective-permute-start | bytes 663560 | tf_op jit(solution)/shard_map/ppermute | solution.py:931
  7.7 16.5 %copy-start.13 = (f32[177]{0:T(256)}, f32[177]{0:T(256)S(1)}, u32[]{:S(2)}) copy-start(f32[177]{0:T(256)S(1)} %pad_maximum_fusion.1.row_ref) | copy-start | bytes 2128
  8.9 15.3 %copy-start.4 = (f32[8,24,256]{2,1,0:T(8,128)}, f32[8,24,256]{2,1,0:T(8,128)S(1)}, u32[]{:S(2)}) copy-start(f32[8,24,256]{2,1,0:T(8,128)S(1)} %collective-permute-done.phlo) | copy-start | bytes 589828
  10.2 2.3 %copy-start = (f32[8,24,24,256]{3,2,1,0:T(8,128)S(1)}, f32[8,24,24,256]{3,2,1,0:T(8,128)}, u32[]{:S(2)}) copy-start(f32[8,24,24,256]{3,2,1,0:T(8,128)} %own.3) | copy-start | bytes 14155780
  12.5 11.7 %copy-start.3 = (f32[9,24,256]{2,1,0:T(8,128)}, f32[9,24,256]{2,1,0:T(8,128)S(1)}, u32[]{:S(2)}) copy-start(f32[9,24,256]{2,1,0:T(8,128)S(1)} %collective-permute-done.1.phhi) | copy-start | bytes 663556
  13.2 8.5 %collective-permute-start.2 = (f32[10,24,256]{2,1,0:T(8,128)S(1)}, f32[10,24,256]{2,1,0:T(8,128)S(1)}, u32[]{:S(2)}, u32[]{:S(2)}) collective-permute-start(f32[10,24,256]{2,1,0:T(8,128)S(1)} %get-tuple-element.26), channel_id=1, source_target_pairs={{0,8},{4,0},{1,9},{5,1},{2,10},{6,2},{3,11},{7,3},{8,16},{12,4},{9... | collective-permute-start | bytes 737288 | tf_op jit(solution)/shard_map/ppermute | solution.py:928
  15.5 8.7 %collective-permute-start.3 = (f32[10,24,256]{2,1,0:T(8,128)S(1)}, f32[10,24,256]{2,1,0:T(8,128)S(1)}, u32[]{:S(2)}, u32[]{:S(2)}) collective-permute-start(f32[10,24,256]{2,1,0:T(8,128)S(1)} %get-tuple-element.27), channel_id=1, source_target_pairs={{8,0},{0,4},{9,1},{1,5},{10,2},{2,6},{11,3},{3,7},{16,8},{4,12},{1... | collective-permute-start | bytes 737288 | tf_op jit(solution)/shard_map/ppermute | solution.py:928
  21.8 2.4 %copy-start.17 = (f32[10,24,256]{2,1,0:T(8,128)}, f32[10,24,256]{2,1,0:T(8,128)S(1)}, u32[]{:S(2)}) copy-start(f32[10,24,256]{2,1,0:T(8,128)S(1)} %collective-permute-done.2.ahead) | copy-start | bytes 737284
  44.9 8.1 %collective-permute-start.5 = (f32[9,24,256]{2,1,0:T(8,128)}, f32[9,24,256]{2,1,0:T(8,128)S(1)}, u32[]{:S(2)}, u32[]{:S(2)}) collective-permute-start(f32[9,24,256]{2,1,0:T(8,128)} %get-tuple-element.30), channel_id=1, source_target_pairs={{1,0},{2,1},{3,2},{4,3},{5,4},{6,5},{7,6},{0,7},{9,8},{10,9},{11,1... | collective-permute-start | bytes 663560 | tf_op jit(solution)/shard_map/ppermute | solution.py:931
  45.2 7.7 %collective-permute-start.4 = (f32[8,24,256]{2,1,0:T(8,128)}, f32[8,24,256]{2,1,0:T(8,128)S(1)}, u32[]{:S(2)}, u32[]{:S(2)}) collective-permute-start(f32[8,24,256]{2,1,0:T(8,128)} %get-tuple-element.29), channel_id=1, source_target_pairs={{0,1},{1,2},{2,3},{3,4},{4,5},{5,6},{6,7},{7,0},{8,9},{9,10},{10,1... | collective-permute-start | bytes 589832 | tf_op jit(solution)/shard_map/ppermute | solution.py:931
  53.0 12.0 %copy-start.8 = (f32[8,24,256]{2,1,0:T(8,128)}, f32[8,24,256]{2,1,0:T(8,128)S(1)}, u32[]{:S(2)}) copy-start(f32[8,24,256]{2,1,0:T(8,128)S(1)} %collective-permute-done.4.phlo) | copy-start | bytes 589828
  53.0 12.0 %copy-start.7 = (f32[9,24,256]{2,1,0:T(8,128)}, f32[9,24,256]{2,1,0:T(8,128)S(1)}, u32[]{:S(2)}) copy-start(f32[9,24,256]{2,1,0:T(8,128)S(1)} %collective-permute-done.5.phhi) | copy-start | bytes 663556
  53.0 2.5 %copy-start.1 = (f32[8,24,24,256]{3,2,1,0:T(8,128)S(1)}, f32[8,24,24,256]{3,2,1,0:T(8,128)}, u32[]{:S(2)}) copy-start(f32[8,24,24,256]{3,2,1,0:T(8,128)} %get-tuple-element.28.state.own) | copy-start | bytes 14155780
  56.8 6.8 %collective-permute-start.6 = (f32[10,24,256]{2,1,0:T(8,128)S(1)}, f32[10,24,256]{2,1,0:T(8,128)S(1)}, u32[]{:S(2)}, u32[]{:S(2)}) collective-permute-start(f32[10,24,256]{2,1,0:T(8,128)S(1)} %get-tuple-element.31), channel_id=1, source_target_pairs={{0,8},{4,0},{1,9},{5,1},{2,10},{6,2},{3,11},{7,3},{8,16},{12,4},{9... | collective-permute-start | bytes 737288 | tf_op jit(solution)/shard_map/ppermute | solution.py:928
  58.4 53.3 %copy-start.15 = (f32[177]{0:T(256)S(1)}, f32[177]{0:T(256)}, u32[]{:S(2)}) copy-start(f32[177]{0:T(256)} %copy-done.13) | copy-start | bytes 2128
  58.4 6.5 %collective-permute-start.7 = (f32[10,24,256]{2,1,0:T(8,128)S(1)}, f32[10,24,256]{2,1,0:T(8,128)S(1)}, u32[]{:S(2)}, u32[]{:S(2)}) collective-permute-start(f32[10,24,256]{2,1,0:T(8,128)S(1)} %get-tuple-element.32), channel_id=1, source_target_pairs={{8,0},{0,4},{9,1},{1,5},{10,2},{2,6},{11,3},{3,7},{16,8},{4,12},{1... | collective-permute-start | bytes 737288 | tf_op jit(solution)/shard_map/ppermute | solution.py:928
  63.6 1.3 copy-start.19
  103.7 6.5 %collective-permute-start.8 = (f32[10,24,256]{2,1,0:T(8,128)}, f32[10,24,256]{2,1,0:T(8,128)S(1)}, u32[]{:S(2)}, u32[]{:S(2)}) collective-permute-start(f32[10,24,256]{2,1,0:T(8,128)} %get-tuple-element.34), channel_id=1, source_target_pairs={{0,8},{4,0},{1,9},{5,1},{2,10},{6,2},{3,11},{7,3},{8,16},{12,4},{9... | collective-permute-start | bytes 737288 | tf_op jit(solution)/shard_map/ppermute | solution.py:928
  105.3 6.4 %collective-permute-start.9 = (f32[10,24,256]{2,1,0:T(8,128)}, f32[10,24,256]{2,1,0:T(8,128)S(1)}, u32[]{:S(2)}, u32[]{:S(2)}) collective-permute-start(f32[10,24,256]{2,1,0:T(8,128)} %get-tuple-element.35), channel_id=1, source_target_pairs={{8,0},{0,4},{9,1},{1,5},{10,2},{2,6},{11,3},{3,7},{16,8},{4,12},{1... | collective-permute-start | bytes 737288 | tf_op jit(solution)/shard_map/ppermute | solution.py:928
  110.1 12.2 %copy-start.5 = (f32[10,24,256]{2,1,0:T(8,128)}, f32[10,24,256]{2,1,0:T(8,128)S(1)}, u32[]{:S(2)}) copy-start(f32[10,24,256]{2,1,0:T(8,128)S(1)} %collective-permute-done.8.ahead.refs_0_) | copy-start | bytes 737284
  111.7 10.6 %copy-start.6 = (f32[10,24,256]{2,1,0:T(8,128)}, f32[10,24,256]{2,1,0:T(8,128)S(1)}, u32[]{:S(2)}) copy-start(f32[10,24,256]{2,1,0:T(8,128)S(1)} %collective-permute-done.9.behind.refs_1_) | copy-start | bytes 737284
  113.7 67.7 %slice-start = ((s8[4718592]{0:T(1024)(128)(4,1)}), s8[4194304]{0:T(1024)(128)(4,1)S(1)}, s32[]{:S(2)}) async-start(s8[4718592]{0:T(1024)(128)(4,1)} %bitcast.12), calls=%async_computation | async-start | bytes 8388608
  114.3 8.0 %collective-permute-start.11 = (f32[9,24,256]{2,1,0:T(8,128)S(1)}, f32[9,24,256]{2,1,0:T(8,128)S(1)}, u32[]{:S(2)}, u32[]{:S(2)}) collective-permute-start(f32[9,24,256]{2,1,0:T(8,128)S(1)} %get-tuple-element.39), channel_id=1, source_target_pairs={{0,1},{1,2},{2,3},{3,4},{4,5},{5,6},{6,7},{7,0},{8,9},{9,10},{10,1... | collective-permute-start | bytes 663560 | tf_op jit(solution)/shard_map/ppermute | solution.py:931
  114.4 7.9 %collective-permute-start.10 = (f32[8,24,256]{2,1,0:T(8,128)S(1)}, f32[8,24,256]{2,1,0:T(8,128)S(1)}, u32[]{:S(2)}, u32[]{:S(2)}) collective-permute-start(f32[8,24,256]{2,1,0:T(8,128)S(1)} %get-tuple-element.38), channel_id=1, source_target_pairs={{1,0},{2,1},{3,2},{4,3},{5,4},{6,5},{7,6},{0,7},{9,8},{10,9},{11,1... | collective-permute-start | bytes 589832 | tf_op jit(solution)/shard_map/ppermute | solution.py:931
  123.0 48.5 %copy-start.16 = (f32[177]{0:T(256)S(1)}, f32[177]{0:T(256)}, u32[]{:S(2)}) copy-start(f32[177]{0:T(256)} %copy-done.13) | copy-start | bytes 2128
  123.0 58.3 %slice-start.1 = ((s8[4718592]{0:T(1024)(128)(4,1)}), s8[524288]{0:T(1024)(128)(4,1)S(1)}, s32[]{:S(2)}) async-start(s8[4718592]{0:T(1024)(128)(4,1)} %bitcast.12), calls=%async_computation.1 | async-start | bytes 1048576
  162.0 8.4 %collective-permute-start.12 = (f32[10,24,256]{2,1,0:T(8,128)}, f32[10,24,256]{2,1,0:T(8,128)S(1)}, u32[]{:S(2)}, u32[]{:S(2)}) collective-permute-start(f32[10,24,256]{2,1,0:T(8,128)} %get-tuple-element.41), channel_id=1, source_target_pairs={{0,8},{4,0},{1,9},{5,1},{2,10},{6,2},{3,11},{7,3},{8,16},{12,4},{9... | collective-permute-start | bytes 737288 | tf_op jit(solution)/shard_map/ppermute | solution.py:928
  163.3 8.2 %collective-permute-start.13 = (f32[10,24,256]{2,1,0:T(8,128)}, f32[10,24,256]{2,1,0:T(8,128)S(1)}, u32[]{:S(2)}, u32[]{:S(2)}) collective-permute-start(f32[10,24,256]{2,1,0:T(8,128)} %get-tuple-element.42), channel_id=1, source_target_pairs={{8,0},{0,4},{9,1},{1,5},{10,2},{2,6},{11,3},{3,7},{16,8},{4,12},{1... | collective-permute-start | bytes 737288 | tf_op jit(solution)/shard_map/ppermute | solution.py:928
  174.0 7.3 %collective-permute-start.15 = (f32[9,24,256]{2,1,0:T(8,128)S(1)}, f32[9,24,256]{2,1,0:T(8,128)S(1)}, u32[]{:S(2)}, u32[]{:S(2)}) collective-permute-start(f32[9,24,256]{2,1,0:T(8,128)S(1)} %get-tuple-element.46), channel_id=1, source_target_pairs={{0,1},{1,2},{2,3},{3,4},{4,5},{5,6},{6,7},{7,0},{8,9},{9,10},{10,1... | collective-permute-start | bytes 663560 | tf_op jit(solution)/shard_map/ppermute | solution.py:931
  174.1 6.0 %collective-permute-start.14 = (f32[8,24,256]{2,1,0:T(8,128)S(1)}, f32[8,24,256]{2,1,0:T(8,128)S(1)}, u32[]{:S(2)}, u32[]{:S(2)}) collective-permute-start(f32[8,24,256]{2,1,0:T(8,128)S(1)} %get-tuple-element.45), channel_id=1, source_target_pairs={{1,0},{2,1},{3,2},{4,3},{5,4},{6,5},{7,6},{0,7},{9,8},{10,9},{11,1... | collective-permute-start | bytes 589832 | tf_op jit(solution)/shard_map/ppermute | solution.py:931
  181.4 2.3 %copy-start.2 = (f32[8,24,24,256]{3,2,1,0:T(8,128)S(1)}, f32[8,24,24,256]{3,2,1,0:T(8,128)}, u32[]{:S(2)}) copy-start(f32[8,24,24,256]{3,2,1,0:T(8,128)} %get-tuple-element.40.part) | copy-start | bytes 14155780
  (9 other events, 7.3 us)

commit v3 on v2

--- a/solution.py
+++ b/solution.py
@@ -20,7 +20,7 @@
 G1 = GAMMA - 1.0
 LANES = 128
 PAD = 32
-FACE_SLOTS, PULL_SLOTS = 16, 16
+FACE_SLOTS, PULL_SLOTS = 32, 32
 FLIPS = (1.0, 1.0, -1.0, -1.0, 1.0, 1.0, -1.0, -1.0)
 SH, SL, AZ, COT, AK, KEEP, N_ROW = 0, 1, 2, 3, 4, 5, 6
 BOTTOM, TOP_END, NEAR = 0, 1, 2
@@ -143,17 +143,19 @@
     return low, high
 
 
-def row_copies(g, hbm, ref, sem):
-    for j in range(g.rows):
+def row_copies(g, hbm, ref, sem, row=None):
+    for j in range(g.rows) if row is None else (row,):
         for h in range(2):
             yield pltpu.make_async_copy(
                 hbm.at[:, j, :, pl.ds(h * LANES, LANES)], ref.at[:, h, pl.ds(g.at(j, 0), g.cols), :], sem.at[j, h]
             )
 
 
-def fill_state(g, us, row_ref, own, sem, phlo, phhi, ahead, behind):
+def fill_state(g, us, row_ref, halos):
     rows, cols = g.rows, g.cols
+    phlo, phhi, ahead, behind, corner_ahead, corner_behind = halos
     low, high = picker(g, row_ref, ahead, behind)
+    corner_low, corner_high = picker(g, row_ref, corner_ahead, corner_behind)
     calm = [jnp.full((2, 8, LANES), 1.0 if c == 0 else 0.0, jnp.float32) for c in range(8)]
 
     def keep(j):
@@ -172,32 +174,36 @@
             for t in range(cols // 8):
                 x = split(side(c, slice(t * 8, t * 8 + 8)))
                 put(us, c, g.at(j, t * 8), x * keep(j) if c == 6 else x)
-            put(us, c, g.at(j, cols), calm[c])
-
-    for c in range(8):
-        put(us, c, g.at(-1, -8), calm[c])
+
+    def still(n, carry):
+        for c in range(8):
+            put(us, c, pl.multiple_of(g.at(-2, cols) + n * g.width, 8), calm[c])
+        return carry
+
+    lax.fori_loop(0, rows + 3, still, 0)
     body_row(-1, low)
-    ends(-1, lambda c, w: low(9, slice((c, 9 + c, 18)[w], (c, 9 + c, 18)[w] + 1)))
+    ends(-1, lambda c, w: corner_low(slice((c, 9 + c, 18)[w], (c, 9 + c, 18)[w] + 1)))
 
     def step(j, carry):
-        for c in range(8):
-            put(us, c, g.at(j, cols), calm[c])
         ends(j, lambda c, w: (phlo[c, pl.ds(j, 1), :], phhi[c, pl.ds(j, 1), :], phhi[8, pl.ds(j, 1), :])[w])
         return carry
 
     lax.fori_loop(0, rows, step, 0)
     body_row(rows, high)
-    ends(rows, lambda c, w: high(9, slice((c, 9 + c, 18)[w], (c, 9 + c, 18)[w] + 1)))
+    ends(rows, lambda c, w: corner_high(slice((c, 9 + c, 18)[w], (c, 9 + c, 18)[w] + 1)))
     far = keep(rows + 1)
     for t in range(g.tiles):
         x = split(high(8, slice(t * 8, t * 8 + 8))) if t < cols // 8 else calm[1]
         put(us, 6, g.at(rows + 1, t * 8), x * far)
-    put_line(us, 6, g.at(rows + 1, -1), high(9, slice(8, 9)) * far)
-    put_line(us, 6, g.at(rows + 1, cols), high(9, slice(17, 18)) * far)
-    for copy in row_copies(g, own, us, sem):
+    put_line(us, 6, g.at(rows + 1, -1), corner_high(slice(8, 9)) * far)
+    put_line(us, 6, g.at(rows + 1, cols), corner_high(slice(17, 18)) * far)
+
+def arrive(g, us, row_ref, own, sem, j):
+    for copy in row_copies(g, own, us, sem, j):
         copy.wait()
-    for t in range(cols // 8):
-        put(us, 6, g.at(0, t * 8), load(us, 6, g.at(0, t * 8)) * keep(0))
+    if isinstance(j, int) and j == 0:
+        for t in range(g.cols // 8):
+            put(us, 6, g.at(0, t * 8), load(us, 6, g.at(0, t * 8)) * row_ref[2 * N_ROW + KEEP])
 
 
 def cell_values(g, us, p, size):
@@ -217,17 +223,23 @@
     return (m0, m1, m2), (v0, v1, v2), (b0, b1, b2), u5, q, pressure, total, energy + total, inv_soft, c2
 
 
-def forward_kernel(
-    g, row_ref, own, phlo, phhi, ahead, behind, rc, out, last_col, first_col, us, cf, gf, ff, stage, sem, sem_out
-):
+def forward_kernel(g, row_ref, own, *refs):
+    halos, rc, refs = refs[:6], refs[6], refs[7:]
+    out, last_col, first_col, go_ahead, go_behind, us, cf, gf, ff, stage, sem, sem_out = refs
     for copy in row_copies(g, own, us, sem):
         copy.start()
-    fill_state(g, us, row_ref, own, sem, phlo, phhi, ahead, behind)
+    fill_state(g, us, row_ref, halos)
     w = g.width
-    wide = g.cols
+    wide = w
+    arrive(g, us, row_ref, own, sem, 0)
 
     def cells(n, carry):
         p = pl.multiple_of(g.at(-1, -8) + n * wide, 8)
+
+        @pl.when((n > 0) & (n < g.rows))
+        def _():
+            arrive(g, us, row_ref, own, sem, n)
+
         m, v, b, u5, q, pressure, total, h, inv_soft, c2 = cell_values(g, us, p, wide)
         put(cf, 0, p, m[0] * v[0] - b[0] * b[0] + total)
         put(cf, 1, p, m[0] * v[1] - b[0] * b[1])
@@ -258,7 +270,7 @@
             gf[f, pl.ds(p, wide), :] = x[0]
         return carry
 
-    lax.fori_loop(0, pl.cdiv((g.rows + 2) * g.width + 8, wide), cells, 0)
+    lax.fori_loop(0, g.rows + 3, cells, 0)
 
     index = ((0, 1, 2), (1, 3, 4), (2, 4, 5))
 
@@ -355,6 +367,8 @@
 
     lax.fori_loop(0, g.rows, combine, 0)
 
+    send_rows(g, row_ref, lambda c, j: stage[c, j], go_ahead, go_behind)
+
     def settle(j, carry):
         leave(j).wait()
         return carry
@@ -362,17 +376,25 @@
     lax.fori_loop(0, g.rows, settle, 0)
 
 
-def adjoint_kernel(g, received, row_ref, own, phlo, phhi, ahead, behind, cot, *refs):
+def adjoint_kernel(g, received, row_ref, own, cot, *refs):
+    halos, rc, refs = refs[:6], refs[6], refs[7:]
     if received:
-        back_ahead, back_behind, from_right, from_left = refs[:4]
-        refs = refs[4:]
-    rc, out, gphlo, gphhi, go_ahead, go_behind, us, cs, cf, ef, zf, ft, fp, stage, sem, sem_cot, sem_out = refs
+        base, *got = refs[:7]
+        refs = refs[7:]
+    out, gphlo, gphhi, go_ahead, go_behind, us, cs, cf, ef, zf, ft, fp, stage, sem, sem_cot, sem_out, sem_base = refs
     w, rows, cols = g.width, g.rows, g.cols
     load = loader(8)
     for copy in row_copies(g, own, us, sem):
         copy.start()
     for copy in row_copies(g, cot, cs, sem_cot):
         copy.start()
+
+    def enter(j):
+        return pltpu.make_async_copy(base.at[:, j], stage.at[:, j], sem_base.at[j])
+
+    if received:
+        for j in range(rows):
+            enter(j).start()
     zero = jnp.zeros((2, 8, LANES), jnp.float32)
     for j in (-2, -1, rows, rows + 1):
         for c in range(8):
@@ -387,10 +409,33 @@
         return carry
 
     lax.fori_loop(0, rows, clear, 0)
-    fill_state(g, us, row_ref, own, sem, phlo, phhi, ahead, behind)
+    fill_state(g, us, row_ref, halos)
+    arrive(g, us, row_ref, own, sem, 0)
+
+    def cells(n, carry):
+        p = pl.multiple_of(g.at(-1, -8) + n * w, 8)
+
+        @pl.when((n > 0) & (n < rows))
+        def _():
+            arrive(g, us, row_ref, own, sem, n)
+
+        m, v, b, u5, q, pressure, total, h, inv_soft, c2 = cell_values(g, us, p, w)
+        for d in range(3):
+            put(cf, d, p, v[d])
+            put(cf, 3 + d, p, b[d])
+            put(cf, 6 + d, p, v[d] * v[d] + c2)
+        put(cf, 9, p, h)
+        put(cf, 10, p, q)
+        put(cf, 11, p, GAMMA * q * (pressure * inv_soft))
+        put(cf, 12, p, c2 * q)
+        return carry
+
+    lax.fori_loop(0, rows + 3, cells, 0)
+
     for copy in row_copies(g, cot, cs, sem_cot):
         copy.wait()
     if received:
+        back_ahead, back_behind, from_right, from_left, lines_right, lines_left = got
         low, high = picker(g, row_ref, back_ahead, back_behind)
         bottom = row_ref[g.flags + BOTTOM]
 
@@ -415,21 +460,14 @@
             for j, share in ((1, 1.0 - bottom), (2, bottom)):
                 p = g.at(j, t * 8)
                 put(cs, 6, p, load(cs, 6, p) + share * split(low(8, at)))
-
-    def cells(n, carry):
-        p = pl.multiple_of(g.at(-1, -8) + n * cols, 8)
-        m, v, b, u5, q, pressure, total, h, inv_soft, c2 = cell_values(g, us, p, cols)
-        for d in range(3):
-            put(cf, d, p, v[d])
-            put(cf, 3 + d, p, b[d])
-            put(cf, 6 + d, p, v[d] * v[d] + c2)
-        put(cf, 9, p, h)
-        put(cf, 10, p, q)
-        put(cf, 11, p, GAMMA * q * (pressure * inv_soft))
-        put(cf, 12, p, c2 * q)
-        return carry
-
-    lax.fori_loop(0, pl.cdiv((rows + 2) * w + 8, cols), cells, 0)
+        for j, right0, left0, second in ((0, 0, 0, 9), (rows - 1, 9, 10, 19)):
+            for c in range(8):
+                add_line(c, g.at(j, cols - 1), lines_right[right0 + c : right0 + c + 1, :])
+                add_line(c, g.at(j, 0), lines_left[left0 + c : left0 + c + 1, :])
+            add_line(7, g.at(j, 1), lines_left[second : second + 1, :])
+        for lines, k in ((lines_right, cols - 1), (lines_left, 0)):
+            for j, share in ((1, 1.0 - bottom), (2, bottom)):
+                add_line(6, g.at(j, k), share * lines[8:9, :])
 
     for f in range(3):
         put(ef, f, g.at(-1, -8), zero)
@@ -673,13 +711,19 @@
         return pltpu.make_async_copy(stage.at[:, j], out.at[:, j], sem_out.at[j])
 
     def give(j, carry):
+        if received:
+            enter(j).wait()
         for t in range(cols // 8):
             p = g.at(j, t * 8)
             at = (j, slice(t * 8, t * 8 + 8))
+
+            def leave_tile(c, x):
+                stage[(c,) + at] = 0.5 * (stage[(c,) + at] + x) if received else x
+
             for c in range(6):
-                stage[(c,) + at] = join(load(us, c, p))
-            stage[(6,) + at] = join(load(cs, 6, p) + tile6(j, p))
-            stage[(7,) + at] = join(load(cs, 7, p) + tile7(p))
+                leave_tile(c, join(load(us, c, p)))
+            leave_tile(6, join(load(cs, 6, p) + tile6(j, p)))
+            leave_tile(7, join(load(cs, 7, p) + tile7(p)))
         leave(j).start()
         for c in range(8):
             gphlo[c, pl.ds(j, 1), :] = line_of(c, j, -1)
@@ -739,88 +783,135 @@
     lax.fori_loop(0, rows, settle, 0)
 
 
-def pack_kernel(g, row_ref, state, phlo, phhi, go_ahead, go_behind, edge, sem):
+def polar_nine(g, pole, of, low):
+    signs = [1.0 if f > 0 else 1.0 - 2.0 * pole for f in FLIPS]
+    values = [of(c, 0 if low else g.rows - 1) * signs[c] for c in range(8)]
+    if low:
+        values[6] = of(6, 0) * (1.0 - pole) - of(6, 2) * pole
+        return values + [of(6, 1)]
+    return values + [-of(6, g.rows - 1)]
+
+
+def sender(g, row_ref, go_ahead, go_behind):
+    near = row_ref[g.flags + NEAR] > 0.5
+
+    def send(at, low_value, high_value):
+        go_ahead[at] = jnp.where(near, high_value, low_value)
+        go_behind[at] = jnp.where(near, low_value, high_value)
+
+    return send
+
+
+def send_rows(g, row_ref, of, go_ahead, go_behind):
+    bottom, top = row_ref[g.flags + BOTTOM], row_ref[g.flags + TOP_END]
+    send = sender(g, row_ref, go_ahead, go_behind)
+    for c, (x, y) in enumerate(zip(polar_nine(g, bottom, of, True), polar_nine(g, top, of, False))):
+        send(c, x, y)
+
+
+def pack_kernel(g, row_ref, state, last_col, first_col, go_ahead, go_behind, edge, left, right, sem):
     rows, cols = g.rows, g.cols
     copies = [
-        pltpu.make_async_copy(state.at[:, pl.ds(j0, n)], edge.at[:, pl.ds(e0, n)], sem.at[i])
-        for i, (j0, n, e0) in enumerate(((0, 3, 0), (rows - 1, 1, 3)))
+        pltpu.make_async_copy(state.at[:, pl.ds(0, 3)], edge.at[:, pl.ds(0, 3)], sem.at[0]),
+        pltpu.make_async_copy(state.at[:, pl.ds(rows - 1, 1)], edge.at[:, pl.ds(3, 1)], sem.at[1]),
+        pltpu.make_async_copy(state.at[:, :, pl.ds(0, 8)], left, sem.at[2]),
+        pltpu.make_async_copy(state.at[:, :, pl.ds(cols - 8, 8)], right, sem.at[3]),
     ]
     for copy in copies:
         copy.start()
+    for copy in copies[:2]:
+        copy.wait()
+    send_rows(g, row_ref, lambda c, j: edge[c, j if j < 3 else 3], go_ahead, go_behind)
+    for copy in copies[2:]:
+        copy.wait()
+
+    def line(j, carry):
+        for c in range(8):
+            first_col[c, pl.ds(j, 1), :] = left[c, j, 0:1, :]
+            last_col[c, pl.ds(j, 1), :] = right[c, j, 7:8, :]
+        first_col[8, pl.ds(j, 1), :] = left[7, j, 1:2, :]
+        return carry
+
+    lax.fori_loop(0, rows, line, 0)
+
+
+def pack_corner_kernel(g, row_ref, phlo, phhi, go_ahead, go_behind):
     bottom, top = row_ref[g.flags + BOTTOM], row_ref[g.flags + TOP_END]
-    near = row_ref[g.flags + NEAR] > 0.5
-
-    def nine(of, low):
-        pole = bottom if low else top
-        signs = [1.0 if f > 0 else 1.0 - 2.0 * pole for f in FLIPS]
-        j = 0 if low else rows - 1
-        values = [of(c, j) * signs[c] for c in range(8)]
-        if low:
-            values[6] = of(6, 0) * (1.0 - bottom) - of(6, 2) * bottom
-            return values + [of(6, 1)]
-        return values + [-of(6, rows - 1)]
-
-    def send(at, low_value, high_value):
-        go_ahead[at] = jnp.where(near, high_value, low_value)
-        go_behind[at] = jnp.where(near, low_value, high_value)
-
+    send = sender(g, row_ref, go_ahead, go_behind)
     for ref, base in ((phlo, 0), (phhi, 9)):
         of = lambda c, j: ref[c, j : j + 1, :]
-        for c, (x, y) in enumerate(zip(nine(of, True), nine(of, False))):
-            send((9, slice(base + c, base + c + 1)), x, y)
+        for c, (x, y) in enumerate(zip(polar_nine(g, bottom, of, True), polar_nine(g, top, of, False))):
+            send(slice(base + c, base + c + 1), x, y)
     send(
-        (9, slice(18, 19)),
+        slice(18, 19),
         (1.0 - 2.0 * bottom) * phhi[8, 0:1, :],
-        (1.0 - 2.0 * top) * phhi[8, rows - 1 : rows, :],
+        (1.0 - 2.0 * top) * phhi[8, g.rows - 1 : g.rows, :],
     )
-    for copy in copies:
-        copy.wait()
-    of = lambda c, j: edge[c, j if j < 3 else 3]
-    for c, (x, y) in enumerate(zip(nine(of, True), nine(of, False))):
-        send((c,), x, y)
-
-
-def corner_kernel(g, row_ref, gphlo, gphhi, ahead, behind, to_left, to_right):
+
+
+def turn_kernel(g, row_ref, ahead, behind, to_left, to_right):
+    low, high = picker(g, row_ref, ahead, behind)
+    to_left[0:9, :] = low(9, slice(0, 9))
+    to_left[9:18, :] = high(9, slice(0, 9))
+    to_right[0:10, :] = low(9, slice(9, 19))
+    to_right[10:20, :] = high(9, slice(9, 19))
+
+
+def finish_kernel(
+    g, row_ref, part, ahead, behind, from_right, from_left, lines_right, lines_left, out, edge, left, right, sem
+):
+    rows, cols = g.rows, g.cols
+    inner = pl.ds(3, rows - 4)
+    places = (
+        ((slice(None), pl.ds(0, 3)), edge.at[:, pl.ds(0, 3)]),
+        ((slice(None), pl.ds(rows - 1, 1)), edge.at[:, pl.ds(3, 1)]),
+        ((slice(None), inner, pl.ds(0, 8)), left),
+        ((slice(None), inner, pl.ds(cols - 8, 8)), right),
+    )
+    enter = [pltpu.make_async_copy(part.at[at], ref, sem.at[i]) for i, (at, ref) in enumerate(places)]
+    leave = [pltpu.make_async_copy(ref, out.at[at], sem.at[4 + i]) for i, (at, ref) in enumerate(places)]
+    for copy in enter:
+        copy.start()
     low, high = picker(g, row_ref, ahead, behind)
     bottom = row_ref[g.flags + BOTTOM]
-    for ref, got, base in ((to_left, gphlo, 0), (to_right, gphhi, 9)):
-        ref[...] = got[...]
+    for copy in enter[:2]:
+        copy.wait()
+    for c in range(8):
+        edge[c, 0] += 0.5 * low(c)
+        edge[c, 3] += 0.5 * high(c)
+    for e, share in ((1, 0.5 - 0.5 * bottom), (2, 0.5 * bottom)):
+        edge[6, e] += share * low(8)
+        for lines, k in ((lines_right, cols - 1), (lines_left, 0)):
+            edge[6, e, k : k + 1, :] += share * lines[8:9, :]
+    for e, right0, left0, second in ((0, 0, 0, 9), (3, 9, 10, 19)):
         for c in range(8):
-            for side, j in ((low, 0), (high, g.rows - 1)):
-                ref[c, j : j + 1, :] += side(9, slice(base + c, base + c + 1))
-        for j, share in ((1, 1.0 - bottom), (2, bottom)):
-            ref[6, j : j + 1, :] += share * low(9, slice(base + 8, base + 9))
-    for side, j in ((low, 0), (high, g.rows - 1)):
-        to_right[8, j : j + 1, :] += side(9, slice(18, 19))
-
-
-def finish_kernel(g, block, row_ref, cot, part, ahead, behind, from_right, from_left, out):
-    low, high = picker(g, row_ref, ahead, behind)
-    bottom = row_ref[g.flags + BOTTOM]
-    for c in range(8):
-        for j in range(block):
-            out[c, j] = 0.5 * (cot[c, j] + part[c, j])
-
-    def columns(j, carry):
+            edge[c, e, cols - 1 : cols, :] += 0.5 * lines_right[right0 + c : right0 + c + 1, :]
+            edge[c, e, 0:1, :] += 0.5 * lines_left[left0 + c : left0 + c + 1, :]
+        edge[7, e, 1:2, :] += 0.5 * lines_left[second : second + 1, :]
+
+    def columns(ref0, ref1, e, j):
         for c in range(8):
-            out[c, j, 0:1, :] += 0.5 * from_left[c, pl.ds(j, 1), :]
-            out[c, j, g.cols - 1 : g.cols, :] += 0.5 * from_right[c, pl.ds(j, 1), :]
-        out[7, j, 1:2, :] += 0.5 * from_left[8, pl.ds(j, 1), :]
-        return carry
-
-    lax.fori_loop(0, block, columns, 0)
-
-    @pl.when(pl.program_id(0) == 0)
-    def _():
-        for c in range(8):
-            out[c, 0] += 0.5 * low(c)
-        out[6, 1] += (0.5 - 0.5 * bottom) * low(8)
-        out[6, 2] += (0.5 * bottom) * low(8)
-
-    @pl.when(pl.program_id(0) == pl.num_programs(0) - 1)
-    def _():
-        for c in range(8):
-            out[c, block - 1] += 0.5 * high(c)
+            ref0[c, e, 0:1, :] += 0.5 * from_left[c, pl.ds(j, 1), :]
+            k = ref1.shape[2]
+            ref1[c, e, k - 1 : k, :] += 0.5 * from_right[c, pl.ds(j, 1), :]
+        ref0[7, e, 1:2, :] += 0.5 * from_left[8, pl.ds(j, 1), :]
+
+    for e, j in ((0, 0), (1, 1), (2, 2), (3, rows - 1)):
+        columns(edge, edge, e, j)
+    for copy in leave[:2]:
+        copy.start()
+    for copy in enter[2:]:
+        copy.wait()
+
+    def step(e, carry):
+        columns(left, right, e, e + 3)
+        return carry
+
+    lax.fori_loop(0, rows - 4, step, 0)
+    for copy in leave[2:]:
+        copy.start()
+    for copy in leave:
+        copy.wait()
 
 
 ANY = pl.BlockSpec(memory_space=pl.ANY)
@@ -845,21 +936,31 @@
     return [pltpu.VMEM(s, jnp.float32) for s in shapes]
 
 
+def sizes(g):
+    return (
+        (8, g.rows, g.cols, g.rads),
+        [(8, g.rows, g.rads), (9, g.rows, g.rads)],
+        (9, g.cols, g.rads),
+        (24, g.rads),
+    )
+
+
 def forward(g, table, own, halos, planes, interpret=False):
     n = g.slots
-    shape = (8, g.rows, g.cols, g.rads)
+    shape, sides, body, lines = sizes(g)
     scratch = buffers((8, 2, n, LANES), (15, 2, n, LANES), (6, n, LANES), (10, 2, n, LANES), shape)
-    scratch += [pltpu.SemaphoreType.DMA((g.rows, 2)), pltpu.SemaphoreType.DMA((g.rows,))]
-    outs = [(ANY, shape), (VMEM, (8, g.rows, g.rads)), (VMEM, (9, g.rows, g.rads))]
-    run = call(functools.partial(forward_kernel, g), [ANY] + [VMEM] * 5, outs, scratch, 10**8, 58, interpret)
+    dma = pltpu.SemaphoreType.DMA
+    scratch += [dma((g.rows, 2)), dma((g.rows,))]
+    outs = [(ANY, shape)] + [(VMEM, s) for s in sides + [body, body]]
+    run = call(functools.partial(forward_kernel, g), [ANY] + [VMEM] * 7, outs, scratch, 10**8, 48, interpret)
     return run(table, own, *halos, planes)
 
 
 def adjoint(g, table, own, halos, cot, planes, received=(), interpret=False):
     n = g.slots
-    shape = (8, g.rows, g.cols, g.rads)
+    shape, sides, body, lines = sizes(g)
     message = (10, g.cols, g.rads)
-    outs = [(ANY, shape), (VMEM, (8, g.rows, g.rads)), (VMEM, (9, g.rows, g.rads)), (VMEM, message), (VMEM, message)]
+    outs = [(ANY, shape)] + [(VMEM, s) for s in sides + [message, message]]
     scratch = buffers(
         (8, 2, n, LANES),
         (8, 2, n, LANES),
@@ -870,40 +971,47 @@
         (11, 2, 8 + PULL_SLOTS, LANES),
         shape,
     )
-    rows_sem = pltpu.SemaphoreType.DMA((g.rows, 2))
-    scratch += [rows_sem, rows_sem, pltpu.SemaphoreType.DMA((g.rows,))]
-    ins = [ANY] + [VMEM] * 4 + [ANY] + [VMEM] * (len(received) + 1)
-    run = call(functools.partial(adjoint_kernel, g, bool(received)), ins, outs, scratch, 3 * 10**8, 58, interpret)
-    return run(table, own, *halos, cot, *received, planes)
-
-
-def pack(g, table, state, phlo, phhi):
-    message = (10, g.cols, g.rads)
-    scratch = buffers((8, 4, g.cols, g.rads)) + [pltpu.SemaphoreType.DMA((2,))]
-    run = call(functools.partial(pack_kernel, g), [ANY, VMEM, VMEM], [(VMEM, message)] * 2, scratch, 10**6, 16)
-    return run(table, state, phlo, phhi)
-
-
-def corners(g, table, gphlo, gphhi, ahead, behind):
-    outs = [(VMEM, gphlo.shape), (VMEM, gphhi.shape)]
-    run = call(functools.partial(corner_kernel, g), [VMEM] * 4, outs, [], 10**6, 16)
-    return run(table, gphlo, gphhi, ahead, behind)
-
-
-def finish(g, table, cot, part, ahead, behind, from_right, from_left):
-    block = 8
-    body = pl.BlockSpec((8, block, g.cols, g.rads), lambda n: (0, n, 0, 0))
-    message = pl.BlockSpec((10, g.cols, g.rads), lambda n: (0, 0, 0))
-    side = [pl.BlockSpec((m, block, g.rads), lambda n: (0, n, 0)) for m in (8, 9)]
+    dma = pltpu.SemaphoreType.DMA
+    scratch += [dma((g.rows, 2)), dma((g.rows, 2)), dma((g.rows,)), dma((g.rows,))]
+    ins = [ANY, ANY] + [VMEM] * 7 + ([ANY] + [VMEM] * 6 if received else [])
+    run = call(functools.partial(adjoint_kernel, g, bool(received)), ins, outs, scratch, 3 * 10**8, 48, interpret)
+    return run(table, own, cot, *halos, planes, *received)
+
+
+def pack(g, table, state):
+    shape, sides, body, lines = sizes(g)
+    strip = (8, g.rows, 8, g.rads)
+    scratch = buffers((8, 4, g.cols, g.rads), strip, strip) + [pltpu.SemaphoreType.DMA((4,))]
+    outs = [(VMEM, s) for s in sides + [body, body]]
+    return call(functools.partial(pack_kernel, g), [ANY], outs, scratch, 10**6, 58)(table, state)
+
+
+def pack_corners(g, table, phlo, phhi):
+    lines = sizes(g)[3]
+    return call(functools.partial(pack_corner_kernel, g), [VMEM] * 2, [(VMEM, lines)] * 2, [], 10**6, 16)(
+        table, phlo, phhi
+    )
+
+
+def turn(g, table, ahead, behind):
+    lines = sizes(g)[3]
+    return call(functools.partial(turn_kernel, g), [VMEM] * 2, [(VMEM, lines)] * 2, [], 10**6, 16)(
+        table, ahead, behind
+    )
+
+
+def finish(g, table, part, *received):
+    strip = (8, g.rows - 4, 8, g.rads)
     return pl.pallas_call(
-        functools.partial(finish_kernel, g, block),
-        grid=(g.rows // block,),
-        out_shape=jax.ShapeDtypeStruct(cot.shape, jnp.float32),
-        in_specs=[SMEM, body, body, message, message] + side,
-        out_specs=body,
-        compiler_params=pltpu.CompilerParams(vmem_limit_bytes=32 << 20),
-        cost_estimate=pl.CostEstimate(flops=10**6, bytes_accessed=14 << 20, transcendentals=0),
-    )(table, cot, part, ahead, behind, from_right, from_left)
+        functools.partial(finish_kernel, g),
+        out_shape=jax.ShapeDtypeStruct(part.shape, jnp.float32),
+        in_specs=[SMEM, ANY] + [VMEM] * 6,
+        out_specs=ANY,
+        input_output_aliases={1: 0},
+        scratch_shapes=buffers((8, 4, g.cols, g.rads), strip, strip) + [pltpu.SemaphoreType.DMA((8,))],
+        compiler_params=pltpu.CompilerParams(vmem_limit_bytes=44 << 20),
+        cost_estimate=pl.CostEstimate(flops=10**6, bytes_accessed=7 << 20, transcendentals=0),
+    )(table, part, *received)
 
 
 class Place:
@@ -940,24 +1048,25 @@
     table = jnp.concatenate([table, flags])
     planes = jnp.asarray(g.radial_planes())
 
-    def halos_of(value, last, first):
+    def halos_of(last, first, ahead, behind):
         phlo, phhi = place.sideways(last, first)
-        return (phlo, phhi) + tuple(place.polar(*pack(g, table, value, phlo, phhi)))
+        body = place.polar(ahead, behind)
+        return (phlo, phhi) + tuple(body) + tuple(place.polar(*pack_corners(g, table, phlo, phhi)))
 
     def give_back(parts):
         gphlo, gphhi, ahead, behind = parts
+        from_left, from_right = place.sideways(gphhi, gphlo)
         ahead, behind = place.polar(ahead, behind)
-        to_left, to_right = corners(g, table, gphlo, gphhi, ahead, behind)
-        from_left, from_right = place.sideways(to_right, to_left)
-        return ahead, behind, from_right, from_left
-
-    first = jnp.concatenate([state[:, :, 0], state[7:8, :, 1]], 0)
-    halos_zero = halos_of(state, state[:, :, cols - 1], first)
-    moved, last, first = forward(g, table, state, halos_zero, planes)
-    halos_one = halos_of(moved, last, first)
+        to_left, to_right = turn(g, table, ahead, behind)
+        lines_left, lines_right = place.sideways(to_right, to_left)
+        return ahead, behind, from_right, from_left, lines_right, lines_left
+
+    halos_zero = halos_of(*pack(g, table, state))
+    moved, *rims = forward(g, table, state, halos_zero, planes)
+    halos_one = halos_of(*rims)
     part, *ghosts = adjoint(g, table, moved, halos_one, cotangent, planes)
-    part, *ghosts = adjoint(g, table, state, halos_zero, part, planes, give_back(ghosts))
-    return finish(g, table, cotangent, part, *give_back(ghosts))
+    part, *ghosts = adjoint(g, table, state, halos_zero, part, planes, (cotangent,) + give_back(ghosts))
+    return finish(g, table, part, *give_back(ghosts))
 
 
 def solution(mesh):

time: 188 us -> 143 us (0.76)
  waiting for transfers between devices: 48 us -> 28.8 us
  Pallas kernels: 103 us -> 85.4 us
  local copies, waits for them, and re-layouts: 17.8 us -> 0.87 us
  starting transfers between devices: 18 us -> 27.3 us
    pallas_call x7 -> x8, Pallas kernels: 83.4 us -> 69.5 us  [the longest x2 58.5 us: adjoint(): return run(table, own, cot, *halos, planes, *received)]
    unnamed x53 -> x4, local copies, waits for them, and re-layouts: 13.8 us -> 0.01 us
    ppermute x4 -> x6, waiting for transfers between devices: 21.7 us -> 7.87 us  [polar(): lax.ppermute(ahead, both, self.round)]
    ppermute x4 -> x6, waiting for transfers between devices: 9.93 us -> 1.62 us  [sideways(): lax.ppermute(to_left, 'ph', self.left)]
    ppermute x4 -> x6, starting transfers between devices: 8.55 us -> 13.4 us  [sideways(): lax.ppermute(to_left, 'ph', self.left)]
    ppermute x4 -> x6, waiting for transfers between devices: 9.99 us -> 14.7 us  [sideways(): lax.ppermute(to_right, 'ph', self.right)]
    pallas_call x1, Pallas kernels: 20 us -> 15.8 us  [forward(): return run(table, own, *halos, planes)]
    slice x2 -> x0, local copies, waits for them, and re-layouts: 3.11 us -> none  [shards(): first = jnp.concatenate([state[:, :, 0], state[7:8, :, 1]], 0)]
  transfers between devices with their start and end apart: 16 -> 24, of which waited for: 14 -> 17; matrix products, arithmetic and copies ran while one was open for 1% -> 0% of each run, Pallas kernels for 0% -> 2%
where the time goes in v3:
time: 143 us
  Pallas kernels  85.4 us (60%)
  waiting for transfers between devices  28.8 us (20%)
  starting transfers between devices  27.3 us (19%)
    pallas_call x2, Pallas kernels, adjoint(): return run(table, own, cot, *halos, planes, *received)  58.5 us
    pallas_call x1, Pallas kernels, forward(): return run(table, own, *halos, planes)  15.8 us
    ppermute x6, waiting for transfers between devices, sideways(): lax.ppermute(to_right, 'ph', self.right)  14.7 us
    ppermute x6, starting transfers between devices, sideways(): lax.ppermute(to_left, 'ph', self.left)  13.4 us
    ppermute x6, starting transfers between devices, polar(): lax.ppermute(ahead, both, self.round)  9.32 us
    ppermute x6, waiting for transfers between devices, polar(): lax.ppermute(ahead, both, self.round)  7.87 us
    ppermute x6, waiting for transfers between devices, polar(): lax.ppermute(behind, both, self.back)  4.6 us
    pallas_call x1, Pallas kernels, finish(): pl.pallas_call(functools.partial(finish_kernel, g), out_shape=jax.ShapeDt...  4.54 us
  transfers between devices with their start and end apart: 24, of which 17 were waited for; matrix products, arithmetic and copies ran while one was open for 0% of the time, Pallas kernels for 2%

profile of v3, /device:TPU:0, one launch (start us, length us, event | category | flops | bytes accessed | tf_op | source)
XLA Modules:
  0.0 143.2 jit_solution(13973430601646806920)
XLA Ops:
  0.0 0.8 constant_dynamic-slice_fusion
  1.0 0.6 pad_maximum_fusion.row_ref
  1.6 4.2 %shard_map.46 = (f32[8,24,256]{2,1,0:T(8,128)}, f32[9,24,256]{2,1,0:T(8,128)}, f32[9,24,256]{2,1,0:T(8,128)}, f32[9,24,256]{2,1,0:T(8,128)}) custom-call(f32[177]{0:T(256)} %pad_maximum_fusion.row_ref, f32[8,24,24,256]{3,2,1,0:T(8,128)} %own.3), custom_call_target="tpu_custom_call" | custom-call | flops 1000000 | bytes 16777216 | tf_op jit(solution)/shard_map/pallas_call | solution.py:986
  5.8 3.4 %collective-permute-start.1 = (f32[9,24,256]{2,1,0:T(8,128)}, f32[9,24,256]{2,1,0:T(8,128)S(1)}, u32[]{:S(2)}, u32[]{:S(2)}) collective-permute-start(f32[9,24,256]{2,1,0:T(8,128)} %get-tuple-element.33), channel_id=1, source_target_pairs={{1,0},{2,1},{3,2},{4,3},{5,4},{6,5},{7,6},{0,7},{9,8},{10,9},{11,1... | collective-permute-start | bytes 663560 | tf_op jit(solution)/shard_map/ppermute | solution.py:1039
  9.2 1.6 %collective-permute-start.2 = (f32[9,24,256]{2,1,0:T(8,128)}, f32[9,24,256]{2,1,0:T(8,128)S(1)}, u32[]{:S(2)}, u32[]{:S(2)}) collective-permute-start(f32[9,24,256]{2,1,0:T(8,128)} %get-tuple-element.34), channel_id=1, source_target_pairs={{0,8},{4,0},{1,9},{5,1},{2,10},{6,2},{3,11},{7,3},{8,16},{12,4},{9... | collective-permute-start | bytes 663560 | tf_op jit(solution)/shard_map/ppermute | solution.py:1036
  11.2 4.9 %collective-permute-done.phlo.refs_0_ = f32[8,24,256]{2,1,0:T(8,128)S(1)} collective-permute-done((f32[8,24,256]{2,1,0:T(8,128)}, f32[8,24,256]{2,1,0:T(8,128)S(1)}, u32[]{:S(2)}, u32[]{:S(2)}) %collective-permute-start) | collective-permute-done | bytes 196640 | tf_op jit(solution)/shard_map/ppermute | solution.py:1039
  16.1 0.6 shard_map.47
  16.7 1.5 %collective-permute-start.4 = (f32[24,256]{1,0:T(8,128)S(1)}, f32[24,256]{1,0:T(8,128)S(1)}, u32[]{:S(2)}, u32[]{:S(2)}) collective-permute-start(f32[24,256]{1,0:T(8,128)S(1)} %get-tuple-element.36), channel_id=1, source_target_pairs={{0,8},{4,0},{1,9},{5,1},{2,10},{6,2},{3,11},{7,3},{8,16},{12,4},{9... | collective-permute-start | bytes 73736 | tf_op jit(solution)/shard_map/ppermute | solution.py:1036
  18.9 1.7 %collective-permute-done.4.refs_4_ = f32[24,256]{1,0:T(8,128)S(1)} collective-permute-done((f32[24,256]{1,0:T(8,128)S(1)}, f32[24,256]{1,0:T(8,128)S(1)}, u32[]{:S(2)}, u32[]{:S(2)}) %collective-permute-start.4) | collective-permute-done | bytes 24608 | tf_op jit(solution)/shard_map/ppermute | solution.py:1036
  20.5 1.5 %collective-permute-done.5.refs_5_ = f32[24,256]{1,0:T(8,128)S(1)} collective-permute-done((f32[24,256]{1,0:T(8,128)S(1)}, f32[24,256]{1,0:T(8,128)S(1)}, u32[]{:S(2)}, u32[]{:S(2)}) %collective-permute-start.5) | collective-permute-done | bytes 24608 | tf_op jit(solution)/shard_map/ppermute | solution.py:1036
  22.0 15.8 %shard_map.48 = (f32[8,24,24,256]{3,2,1,0:T(8,128)}, f32[8,24,256]{2,1,0:T(8,128)S(1)}, f32[9,24,256]{2,1,0:T(8,128)S(1)}, f32[9,24,256]{2,1,0:T(8,128)S(1)}, f32[9,24,256]{2,1,0:T(8,128)S(1)}) custom-call(f32[177]{0:T(256)S(1)} %copy-done.1, f32[8,24,24,256]{3,2,1,0:T(8,128)} %own.3, f32[8,24,256]{2,1,0:T(8,128)S(1)} %collective-permute-done.phlo.refs_0_, ...), custom_call_target="tpu_custom_call" | custom-call | flops 100000000 | bytes 16777216 | tf_op jit(solution)/shard_map/pallas_call | solution.py:956
  38.4 1.6 %collective-permute-start.8 = (f32[9,24,256]{2,1,0:T(8,128)S(1)}, f32[9,24,256]{2,1,0:T(8,128)S(1)}, u32[]{:S(2)}, u32[]{:S(2)}) collective-permute-start(f32[9,24,256]{2,1,0:T(8,128)S(1)} %get-tuple-element.41), channel_id=1, source_target_pairs={{0,8},{4,0},{1,9},{5,1},{2,10},{6,2},{3,11},{7,3},{8,16},{12,4},{9... | collective-permute-start | bytes 663560 | tf_op jit(solution)/shard_map/ppermute | solution.py:1036
  40.4 3.6 %collective-permute-done.6.phlo.refs_0_ = f32[8,24,256]{2,1,0:T(8,128)S(1)} collective-permute-done((f32[8,24,256]{2,1,0:T(8,128)S(1)}, f32[8,24,256]{2,1,0:T(8,128)S(1)}, u32[]{:S(2)}, u32[]{:S(2)}) %collective-permute-start.6) | collective-permute-done | bytes 196640 | tf_op jit(solution)/shard_map/ppermute | solution.py:1039
  44.7 1.6 %collective-permute-start.10 = (f32[24,256]{1,0:T(8,128)S(1)}, f32[24,256]{1,0:T(8,128)S(1)}, u32[]{:S(2)}, u32[]{:S(2)}) collective-permute-start(f32[24,256]{1,0:T(8,128)S(1)} %get-tuple-element.43), channel_id=1, source_target_pairs={{0,8},{4,0},{1,9},{5,1},{2,10},{6,2},{3,11},{7,3},{8,16},{12,4},{9... | collective-permute-start | bytes 73736 | tf_op jit(solution)/shard_map/ppermute | solution.py:1036
  46.7 1.4 collective-permute-done.8.refs_2_
  48.5 1.5 %collective-permute-done.11.refs_5_ = f32[24,256]{1,0:T(8,128)S(1)} collective-permute-done((f32[24,256]{1,0:T(8,128)S(1)}, f32[24,256]{1,0:T(8,128)S(1)}, u32[]{:S(2)}, u32[]{:S(2)}) %collective-permute-start.11) | collective-permute-done | bytes 24608 | tf_op jit(solution)/shard_map/ppermute | solution.py:1036
  50.1 28.9 %shard_map.50 = (f32[8,24,24,256]{3,2,1,0:T(8,128)}, f32[8,24,256]{2,1,0:T(8,128)S(1)}, f32[9,24,256]{2,1,0:T(8,128)S(1)}, f32[10,24,256]{2,1,0:T(8,128)S(1)}, f32[10,24,256]{2,1,0:T(8,128)S(1)}) custom-call(f32[177]{0:T(256)S(1)} %copy-done.1, f32[8,24,24,256]{3,2,1,0:T(8,128)} %get-tuple-element.38.own, f32[8,24,24,256]{3,2,1,0:T(8,128)} %refs_7_.1, ...), custom_call_target="tpu_custom_call" | custom-call | flops 300000000 | bytes 16777216 | tf_op jit(solution)/shard_map/pallas_call | solution.py:978
  79.0 1.7 %collective-permute-start.12 = (f32[10,24,256]{2,1,0:T(8,128)S(1)}, f32[10,24,256]{2,1,0:T(8,128)S(1)}, u32[]{:S(2)}, u32[]{:S(2)}) collective-permute-start(f32[10,24,256]{2,1,0:T(8,128)S(1)} %get-tuple-element.46), channel_id=1, source_target_pairs={{0,8},{4,0},{1,9},{5,1},{2,10},{6,2},{3,11},{7,3},{8,16},{12,4},{9... | collective-permute-start | bytes 737288 | tf_op jit(solution)/shard_map/ppermute | solution.py:1036
  81.0 2.6 %collective-permute-start.14 = (f32[8,24,256]{2,1,0:T(8,128)S(1)}, f32[8,24,256]{2,1,0:T(8,128)S(1)}, u32[]{:S(2)}, u32[]{:S(2)}) collective-permute-start(f32[8,24,256]{2,1,0:T(8,128)S(1)} %get-tuple-element.48), channel_id=1, source_target_pairs={{1,0},{2,1},{3,2},{4,3},{5,4},{6,5},{7,6},{0,7},{9,8},{10,9},{11,1... | collective-permute-start | bytes 589832 | tf_op jit(solution)/shard_map/ppermute | solution.py:1039
  83.7 2.3 %collective-permute-done.12.ahead.refs_8_ = f32[10,24,256]{2,1,0:T(8,128)S(1)} collective-permute-done((f32[10,24,256]{2,1,0:T(8,128)S(1)}, f32[10,24,256]{2,1,0:T(8,128)S(1)}, u32[]{:S(2)}, u32[]{:S(2)}) %collective-permute-start.12) | collective-permute-done | bytes 245792 | tf_op jit(solution)/shard_map/ppermute | solution.py:1036
  86.0 1.1 collective-permute-done.13.behind.refs_9_
  88.3 0.9 collective-permute-done.15.refs_11_
  89.3 2.7 %collective-permute-done.17.refs_13_ = f32[24,256]{1,0:T(8,128)S(1)} collective-permute-done((f32[24,256]{1,0:T(8,128)S(1)}, f32[24,256]{1,0:T(8,128)S(1)}, u32[]{:S(2)}, u32[]{:S(2)}) %collective-permute-start.17) | collective-permute-done | bytes 24608 | tf_op jit(solution)/shard_map/ppermute | solution.py:1039
  92.0 29.7 %shard_map.52 = (f32[8,24,24,256]{3,2,1,0:T(8,128)}, f32[8,24,256]{2,1,0:T(8,128)S(1)}, f32[9,24,256]{2,1,0:T(8,128)S(1)}, f32[10,24,256]{2,1,0:T(8,128)S(1)}, f32[10,24,256]{2,1,0:T(8,128)S(1)}) custom-call(f32[177]{0:T(256)S(1)} %copy-done.1, f32[8,24,24,256]{3,2,1,0:T(8,128)} %own.3, f32[8,24,24,256]{3,2,1,0:T(8,128)} %get-tuple-element.45.cot, ...), custom_call_target="tpu_custom_call" | custom-call | flops 300000000 | bytes 16777216 | tf_op jit(solution)/shard_map/pallas_call | solution.py:978
  121.6 1.4 collective-permute-start.18
  123.0 1.2 collective-permute-start.19
  124.2 2.6 %collective-permute-start.20 = (f32[8,24,256]{2,1,0:T(8,128)S(1)}, f32[8,24,256]{2,1,0:T(8,128)S(1)}, u32[]{:S(2)}, u32[]{:S(2)}) collective-permute-start(f32[8,24,256]{2,1,0:T(8,128)S(1)} %get-tuple-element.55), channel_id=1, source_target_pairs={{1,0},{2,1},{3,2},{4,3},{5,4},{6,5},{7,6},{0,7},{9,8},{10,9},{11,1... | collective-permute-start | bytes 589832 | tf_op jit(solution)/shard_map/ppermute | solution.py:1039
  126.9 2.0 %collective-permute-done.18.ahead = f32[10,24,256]{2,1,0:T(8,128)S(1)} collective-permute-done((f32[10,24,256]{2,1,0:T(8,128)S(1)}, f32[10,24,256]{2,1,0:T(8,128)S(1)}, u32[]{:S(2)}, u32[]{:S(2)}) %collective-permute-start.18) | collective-permute-done | bytes 245792 | tf_op jit(solution)/shard_map/ppermute | solution.py:1036
  129.9 4.6 %collective-permute-start.22 = (f32[24,256]{1,0:T(8,128)S(1)}, f32[24,256]{1,0:T(8,128)S(1)}, u32[]{:S(2)}, u32[]{:S(2)}) collective-permute-start(f32[24,256]{1,0:T(8,128)S(1)} %get-tuple-element.57), channel_id=1, source_target_pairs={{1,0},{2,1},{3,2},{4,3},{5,4},{6,5},{7,6},{0,7},{9,8},{10,9},{11,1... | collective-permute-start | bytes 73736 | tf_op jit(solution)/shard_map/ppermute | solution.py:1039
  134.5 1.5 %collective-permute-done.22.lines_right = f32[24,256]{1,0:T(8,128)S(1)} collective-permute-done((f32[24,256]{1,0:T(8,128)S(1)}, f32[24,256]{1,0:T(8,128)S(1)}, u32[]{:S(2)}, u32[]{:S(2)}) %collective-permute-start.22) | collective-permute-done | bytes 24608 | tf_op jit(solution)/shard_map/ppermute | solution.py:1039
  136.0 2.6 %collective-permute-done.23.lines_left = f32[24,256]{1,0:T(8,128)S(1)} collective-permute-done((f32[24,256]{1,0:T(8,128)S(1)}, f32[24,256]{1,0:T(8,128)S(1)}, u32[]{:S(2)}, u32[]{:S(2)}) %collective-permute-start.23) | collective-permute-done | bytes 24608 | tf_op jit(solution)/shard_map/ppermute | solution.py:1039
  138.7 4.5 %shard_map.54 = f32[8,24,24,256]{3,2,1,0:T(8,128)} custom-call(f32[177]{0:T(256)S(1)} %copy-done.1, f32[8,24,24,256]{3,2,1,0:T(8,128)} %get-tuple-element.52.part, f32[10,24,256]{2,1,0:T(8,128)S(1)} %collective-permute-done.18.ahead, f32[10,24,256]{2,1,0:T(8,128)S(1)} %collective-permute-done.19.behind, ...), custom_call_target="tpu_custom_call", output_to_operand_aliasing={{}: (1, {})} | custom-call | flops 1000000 | bytes 7340032 | tf_op jit(solution)/shard_map/pallas_call | solution.py:1005
  (33 shorter events, 6.5 us)
Async XLA Ops:
  0.0 22.0 %copy-start = (f32[13,2,8,128]{3,2,1,0:T(8,128)S(1)}, f32[13,2,8,128]{3,2,1,0:T(8,128)}, u32[]{:S(2)}) copy-start(f32[13,2,8,128]{3,2,1,0:T(8,128)} %constant.23.clone.refs_6_) | copy-start | bytes 319492
  1.6 14.5 %copy-start.1 = (f32[177]{0:T(256)S(1)}, f32[177]{0:T(256)}, u32[]{:S(2)}) copy-start(f32[177]{0:T(256)} %pad_maximum_fusion.row_ref) | copy-start | bytes 2128
  5.8 10.3 %collective-permute-start.1 = (f32[9,24,256]{2,1,0:T(8,128)}, f32[9,24,256]{2,1,0:T(8,128)S(1)}, u32[]{:S(2)}, u32[]{:S(2)}) collective-permute-start(f32[9,24,256]{2,1,0:T(8,128)} %get-tuple-element.33), channel_id=1, source_target_pairs={{1,0},{2,1},{3,2},{4,3},{5,4},{6,5},{7,6},{0,7},{9,8},{10,9},{11,1... | collective-permute-start | bytes 663560 | tf_op jit(solution)/shard_map/ppermute | solution.py:1039
  9.2 6.9 %collective-permute-start = (f32[8,24,256]{2,1,0:T(8,128)}, f32[8,24,256]{2,1,0:T(8,128)S(1)}, u32[]{:S(2)}, u32[]{:S(2)}) collective-permute-start(f32[8,24,256]{2,1,0:T(8,128)} %get-tuple-element.32), channel_id=1, source_target_pairs={{0,1},{1,2},{2,3},{3,4},{4,5},{5,6},{6,7},{7,0},{8,9},{9,10},{10,1... | collective-permute-start | bytes 589832 | tf_op jit(solution)/shard_map/ppermute | solution.py:1039
  9.2 9.7 %collective-permute-start.2 = (f32[9,24,256]{2,1,0:T(8,128)}, f32[9,24,256]{2,1,0:T(8,128)S(1)}, u32[]{:S(2)}, u32[]{:S(2)}) collective-permute-start(f32[9,24,256]{2,1,0:T(8,128)} %get-tuple-element.34), channel_id=1, source_target_pairs={{0,8},{4,0},{1,9},{5,1},{2,10},{6,2},{3,11},{7,3},{8,16},{12,4},{9... | collective-permute-start | bytes 663560 | tf_op jit(solution)/shard_map/ppermute | solution.py:1036
  10.7 8.1 %collective-permute-start.3 = (f32[9,24,256]{2,1,0:T(8,128)}, f32[9,24,256]{2,1,0:T(8,128)S(1)}, u32[]{:S(2)}, u32[]{:S(2)}) collective-permute-start(f32[9,24,256]{2,1,0:T(8,128)} %get-tuple-element.35), channel_id=1, source_target_pairs={{8,0},{0,4},{9,1},{1,5},{10,2},{2,6},{11,3},{3,7},{16,8},{4,12},{1... | collective-permute-start | bytes 663560 | tf_op jit(solution)/shard_map/ppermute | solution.py:1036
  16.7 3.9 %collective-permute-start.4 = (f32[24,256]{1,0:T(8,128)S(1)}, f32[24,256]{1,0:T(8,128)S(1)}, u32[]{:S(2)}, u32[]{:S(2)}) collective-permute-start(f32[24,256]{1,0:T(8,128)S(1)} %get-tuple-element.36), channel_id=1, source_target_pairs={{0,8},{4,0},{1,9},{5,1},{2,10},{6,2},{3,11},{7,3},{8,16},{12,4},{9... | collective-permute-start | bytes 73736 | tf_op jit(solution)/shard_map/ppermute | solution.py:1036
  18.2 3.8 %collective-permute-start.5 = (f32[24,256]{1,0:T(8,128)S(1)}, f32[24,256]{1,0:T(8,128)S(1)}, u32[]{:S(2)}, u32[]{:S(2)}) collective-permute-start(f32[24,256]{1,0:T(8,128)S(1)} %get-tuple-element.37), channel_id=1, source_target_pairs={{8,0},{0,4},{9,1},{1,5},{10,2},{2,6},{11,3},{3,7},{16,8},{4,12},{1... | collective-permute-start | bytes 73736 | tf_op jit(solution)/shard_map/ppermute | solution.py:1036
  37.8 6.2 %collective-permute-start.7 = (f32[9,24,256]{2,1,0:T(8,128)S(1)}, f32[9,24,256]{2,1,0:T(8,128)S(1)}, u32[]{:S(2)}, u32[]{:S(2)}) collective-permute-start(f32[9,24,256]{2,1,0:T(8,128)S(1)} %get-tuple-element.40), channel_id=1, source_target_pairs={{1,0},{2,1},{3,2},{4,3},{5,4},{6,5},{7,6},{0,7},{9,8},{10,9},{11,1... | collective-permute-start | bytes 663560 | tf_op jit(solution)/shard_map/ppermute | solution.py:1039
  37.9 6.2 %collective-permute-start.6 = (f32[8,24,256]{2,1,0:T(8,128)S(1)}, f32[8,24,256]{2,1,0:T(8,128)S(1)}, u32[]{:S(2)}, u32[]{:S(2)}) collective-permute-start(f32[8,24,256]{2,1,0:T(8,128)S(1)} %get-tuple-element.39), channel_id=1, source_target_pairs={{0,1},{1,2},{2,3},{3,4},{4,5},{5,6},{6,7},{7,0},{8,9},{9,10},{10,1... | collective-permute-start | bytes 589832 | tf_op jit(solution)/shard_map/ppermute | solution.py:1039
  38.4 9.7 %collective-permute-start.8 = (f32[9,24,256]{2,1,0:T(8,128)S(1)}, f32[9,24,256]{2,1,0:T(8,128)S(1)}, u32[]{:S(2)}, u32[]{:S(2)}) collective-permute-start(f32[9,24,256]{2,1,0:T(8,128)S(1)} %get-tuple-element.41), channel_id=1, source_target_pairs={{0,8},{4,0},{1,9},{5,1},{2,10},{6,2},{3,11},{7,3},{8,16},{12,4},{9... | collective-permute-start | bytes 663560 | tf_op jit(solution)/shard_map/ppermute | solution.py:1036
  40.0 8.1 %collective-permute-start.9 = (f32[9,24,256]{2,1,0:T(8,128)S(1)}, f32[9,24,256]{2,1,0:T(8,128)S(1)}, u32[]{:S(2)}, u32[]{:S(2)}) collective-permute-start(f32[9,24,256]{2,1,0:T(8,128)S(1)} %get-tuple-element.42), channel_id=1, source_target_pairs={{8,0},{0,4},{9,1},{1,5},{10,2},{2,6},{11,3},{3,7},{16,8},{4,12},{1... | collective-permute-start | bytes 663560 | tf_op jit(solution)/shard_map/ppermute | solution.py:1036
  44.7 3.9 %collective-permute-start.10 = (f32[24,256]{1,0:T(8,128)S(1)}, f32[24,256]{1,0:T(8,128)S(1)}, u32[]{:S(2)}, u32[]{:S(2)}) collective-permute-start(f32[24,256]{1,0:T(8,128)S(1)} %get-tuple-element.43), channel_id=1, source_target_pairs={{0,8},{4,0},{1,9},{5,1},{2,10},{6,2},{3,11},{7,3},{8,16},{12,4},{9... | collective-permute-start | bytes 73736 | tf_op jit(solution)/shard_map/ppermute | solution.py:1036
  46.2 3.8 %collective-permute-start.11 = (f32[24,256]{1,0:T(8,128)S(1)}, f32[24,256]{1,0:T(8,128)S(1)}, u32[]{:S(2)}, u32[]{:S(2)}) collective-permute-start(f32[24,256]{1,0:T(8,128)S(1)} %get-tuple-element.44), channel_id=1, source_target_pairs={{8,0},{0,4},{9,1},{1,5},{10,2},{2,6},{11,3},{3,7},{16,8},{4,12},{1... | collective-permute-start | bytes 73736 | tf_op jit(solution)/shard_map/ppermute | solution.py:1036
  79.0 7.0 %collective-permute-start.12 = (f32[10,24,256]{2,1,0:T(8,128)S(1)}, f32[10,24,256]{2,1,0:T(8,128)S(1)}, u32[]{:S(2)}, u32[]{:S(2)}) collective-permute-start(f32[10,24,256]{2,1,0:T(8,128)S(1)} %get-tuple-element.46), channel_id=1, source_target_pairs={{0,8},{4,0},{1,9},{5,1},{2,10},{6,2},{3,11},{7,3},{8,16},{12,4},{9... | collective-permute-start | bytes 737288 | tf_op jit(solution)/shard_map/ppermute | solution.py:1036
  80.6 6.5 %collective-permute-start.13 = (f32[10,24,256]{2,1,0:T(8,128)S(1)}, f32[10,24,256]{2,1,0:T(8,128)S(1)}, u32[]{:S(2)}, u32[]{:S(2)}) collective-permute-start(f32[10,24,256]{2,1,0:T(8,128)S(1)} %get-tuple-element.47), channel_id=1, source_target_pairs={{8,0},{0,4},{9,1},{1,5},{10,2},{2,6},{11,3},{3,7},{16,8},{4,12},{1... | collective-permute-start | bytes 737288 | tf_op jit(solution)/shard_map/ppermute | solution.py:1036
  81.0 8.1 %collective-permute-start.15 = (f32[9,24,256]{2,1,0:T(8,128)S(1)}, f32[9,24,256]{2,1,0:T(8,128)S(1)}, u32[]{:S(2)}, u32[]{:S(2)}) collective-permute-start(f32[9,24,256]{2,1,0:T(8,128)S(1)} %get-tuple-element.49), channel_id=1, source_target_pairs={{0,1},{1,2},{2,3},{3,4},{4,5},{5,6},{6,7},{7,0},{8,9},{9,10},{10,1... | collective-permute-start | bytes 663560 | tf_op jit(solution)/shard_map/ppermute | solution.py:1039
  81.0 7.2 %collective-permute-start.14 = (f32[8,24,256]{2,1,0:T(8,128)S(1)}, f32[8,24,256]{2,1,0:T(8,128)S(1)}, u32[]{:S(2)}, u32[]{:S(2)}) collective-permute-start(f32[8,24,256]{2,1,0:T(8,128)S(1)} %get-tuple-element.48), channel_id=1, source_target_pairs={{1,0},{2,1},{3,2},{4,3},{5,4},{6,5},{7,6},{0,7},{9,8},{10,9},{11,1... | collective-permute-start | bytes 589832 | tf_op jit(solution)/shard_map/ppermute | solution.py:1039
  87.7 1.6 %collective-permute-start.16 = (f32[24,256]{1,0:T(8,128)S(1)}, f32[24,256]{1,0:T(8,128)S(1)}, u32[]{:S(2)}, u32[]{:S(2)}) collective-permute-start(f32[24,256]{1,0:T(8,128)S(1)} %get-tuple-element.50), channel_id=1, source_target_pairs={{1,0},{2,1},{3,2},{4,3},{5,4},{6,5},{7,6},{0,7},{9,8},{10,9},{11,1... | collective-permute-start | bytes 73736 | tf_op jit(solution)/shard_map/ppermute | solution.py:1039
  87.8 4.2 %collective-permute-start.17 = (f32[24,256]{1,0:T(8,128)S(1)}, f32[24,256]{1,0:T(8,128)S(1)}, u32[]{:S(2)}, u32[]{:S(2)}) collective-permute-start(f32[24,256]{1,0:T(8,128)S(1)} %get-tuple-element.51), channel_id=1, source_target_pairs={{0,1},{1,2},{2,3},{3,4},{4,5},{5,6},{6,7},{7,0},{8,9},{9,10},{10,1... | collective-permute-start | bytes 73736 | tf_op jit(solution)/shard_map/ppermute | solution.py:1039
  121.6 7.2 %collective-permute-start.18 = (f32[10,24,256]{2,1,0:T(8,128)S(1)}, f32[10,24,256]{2,1,0:T(8,128)S(1)}, u32[]{:S(2)}, u32[]{:S(2)}) collective-permute-start(f32[10,24,256]{2,1,0:T(8,128)S(1)} %get-tuple-element.53), channel_id=1, source_target_pairs={{0,8},{4,0},{1,9},{5,1},{2,10},{6,2},{3,11},{7,3},{8,16},{12,4},{9... | collective-permute-start | bytes 737288 | tf_op jit(solution)/shard_map/ppermute | solution.py:1036
  123.0 6.3 %collective-permute-start.19 = (f32[10,24,256]{2,1,0:T(8,128)S(1)}, f32[10,24,256]{2,1,0:T(8,128)S(1)}, u32[]{:S(2)}, u32[]{:S(2)}) collective-permute-start(f32[10,24,256]{2,1,0:T(8,128)S(1)} %get-tuple-element.54), channel_id=1, source_target_pairs={{8,0},{0,4},{9,1},{1,5},{10,2},{2,6},{11,3},{3,7},{16,8},{4,12},{1... | collective-permute-start | bytes 737288 | tf_op jit(solution)/shard_map/ppermute | solution.py:1036
  124.2 10.3 %collective-permute-start.21 = (f32[9,24,256]{2,1,0:T(8,128)S(1)}, f32[9,24,256]{2,1,0:T(8,128)S(1)}, u32[]{:S(2)}, u32[]{:S(2)}) collective-permute-start(f32[9,24,256]{2,1,0:T(8,128)S(1)} %get-tuple-element.56), channel_id=1, source_target_pairs={{0,1},{1,2},{2,3},{3,4},{4,5},{5,6},{6,7},{7,0},{8,9},{9,10},{10,1... | collective-permute-start | bytes 663560 | tf_op jit(solution)/shard_map/ppermute | solution.py:1039
  124.2 10.3 %collective-permute-start.20 = (f32[8,24,256]{2,1,0:T(8,128)S(1)}, f32[8,24,256]{2,1,0:T(8,128)S(1)}, u32[]{:S(2)}, u32[]{:S(2)}) collective-permute-start(f32[8,24,256]{2,1,0:T(8,128)S(1)} %get-tuple-element.55), channel_id=1, source_target_pairs={{1,0},{2,1},{3,2},{4,3},{5,4},{6,5},{7,6},{0,7},{9,8},{10,9},{11,1... | collective-permute-start | bytes 589832 | tf_op jit(solution)/shard_map/ppermute | solution.py:1039
  129.9 6.2 %collective-permute-start.22 = (f32[24,256]{1,0:T(8,128)S(1)}, f32[24,256]{1,0:T(8,128)S(1)}, u32[]{:S(2)}, u32[]{:S(2)}) collective-permute-start(f32[24,256]{1,0:T(8,128)S(1)} %get-tuple-element.57), channel_id=1, source_target_pairs={{1,0},{2,1},{3,2},{4,3},{5,4},{6,5},{7,6},{0,7},{9,8},{10,9},{11,1... | collective-permute-start | bytes 73736 | tf_op jit(solution)/shard_map/ppermute | solution.py:1039
  134.5 4.2 %collective-permute-start.23 = (f32[24,256]{1,0:T(8,128)S(1)}, f32[24,256]{1,0:T(8,128)S(1)}, u32[]{:S(2)}, u32[]{:S(2)}) collective-permute-start(f32[24,256]{1,0:T(8,128)S(1)} %get-tuple-element.58), channel_id=1, source_target_pairs={{0,1},{1,2},{2,3},{3,4},{4,5},{5,6},{6,7},{7,0},{8,9},{9,10},{10,1... | collective-permute-start | bytes 73736 | tf_op jit(solution)/shard_map/ppermute | solution.py:1039

commit v4 on v3

--- a/solution.py
+++ b/solution.py
@@ -20,7 +20,7 @@
 G1 = GAMMA - 1.0
 LANES = 128
 PAD = 32
-FACE_SLOTS, PULL_SLOTS = 32, 32
+FACE_SLOTS = 32
 FLIPS = (1.0, 1.0, -1.0, -1.0, 1.0, 1.0, -1.0, -1.0)
 SH, SL, AZ, COT, AK, KEEP, N_ROW = 0, 1, 2, 3, 4, 5, 6
 BOTTOM, TOP_END, NEAR = 0, 1, 2
@@ -131,6 +131,14 @@
     return jnp.concatenate([ref[field, 0, pl.ds(slot, 1), :], ref[field, 1, pl.ds(slot, 1), :]], 1)
 
 
+def put_column(g, ref, field, k, value):
+    ref[field, :, pl.ds(g.at(0, k), g.rows, stride=g.width), :] = value
+
+
+def column_of(g, ref, field, k, row=0):
+    return ref[field, :, pl.ds(g.at(row, k), g.rows, stride=g.width), :]
+
+
 def picker(g, row_ref, ahead, behind):
     near = row_ref[g.flags + NEAR] > 0.5
 
@@ -143,11 +151,11 @@
     return low, high
 
 
-def row_copies(g, hbm, ref, sem, row=None):
+def row_copies(g, hbm, ref, sem, row=None, parts=slice(None)):
     for j in range(g.rows) if row is None else (row,):
         for h in range(2):
             yield pltpu.make_async_copy(
-                hbm.at[:, j, :, pl.ds(h * LANES, LANES)], ref.at[:, h, pl.ds(g.at(j, 0), g.cols), :], sem.at[j, h]
+                hbm.at[parts, j, :, pl.ds(h * LANES, LANES)], ref.at[:, h, pl.ds(g.at(j, 0), g.cols), :], sem.at[j, h]
             )
 
 
@@ -184,11 +192,12 @@
     body_row(-1, low)
     ends(-1, lambda c, w: corner_low(slice((c, 9 + c, 18)[w], (c, 9 + c, 18)[w] + 1)))
 
-    def step(j, carry):
-        ends(j, lambda c, w: (phlo[c, pl.ds(j, 1), :], phhi[c, pl.ds(j, 1), :], phhi[8, pl.ds(j, 1), :])[w])
-        return carry
-
-    lax.fori_loop(0, rows, step, 0)
+    for c in range(8):
+        put_column(g, us, c, -1, split(phlo[c]))
+        put_column(g, us, c, cols, split(phhi[c]))
+    put_column(g, us, 7, cols + 1, split(phhi[8]))
+    for ref, k in ((phlo, -1), (phhi, cols)):
+        put_line(us, 6, g.at(0, k), ref[6, 0:1, :] * keep(0))
     body_row(rows, high)
     ends(rows, lambda c, w: corner_high(slice((c, 9 + c, 18)[w], (c, 9 + c, 18)[w] + 1)))
     far = keep(rows + 1)
@@ -376,40 +385,8 @@
     lax.fori_loop(0, g.rows, settle, 0)
 
 
-def adjoint_kernel(g, received, row_ref, own, cot, *refs):
-    halos, rc, refs = refs[:6], refs[6], refs[7:]
-    if received:
-        base, *got = refs[:7]
-        refs = refs[7:]
-    out, gphlo, gphhi, go_ahead, go_behind, us, cs, cf, ef, zf, ft, fp, stage, sem, sem_cot, sem_out, sem_base = refs
-    w, rows, cols = g.width, g.rows, g.cols
-    load = loader(8)
-    for copy in row_copies(g, own, us, sem):
-        copy.start()
-    for copy in row_copies(g, cot, cs, sem_cot):
-        copy.start()
-
-    def enter(j):
-        return pltpu.make_async_copy(base.at[:, j], stage.at[:, j], sem_base.at[j])
-
-    if received:
-        for j in range(rows):
-            enter(j).start()
-    zero = jnp.zeros((2, 8, LANES), jnp.float32)
-    for j in (-2, -1, rows, rows + 1):
-        for c in range(8):
-            for t in range(g.tiles):
-                put(cs, c, g.at(j, t * 8), zero)
-    for c in range(8):
-        put(cs, c, g.at(-2, -8), zero)
-
-    def clear(j, carry):
-        for c in range(8):
-            put(cs, c, g.at(j, cols), zero)
-        return carry
-
-    lax.fori_loop(0, rows, clear, 0)
-    fill_state(g, us, row_ref, halos)
+def cell_pass(g, us, row_ref, own, sem, cf):
+    w, rows = g.width, g.rows
     arrive(g, us, row_ref, own, sem, 0)
 
     def cells(n, carry):
@@ -432,6 +409,213 @@
 
     lax.fori_loop(0, rows + 3, cells, 0)
 
+
+def edge_pass(g, row_ref, rc, cs, base, ef, zf):
+    w, rows = g.width, g.rows
+    zero = jnp.zeros((2, 8, LANES), jnp.float32)
+    for f in range(3):
+        put(ef, f, g.at(-1, -8), zero)
+    for f in range(2):
+        zf[f, pl.ds(g.at(-1, -8), 8), :] = zero[0]
+
+    def edges(n, carry):
+        load = loader(w)
+        plane = planes_of(rc, w)
+        none = jnp.zeros((1, w, LANES), jnp.float32)
+        p = pl.multiple_of(g.at(-1, 0) + n * w, 8)
+        j = n - 1
+        row = (j + 2) * N_ROW
+        sl, az, ak, keep = [row_ref[row + i] for i in (SL, AZ, AK, KEEP)]
+        sh_below = row_ref[row - N_ROW + SH]
+        shell, lo, hi = plane(INV_SHELL), plane(LO), plane(HI)
+        c5, c6, c7 = load(cs, base, p), load(cs, base + 1, p), load(cs, base + 2, p)
+        rb = ak * (c6 - load(cs, base + 1, p - 1)) + (1.0 / g.dth) * (load(cs, base + 2, p - w) - c7)
+        put(ef, 0, p, (0.25 * g.dt * g.dr) * shell * rb)
+        q6 = keep * c6 * shell
+        zb = plane(INV_LO) * (sl * c5 - sh_below * load(cs, base, p - w)) + prev_r(hi * q6, none) - lo * q6
+        q7 = c7 * shell
+        hq7 = hi * q7
+        pb = plane(INV_LO) * az * (load(cs, base, p - 1) - c5) + lo * q7 - prev_r(hq7, none)
+        zl = 2.0 * hi[1:2] * q6[1:2]
+        plast = -2.0 * hq7[1:2]
+        put(ef, 1, p, (0.25 * g.dt) * (zb + next_r(zb, zl)))
+        put(ef, 2, p, (0.25 * g.dt) * (pb + next_r(pb, plast)))
+        zf[0, pl.ds(p, w), :] = (0.25 * g.dt) * zb[0]
+        zf[1, pl.ds(p, w), :] = (0.25 * g.dt) * pb[0]
+        return carry
+
+    lax.fori_loop(0, rows + 3, edges, 0)
+
+
+def clear_ghosts(g, cs, count):
+    zero = jnp.zeros((2, 8, LANES), jnp.float32)
+    for j in (-2, -1, g.rows, g.rows + 1):
+        for c in range(count):
+            for t in range(g.tiles):
+                put(cs, c, g.at(j, t * 8), zero)
+    for c in range(count):
+        put(cs, c, g.at(-2, -8), zero)
+
+    def clear(j, carry):
+        for c in range(count):
+            put(cs, c, g.at(j, g.cols), zero)
+        return carry
+
+    lax.fori_loop(0, g.rows, clear, 0)
+
+
+def edge_kernel(g, row_ref, cot, rc, ef_out, zf_out, cs, ef, zf, sem, sem_out):
+    for copy in row_copies(g, cot, cs, sem, parts=pl.ds(5, 3)):
+        copy.start()
+    clear_ghosts(g, cs, 3)
+    for copy in row_copies(g, cot, cs, sem, parts=pl.ds(5, 3)):
+        copy.wait()
+    edge_pass(g, row_ref, rc, cs, 0, ef, zf)
+    leave = [pltpu.make_async_copy(ef, ef_out, sem_out.at[0]), pltpu.make_async_copy(zf, zf_out, sem_out.at[1])]
+    for copy in leave:
+        copy.start()
+    for copy in leave:
+        copy.wait()
+
+
+def cell_pull(load, plane, us, cf, p, fr_, ft_, fp_, ub, sb, sources, cot, e, first, ghost_e):
+    none = jnp.zeros_like(first[0])
+    w1, w2, w3 = sources
+    e0, e1, e2 = e
+    s00, s11 = fr_[1], ft_[2] + w1
+    s22 = fp_[3] + w1 + cot * w2
+    s01 = fr_[2] + ft_[1] - w2
+    s02 = fr_[3] + fp_[1] - w3
+    s12 = ft_[3] + fp_[2] - cot * w3
+    v = [load(cf, d, p) for d in range(3)]
+    b = [load(cf, 3 + d, p) for d in range(3)]
+    h, q = load(cf, 9, p), load(cf, 10, p)
+    gg = (fr_[4], ft_[4], fp_[4])
+    flow = v[0] * gg[0] + v[1] * gg[1] + v[2] * gg[2]
+    beta = b[0] * gg[0] + b[1] * gg[1] + b[2] * gg[2]
+    vb = v[0] * b[0] + v[1] * b[1] + v[2] * b[2]
+    d00, d11, d22 = s00 + s00, s11 + s11, s22 + s22
+    sv = (
+        d00 * v[0] + s01 * v[1] + s02 * v[2],
+        s01 * v[0] + d11 * v[1] + s12 * v[2],
+        s02 * v[0] + s12 * v[1] + d22 * v[2],
+    )
+    sbm = (
+        d00 * b[0] + s01 * b[1] + s02 * b[2],
+        s01 * b[0] + d11 * b[1] + s12 * b[2],
+        s02 * b[0] + s12 * b[1] + d22 * b[2],
+    )
+    c2b = sb[0] + sb[1] + sb[2]
+    ptb = s00 + s11 + s22 + flow
+    pb = c2b * load(cf, 11, p) + ptb
+    pg = G1 * pb
+    bbb = 2.0 * (c2b * q) + ptb - pg
+    bxe = (b[1] * e2 - b[2] * e1, b[2] * e0 - b[0] * e2, b[0] * e1 - b[1] * e0)
+    exv = (e1 * v[2] - e2 * v[1], e2 * v[0] - e0 * v[2], e0 * v[1] - e1 * v[0])
+    rho_bar = ub[0] - c2b * load(cf, 12, p)
+    m_bar, b_bar = [], []
+    for d in range(3):
+        vbar = h * gg[d] - beta * b[d] + 2.0 * (v[d] * sb[d]) - bxe[d]
+        turn = q * vbar - pg * v[d]
+        f0 = (fr_[0], ft_[0], fp_[0])[d]
+        m_bar.append(ub[1 + d] + f0 + sv[d] + turn)
+        rho_bar = rho_bar - v[d] * (0.5 * sv[d] + turn + 0.5 * (pg * v[d]))
+        b_bar.append(b[d] * bbb - sbm[d] - vb * gg[d] - beta * v[d] - exv[d])
+    e_bar = ub[4] + flow + pg
+
+    first_lane = lax.broadcasted_iota(jnp.int32, none.shape, 2) == 0
+    v, b = [[x[0:1] for x in y] for y in (v, b)]
+    q, h = q[0:1], h[0:1]
+    bg = load(us, 5, p)[0:1]
+    h = h + (1.0 - 0.5 * GAMMA) * (bg * bg - b[0] * b[0])
+    vbg = vb[0:1] + v[0] * (bg - b[0])
+    s00, s01, s02, g0 = first[1], first[2], first[3], first[4]
+    e1, e2 = ghost_e
+    flow = v[0] * g0
+    beta = bg * g0
+    pb = s00 + flow
+    pg = G1 * pb
+    bbb = pb - pg
+    d00 = s00 + s00
+    sv = (d00 * v[0] + s01 * v[1] + s02 * v[2], s01 * v[0], s02 * v[0])
+    sbm = (d00 * bg + s01 * b[1] + s02 * b[2], s01 * bg, s02 * bg)
+    vbar = (
+        h * g0 - beta * bg - (b[1] * e2 - b[2] * e1),
+        bg * e2 - beta * b[1],
+        -(beta * b[2]) - bg * e1,
+    )
+    exv = (e1 * v[2] - e2 * v[1], e2 * v[0], -(e1 * v[0]))
+    more = [None] * 8
+    rho_more = none
+    for d in range(3):
+        turn = q * vbar[d] - pg * v[d]
+        more[1 + d] = sv[d] + turn + (first[0] if d == 0 else 0.0)
+        rho_more = rho_more - v[d] * (0.5 * sv[d] + turn + 0.5 * (pg * v[d]))
+        bd = bg if d == 0 else b[d]
+        more[5 + d] = bd * bbb - sbm[d] - beta * v[d] - exv[d]
+    more[5] = more[5] - vbg * g0
+    more[0] = rho_more
+    more[4] = flow + pg
+
+    def with_first(x, extra):
+        return x + jnp.concatenate([jnp.where(first_lane, extra, 0.0), none], 0)
+
+    radial = 0.5 * (plane(TOP) * b_bar[0] + prev_r(b_bar[0], 2.0 * more[5]))
+    values = [with_first(rho_bar, more[0])] + [with_first(m_bar[d], more[1 + d]) for d in range(3)]
+    return values + [
+        with_first(e_bar, more[4]),
+        radial,
+        with_first(b_bar[1], more[6]),
+        with_first(b_bar[2], more[7]),
+    ]
+
+
+def face_pull(halves, state, state2, speed, speed2, closed=None):
+    total = 0.5 * (speed + speed2)
+    inv = lax.rsqrt(total)
+    a = total * inv
+    if closed is not None:
+        a = a * closed
+    dot = halves[0] * (state2[0] - state[0])
+    for c in range(1, 5):
+        dot = dot + halves[c] * (state2[c] - state[c])
+    return halves + [a * x for x in halves] + [-0.25 * inv * dot]
+
+
+def adjoint_kernel(g, received, row_ref, own, cot, *refs):
+    halos, rc, refs = refs[:6], refs[6], refs[7:]
+    if received:
+        base, *got = refs[:7]
+        refs = refs[7:]
+    else:
+        ef_in, zf_in = refs[:2]
+        refs = refs[2:]
+    out, gphlo, gphhi, go_ahead, go_behind, us, cs, cf, ef, zf, ft, fp, stage, line_lo, held, az_col, *refs = refs
+    sem, sem_cot, sem_out, sem_base = refs
+    w, rows, cols = g.width, g.rows, g.cols
+    load = loader(8)
+    for copy in row_copies(g, own, us, sem):
+        copy.start()
+    for copy in row_copies(g, cot, cs, sem_cot):
+        copy.start()
+
+    def enter(j):
+        return pltpu.make_async_copy(base.at[:, j], stage.at[:, j], sem_base.at[j])
+
+    if received:
+        for j in range(rows):
+            enter(j).start()
+    zero = jnp.zeros((2, 8, LANES), jnp.float32)
+    clear_ghosts(g, cs, 8)
+    if not received:
+        enter_edges = [
+            pltpu.make_async_copy(ef_in, ef, sem_base.at[0]),
+            pltpu.make_async_copy(zf_in, zf, sem_base.at[1]),
+        ]
+        for copy in enter_edges:
+            copy.start()
+    fill_state(g, us, row_ref, halos)
+    cell_pass(g, us, row_ref, own, sem, cf)
     for copy in row_copies(g, cot, cs, sem_cot):
         copy.wait()
     if received:
@@ -442,14 +626,10 @@
         def add_line(c, slot, line):
             put_line(cs, c, slot, get_line(cs, c, slot) + line)
 
-        def columns(j, carry):
+        for k, ref in ((0, from_left), (cols - 1, from_right)):
             for c in range(8):
-                add_line(c, g.at(j, 0), from_left[c, pl.ds(j, 1), :])
-                add_line(c, g.at(j, cols - 1), from_right[c, pl.ds(j, 1), :])
-            add_line(7, g.at(j, 1), from_left[8, pl.ds(j, 1), :])
-            return carry
-
-        lax.fori_loop(0, rows, columns, 0)
+                put_column(g, cs, c, k, column_of(g, cs, c, k) + split(ref[c]))
+        put_column(g, cs, 7, 1, column_of(g, cs, 7, 1) + split(from_left[8]))
         for t in range(cols // 8):
             at = slice(t * 8, t * 8 + 8)
             for c in range(8):
@@ -469,87 +649,85 @@
             for j, share in ((1, 1.0 - bottom), (2, bottom)):
                 add_line(6, g.at(j, k), share * lines[8:9, :])
 
-    for f in range(3):
-        put(ef, f, g.at(-1, -8), zero)
-    for f in range(2):
-        zf[f, pl.ds(g.at(-1, -8), 8), :] = zero[0]
-
-    def edges(n, carry):
-        load = loader(w)
-        plane = planes_of(rc, w)
-        none = jnp.zeros((1, w, LANES), jnp.float32)
-        p = pl.multiple_of(g.at(-1, 0) + n * w, 8)
-        j = n - 1
-        row = (j + 2) * N_ROW
-        sl, az, ak, keep = [row_ref[row + i] for i in (SL, AZ, AK, KEEP)]
-        sh_below = row_ref[row - N_ROW + SH]
-        shell, lo, hi = plane(INV_SHELL), plane(LO), plane(HI)
-        c5, c6, c7 = load(cs, 5, p), load(cs, 6, p), load(cs, 7, p)
-        rb = ak * (c6 - load(cs, 6, p - 1)) + (1.0 / g.dth) * (load(cs, 7, p - w) - c7)
-        put(ef, 0, p, (0.25 * g.dt * g.dr) * shell * rb)
-        q6 = keep * c6 * shell
-        zb = plane(INV_LO) * (sl * c5 - sh_below * load(cs, 5, p - w)) + prev_r(hi * q6, none) - lo * q6
-        q7 = c7 * shell
-        hq7 = hi * q7
-        pb = plane(INV_LO) * az * (load(cs, 5, p - 1) - c5) + lo * q7 - prev_r(hq7, none)
-        zl = 2.0 * hi[1:2] * q6[1:2]
-        plast = -2.0 * hq7[1:2]
-        put(ef, 1, p, (0.25 * g.dt) * (zb + next_r(zb, zl)))
-        put(ef, 2, p, (0.25 * g.dt) * (pb + next_r(pb, plast)))
-        zf[0, pl.ds(p, w), :] = (0.25 * g.dt) * zb[0]
-        zf[1, pl.ds(p, w), :] = (0.25 * g.dt) * pb[0]
-        return carry
-
-    lax.fori_loop(0, rows + 3, edges, 0)
-
-    size = PULL_SLOTS
+    if received:
+        edge_pass(g, row_ref, rc, cs, 5, ef, zf)
+    else:
+        for copy in enter_edges:
+            copy.wait()
+
+    size = cols
     load = loader(size)
     plane = planes_of(rc, size)
     none = jnp.zeros((1, size, LANES), jnp.float32)
-    groups = w // size
     for f in range(11):
-        for t in range(g.tiles):
+        for t in range(cols // 8):
             put(ft, f, t * 8, zero)
-        put(fp, f, 0, zero)
-
-    def face_pull(halves, state, state2, speed, speed2, closed=None):
-        total = 0.5 * (speed + speed2)
-        inv = lax.rsqrt(total)
-        a = total * inv
-        if closed is not None:
-            a = a * closed
-        dot = halves[0] * (state2[0] - state[0])
-        for c in range(1, 5):
-            dot = dot + halves[c] * (state2[c] - state[c])
-        return halves + [a * x for x in halves] + [-0.25 * inv * dot]
+
+    def spread(j, carry):
+        az_col[pl.ds(j, 1), :] = jnp.full((1, LANES), row_ref[(j + 2) * N_ROW + AZ], jnp.float32)
+        return carry
+
+    lax.fori_loop(0, rows, spread, 0)
+    along = planes_of(rc, rows)
+
+    def down(ref, field, slot):
+        return ref[field, :, pl.ds(slot, rows, stride=w), :]
+
+    def down_ghost(field, slot):
+        return zf[field, pl.ds(slot, rows, stride=w), :][None]
+
+    def column(k):
+        p = g.at(0, k)
+        left, right = (p, p + 1) if k < 0 else (p - 1, p)
+        sign, source = (1.0, right) if k < 0 else (-1.0, left)
+        kaz = (sign * along(HALF_KV)) * az_col[...][None]
+        face = face_pull(
+            [kaz * down(cs, c, source) for c in range(5)],
+            [down(us, c, left) for c in range(5)],
+            [down(us, c, right) for c in range(5)],
+            down(cf, 8, left),
+            down(cf, 8, right),
+        )
+        nil = jnp.zeros((2, rows, LANES), jnp.float32)
+        nils = [nil] * 5
+        ub = face[5:10] if k < 0 else [-x for x in face[5:10]]
+        edge = p + 1 if k < 0 else p
+        e = (down(ef, 0, edge) + down(ef, 0, edge + w), down(ef, 2, edge), nil)
+        ghost_e = (down_ghost(1, edge), nil[0:1])
+        first = [nil[0:1]] * 5
+        values = cell_pull(
+            down, along, us, cf, p, nils, nils, face[:5], ub, [nil, nil, face[10]], [nil] * 3, 0.0, e, first, ghost_e
+        )
+        return face, values
+
+    face, values = column(-1)
+    for f in range(11):
+        line_lo[f] = jnp.zeros((2, rows + 8, LANES), jnp.float32)
+        line_lo[f, :, 1 : rows + 1, :] = face[f]
+    _, values_hi = column(cols)
+    for c in range(8):
+        us[c, :, pl.ds(g.at(0, -1), rows, stride=w), :] = values[c]
+        held[c] = values_hi[c]
+    for j in (-1, rows):
+        for k in (-1, cols):
+            p = g.at(j, k)
+            e0 = get_line(ef, 0, p) + get_line(ef, 0, p + 1) + get_line(ef, 0, p + w) + get_line(ef, 0, p + w + 1)
+            v1, v2, b1, b2, q = [get_line(cf, f, p) for f in (1, 2, 4, 5, 10)]
+            m1, m2 = -(q * b2 * e0), q * b1 * e0
+            blank = jnp.zeros_like(e0)
+            for c, x in enumerate((-(v1 * m1 + v2 * m2), blank, m1, m2, blank, blank, e0 * v2, -(e0 * v1))):
+                put_line(us, c, p, x)
 
     def pull(n, carry):
-        p = pl.multiple_of(g.at(-1, -8) + n * size, 8)
-        j = n // groups - 1
-        slot = pl.multiple_of(lax.rem(n, groups) * size, 8)
-        row = (j + 2) * N_ROW
-        sh, az, cot = [row_ref[row + i] for i in (SH, AZ, COT)]
+        p = pl.multiple_of(g.at(-1, 0) + n * w, 8)
+        row = (n + 1) * N_ROW
+        sh, az = [row_ref[row + i] for i in (SH, AZ)]
         sl_above = row_ref[row + N_ROW + SL]
         state = [load(us, c, p) for c in range(5)]
         cc = [load(cs, c, p) for c in range(5)]
         kd = plane(HALF_KV)
-        sides = []
-        up = kd * sl_above
-        down = kd * sh
-        pw = pl.multiple_of(p + jnp.where(n >= (rows + 1) * groups, 0, w), 8)
-        high = face_pull(
-            [up * load(cs, c, pw) - down * cc[c] for c in range(5)],
-            state,
-            [load(us, c, pw) for c in range(5)],
-            load(cf, 7, p),
-            load(cf, 7, pw),
-        )
-        low = [load(ft, f, slot) for f in range(11)]
-        for f in range(11):
-            put(ft, f, slot, high[f])
-        sides.append((high, low))
         kaz = kd * az
-        high_p = face_pull(
+        face = face_pull(
             [kaz * (load(cs, c, p + 1) - cc[c]) for c in range(5)],
             state,
             [load(us, c, p + 1) for c in range(5)],
@@ -557,11 +735,27 @@
             load(cf, 8, p + 1),
         )
         for f in range(11):
-            put(fp, f, 8, high_p[f])
+            put(fp, f, 8, face[f])
+            fp[f, :, 7:8, :] = line_lo[f, :, pl.ds(n, 1), :]
+        up = kd * sl_above
+        down_by = kd * sh
+        pw = pl.multiple_of(p + jnp.where(n > rows, 0, w), 8)
+        face = face_pull(
+            [up * load(cs, c, pw) - down_by * cc[c] for c in range(5)],
+            state,
+            [load(us, c, pw) for c in range(5)],
+            load(cf, 7, p),
+            load(cf, 7, pw),
+        )
+        ft_ = [face[c] + load(ft, c, 0) for c in range(5)]
+        ub = [cc[c] + face[5 + c] - load(ft, 5 + c, 0) for c in range(5)]
+        sb1 = face[10] + load(ft, 10, 0)
+        for f in range(11):
+            put(ft, f, 0, face[f])
         per_volume = [plane(INV_V) * x for x in cc]
         half_hi = plane(HALF_HI2)
         speed = load(cf, 6, p)
-        high_r = face_pull(
+        face = face_pull(
             [half_hi * (next_r(x, none) - x) for x in per_volume],
             state,
             [next_r(x) for x in state],
@@ -570,117 +764,33 @@
             plane(OPEN),
         )
         first = [plane(HALF_LO2)[0:1] * x[0:1] for x in per_volume]
-        low_r = [prev_r(high_r[f], first[f] if f < 5 else none) for f in range(11)]
-        low_p = [load(fp, f, 7) for f in range(11)]
-        for f in range(11):
-            fp[f, :, 7:8, :] = fp[f, :, size + 7 : size + 8, :]
-        sides.append((high_p, low_p))
-        ft_, fp_ = [[hi_[c] + lo_[c] for c in range(5)] for hi_, lo_ in sides]
-        fr_ = [plane(TOP) * high_r[c] + low_r[c] for c in range(5)]
-        both = [(high_r, low_r)] + sides
-        ub = []
-        for c in range(5):
-            ub.append(
-                cc[c]
-                + (both[0][0][5 + c] - both[0][1][5 + c])
-                + (both[1][0][5 + c] - both[1][1][5 + c])
-                + (both[2][0][5 + c] - both[2][1][5 + c])
-            )
-        sb = [hi_[10] + lo_[10] for hi_, lo_ in both]
+        fr_ = [plane(TOP) * face[c] + prev_r(face[c], first[c]) for c in range(5)]
+        ub = [ub[c] + (face[5 + c] - prev_r(face[5 + c], none)) for c in range(5)]
+        sb0 = face[10] + prev_r(face[10], none)
+        fp_ = [load(fp, c, 8) + load(fp, c, 7) for c in range(5)]
+        ub = [ub[c] + (load(fp, 5 + c, 8) - load(fp, 5 + c, 7)) for c in range(5)]
+        sb = [sb0, sb1, load(fp, 10, 8) + load(fp, 10, 7)]
         mid = plane(INV_MID) * g.dt
-        w1, w2, w3 = cc[1] * mid, cc[2] * mid, cc[3] * mid
-        s00, s11 = fr_[1], ft_[2] + w1
-        s22 = fp_[3] + w1 + cot * w2
-        s01 = fr_[2] + ft_[1] - w2
-        s02 = fr_[3] + fp_[1] - w3
-        s12 = ft_[3] + fp_[2] - cot * w3
-        e0 = load(ef, 0, p) + load(ef, 0, p + 1) + load(ef, 0, p + w) + load(ef, 0, p + w + 1)
-        e2 = load(ef, 1, p) + load(ef, 1, p + w)
-        e1 = load(ef, 2, p) + load(ef, 2, p + 1)
-        v = [load(cf, d, p) for d in range(3)]
-        b = [load(cf, 3 + d, p) for d in range(3)]
-        h, q = load(cf, 9, p), load(cf, 10, p)
-        gg = (fr_[4], ft_[4], fp_[4])
-        flow = v[0] * gg[0] + v[1] * gg[1] + v[2] * gg[2]
-        beta = b[0] * gg[0] + b[1] * gg[1] + b[2] * gg[2]
-        vb = v[0] * b[0] + v[1] * b[1] + v[2] * b[2]
-        d00, d11, d22 = s00 + s00, s11 + s11, s22 + s22
-        sv = (
-            d00 * v[0] + s01 * v[1] + s02 * v[2],
-            s01 * v[0] + d11 * v[1] + s12 * v[2],
-            s02 * v[0] + s12 * v[1] + d22 * v[2],
+        sources = (cc[1] * mid, cc[2] * mid, cc[3] * mid)
+        e = (
+            load(ef, 0, p) + load(ef, 0, p + 1) + load(ef, 0, p + w) + load(ef, 0, p + w + 1),
+            load(ef, 2, p) + load(ef, 2, p + 1),
+            load(ef, 1, p) + load(ef, 1, p + w),
         )
-        sbm = (
-            d00 * b[0] + s01 * b[1] + s02 * b[2],
-            s01 * b[0] + d11 * b[1] + s12 * b[2],
-            s02 * b[0] + s12 * b[1] + d22 * b[2],
+        ghost_e = (
+            (zf[1, pl.ds(p, size), :] + zf[1, pl.ds(p + 1, size), :])[None],
+            (zf[0, pl.ds(p, size), :] + zf[0, pl.ds(p + w, size), :])[None],
         )
-        c2b = sb[0] + sb[1] + sb[2]
-        ptb = s00 + s11 + s22 + flow
-        pb = c2b * load(cf, 11, p) + ptb
-        pg = G1 * pb
-        bbb = 2.0 * (c2b * q) + ptb - pg
-        bxe = (b[1] * e2 - b[2] * e1, b[2] * e0 - b[0] * e2, b[0] * e1 - b[1] * e0)
-        exv = (e1 * v[2] - e2 * v[1], e2 * v[0] - e0 * v[2], e0 * v[1] - e1 * v[0])
-        rho_bar = ub[0] - c2b * load(cf, 12, p)
-        m_bar, b_bar = [], []
-        for d in range(3):
-            vbar = h * gg[d] - beta * b[d] + 2.0 * (v[d] * sb[d]) - bxe[d]
-            turn = q * vbar - pg * v[d]
-            f0 = (fr_[0], ft_[0], fp_[0])[d]
-            m_bar.append(ub[1 + d] + f0 + sv[d] + turn)
-            rho_bar = rho_bar - v[d] * (0.5 * sv[d] + turn + 0.5 * (pg * v[d]))
-            b_bar.append(b[d] * bbb - sbm[d] - vb * gg[d] - beta * v[d] - exv[d])
-        e_bar = ub[4] + flow + pg
-
-        first_lane = lax.broadcasted_iota(jnp.int32, (1, size, LANES), 2) == 0
-        v, b = [[x[0:1] for x in y] for y in (v, b)]
-        q, h = q[0:1], h[0:1]
-        bg = load(us, 5, p)[0:1]
-        h = h + (1.0 - 0.5 * GAMMA) * (bg * bg - b[0] * b[0])
-        vbg = vb[0:1] + v[0] * (bg - b[0])
-        s00, s01, s02, g0 = first[1], first[2], first[3], first[4]
-        e2 = (zf[0, pl.ds(p, size), :] + zf[0, pl.ds(p + w, size), :])[None]
-        e1 = (zf[1, pl.ds(p, size), :] + zf[1, pl.ds(p + 1, size), :])[None]
-        flow = v[0] * g0
-        beta = bg * g0
-        pb = s00 + flow
-        pg = G1 * pb
-        bbb = pb - pg
-        d00 = s00 + s00
-        sv = (d00 * v[0] + s01 * v[1] + s02 * v[2], s01 * v[0], s02 * v[0])
-        sbm = (d00 * bg + s01 * b[1] + s02 * b[2], s01 * bg, s02 * bg)
-        vbar = (
-            h * g0 - beta * bg - (b[1] * e2 - b[2] * e1),
-            bg * e2 - beta * b[1],
-            -(beta * b[2]) - bg * e1,
-        )
-        exv = (e1 * v[2] - e2 * v[1], e2 * v[0], -(e1 * v[0]))
-        more = [None] * 8
-        rho_more = none
-        for d in range(3):
-            turn = q * vbar[d] - pg * v[d]
-            more[1 + d] = sv[d] + turn + (first[0] if d == 0 else 0.0)
-            rho_more = rho_more - v[d] * (0.5 * sv[d] + turn + 0.5 * (pg * v[d]))
-            bd = bg if d == 0 else b[d]
-            more[5 + d] = bd * bbb - sbm[d] - beta * v[d] - exv[d]
-        more[5] = more[5] - vbg * g0
-        more[0] = rho_more
-        more[4] = flow + pg
-
-        def with_first(x, extra):
-            return x + jnp.concatenate([jnp.where(first_lane, extra, 0.0), none], 0)
-
-        put(us, 0, p, with_first(rho_bar, more[0]))
-        for d in range(3):
-            put(us, 1 + d, p, with_first(m_bar[d], more[1 + d]))
-        put(us, 4, p, with_first(e_bar, more[4]))
-        put(us, 5, p, load(cs, 5, p) + 0.5 * (plane(TOP) * b_bar[0] + prev_r(b_bar[0], 2.0 * more[5])))
-        put(us, 6, p, with_first(b_bar[1], more[6]))
-        put(us, 7, p, with_first(b_bar[2], more[7]))
-        return carry
-
-    lax.fori_loop(0, (rows + 2) * groups + 1, pull, 0)
+        cot = row_ref[row + COT]
+        values = cell_pull(load, plane, us, cf, p, fr_, ft_, fp_, ub, sb, sources, cot, e, first, ghost_e)
+        values[5] = values[5] + load(cs, 5, p)
+        for c in range(8):
+            put(us, c, p, values[c])
+        return carry
+
+    lax.fori_loop(0, rows + 2, pull, 0)
+    for c in range(8):
+        us[c, :, pl.ds(g.at(0, cols), rows, stride=w), :] = held[c]
     load = loader(8)
 
     def keep_of(j):
@@ -725,13 +835,19 @@
             leave_tile(6, join(load(cs, 6, p) + tile6(j, p)))
             leave_tile(7, join(load(cs, 7, p) + tile7(p)))
         leave(j).start()
-        for c in range(8):
-            gphlo[c, pl.ds(j, 1), :] = line_of(c, j, -1)
-            gphhi[c, pl.ds(j, 1), :] = line_of(c, j, cols)
-        gphhi[8, pl.ds(j, 1), :] = 0.5 * get_line(us, 7, g.at(j, cols))
         return carry
 
     lax.fori_loop(0, rows, give, 0)
+    for ref, k in ((gphlo, -1), (gphhi, cols)):
+        for c in range(6):
+            ref[c] = join(column_of(g, us, c, k))
+        faces = join(0.5 * (column_of(g, us, 6, k) + column_of(g, us, 6, k, -1)))
+        ref[6] = faces
+        ref[6, 0:1, :] = faces[0:1] * row_ref[2 * N_ROW + KEEP]
+    here = column_of(g, us, 7, cols)
+    gphlo[7] = join(0.5 * column_of(g, us, 7, -1))
+    gphhi[7] = join(0.5 * (here + column_of(g, us, 7, cols - 1)))
+    gphhi[8] = join(0.5 * here)
 
     bottom, top = row_ref[g.flags + BOTTOM], row_ref[g.flags + TOP_END]
     near = row_ref[g.flags + NEAR] > 0.5
@@ -956,7 +1072,7 @@
     return run(table, own, *halos, planes)
 
 
-def adjoint(g, table, own, halos, cot, planes, received=(), interpret=False):
+def adjoint(g, table, own, halos, cot, planes, more, received, interpret=False):
     n = g.slots
     shape, sides, body, lines = sizes(g)
     message = (10, g.cols, g.rads)
@@ -967,15 +1083,26 @@
         (13, 2, n, LANES),
         (3, 2, n, LANES),
         (2, n, LANES),
-        (11, 2, g.width, LANES),
-        (11, 2, 8 + PULL_SLOTS, LANES),
+        (11, 2, g.cols, LANES),
+        (11, 2, 8 + g.cols, LANES),
         shape,
+        (11, 2, g.rows + 8, LANES),
+        (8, 2, g.rows, LANES),
+        (g.rows, LANES),
     )
     dma = pltpu.SemaphoreType.DMA
     scratch += [dma((g.rows, 2)), dma((g.rows, 2)), dma((g.rows,)), dma((g.rows,))]
-    ins = [ANY, ANY] + [VMEM] * 7 + ([ANY] + [VMEM] * 6 if received else [])
-    run = call(functools.partial(adjoint_kernel, g, bool(received)), ins, outs, scratch, 3 * 10**8, 48, interpret)
-    return run(table, own, cot, *halos, planes, *received)
+    ins = [ANY, ANY] + [VMEM] * 7 + ([ANY] + [VMEM] * 6 if received else [ANY, ANY])
+    run = call(functools.partial(adjoint_kernel, g, received), ins, outs, scratch, 3 * 10**8, 48, interpret)
+    return run(table, own, cot, *halos, planes, *more)
+
+
+def edges_of(g, table, cot, planes):
+    n = g.slots
+    outs = [(ANY, (3, 2, n, LANES)), (ANY, (2, n, LANES))]
+    scratch = buffers((3, 2, n, LANES), *[s for _, s in outs])
+    scratch += [pltpu.SemaphoreType.DMA((g.rows, 2)), pltpu.SemaphoreType.DMA((2,))]
+    return call(functools.partial(edge_kernel, g), [ANY, VMEM], outs, scratch, 10**8, 16)(table, cot, planes)
 
 
 def pack(g, table, state):
@@ -1048,10 +1175,14 @@
     table = jnp.concatenate([table, flags])
     planes = jnp.asarray(g.radial_planes())
 
-    def halos_of(last, first, ahead, behind):
+    def halos_of(rims, beside=None):
+        last, first, ahead, behind = rims
         phlo, phhi = place.sideways(last, first)
         body = place.polar(ahead, behind)
-        return (phlo, phhi) + tuple(body) + tuple(place.polar(*pack_corners(g, table, phlo, phhi)))
+        done = None
+        if beside is not None:
+            phlo, phhi, done = lax.optimization_barrier((phlo, phhi, beside(first)))
+        return (phlo, phhi) + tuple(body) + tuple(place.polar(*pack_corners(g, table, phlo, phhi))), done
 
     def give_back(parts):
         gphlo, gphhi, ahead, behind = parts
@@ -1061,11 +1192,15 @@
         lines_left, lines_right = place.sideways(to_right, to_left)
         return ahead, behind, from_right, from_left, lines_right, lines_left
 
-    halos_zero = halos_of(*pack(g, table, state))
+    def edges_beside(rim):
+        return edges_of(g, table, lax.optimization_barrier((cotangent, rim))[0], planes)
+
+    halos_zero, edges = halos_of(pack(g, table, state), edges_beside)
     moved, *rims = forward(g, table, state, halos_zero, planes)
-    halos_one = halos_of(*rims)
-    part, *ghosts = adjoint(g, table, moved, halos_one, cotangent, planes)
-    part, *ghosts = adjoint(g, table, state, halos_zero, part, planes, (cotangent,) + give_back(ghosts))
+    halos_one, _ = halos_of(rims)
+    part, *ghosts = adjoint(g, table, moved, halos_one, cotangent, planes, edges, False)
+    more = (cotangent,) + give_back(ghosts)
+    part, *ghosts = adjoint(g, table, state, halos_zero, part, planes, more, True)
     return finish(g, table, part, *give_back(ghosts))
 
 

time: 143 us -> 139 us (0.972)
  waiting for transfers between devices: 28.8 us -> 24.1 us
    ppermute x6, waiting for transfers between devices: 14.7 us -> 10 us  [sideways(): lax.ppermute(to_right, 'ph', self.right)]
    pallas_call x2 -> x3, Pallas kernels: 58.5 us -> 57.6 us  [the longest x2 50.8 us: adjoint(): return run(table, own, cot, *halos, planes, *more)]
  transfers between devices with their start and end apart: 24 -> 24, of which waited for: 17 -> 15; matrix products, arithmetic and copies ran while one was open for 0% -> 0% of each run, Pallas kernels for 2% -> 6%
where the time goes in v4:
time: 139 us
  Pallas kernels  84.5 us (61%)
  starting transfers between devices  27.2 us (20%)
  waiting for transfers between devices  24.1 us (17%)
  local copies, waits for them, and re-layouts  1.74 us (1%)
    pallas_call x2, Pallas kernels, adjoint(): return run(table, own, cot, *halos, planes, *more)  50.8 us
    pallas_call x1, Pallas kernels, forward(): return run(table, own, *halos, planes)  15.9 us
    ppermute x6, starting transfers between devices, sideways(): lax.ppermute(to_left, 'ph', self.left)  13.3 us
    ppermute x6, waiting for transfers between devices, sideways(): lax.ppermute(to_right, 'ph', self.right)  10 us
    ppermute x6, starting transfers between devices, polar(): lax.ppermute(ahead, both, self.round)  9.27 us
    ppermute x6, waiting for transfers between devices, polar(): lax.ppermute(ahead, both, self.round)  7.78 us
    pallas_call x1, Pallas kernels, edges_of(): call(functools.partial(edge_kernel, g), [ANY, VMEM], outs, scratch, 10 **...  6.74 us
    ppermute x6, waiting for transfers between devices, polar(): lax.ppermute(behind, both, self.back)  4.6 us
  transfers between devices with their start and end apart: 24, of which 15 were waited for; matrix products, arithmetic and copies ran while one was open for 0% of the time, Pallas kernels for 6%

profile of v4, /device:TPU:0, one launch (start us, length us, event | category | flops | bytes accessed | tf_op | source)
XLA Modules:
  0.0 138.6 jit_solution(1258225817588931163)
XLA Ops:
  0.0 0.7 constant_dynamic-slice_fusion
  0.9 0.7 pad_maximum_fusion.row_ref
  1.6 4.3 %shard_map.46 = (f32[8,24,256]{2,1,0:T(8,128)}, f32[9,24,256]{2,1,0:T(8,128)}, f32[9,24,256]{2,1,0:T(8,128)}, f32[9,24,256]{2,1,0:T(8,128)}) custom-call(f32[177]{0:T(256)} %pad_maximum_fusion.row_ref, f32[8,24,24,256]{3,2,1,0:T(8,128)} %own.3), custom_call_target="tpu_custom_call" | custom-call | flops 1000000 | bytes 16777216 | tf_op jit(solution)/shard_map/pallas_call | solution.py:1113
  5.9 3.4 %collective-permute-start.1 = (f32[9,24,256]{2,1,0:T(8,128)}, f32[9,24,256]{2,1,0:T(8,128)S(1)}, u32[]{:S(2)}, u32[]{:S(2)}) collective-permute-start(f32[9,24,256]{2,1,0:T(8,128)} %get-tuple-element.40), channel_id=1, source_target_pairs={{1,0},{2,1},{3,2},{4,3},{5,4},{6,5},{7,6},{0,7},{9,8},{10,9},{11,1... | collective-permute-start | bytes 663560 | tf_op jit(solution)/shard_map/ppermute | solution.py:1166
  9.3 1.6 %collective-permute-start.2 = (f32[9,24,256]{2,1,0:T(8,128)}, f32[9,24,256]{2,1,0:T(8,128)S(1)}, u32[]{:S(2)}, u32[]{:S(2)}) collective-permute-start(f32[9,24,256]{2,1,0:T(8,128)} %get-tuple-element.46), channel_id=1, source_target_pairs={{0,8},{4,0},{1,9},{5,1},{2,10},{6,2},{3,11},{7,3},{8,16},{12,4},{9... | collective-permute-start | bytes 663560 | tf_op jit(solution)/shard_map/ppermute | solution.py:1163
  11.3 0.9 copy-done.1
  12.2 6.7 %shard_map.47 = (f32[3,2,960,128]{3,2,1,0:T(8,128)S(1)}, f32[2,960,128]{2,1,0:T(8,128)S(1)}) custom-call(f32[177]{0:T(256)S(1)} %copy-done.2, f32[8,24,24,256]{3,2,1,0:T(8,128)S(1)} %copy-done, f32[13,2,8,128]{3,2,1,0:T(8,128)S(1)} %copy-done.1), custom_call_target="tpu_custom_call" | custom-call | flops 100000000 | bytes 16777216 | tf_op jit(solution)/shard_map/pallas_call | solution.py:1105
  19.6 1.6 %collective-permute-start.4 = (f32[24,256]{1,0:T(8,128)S(1)}, f32[24,256]{1,0:T(8,128)S(1)}, u32[]{:S(2)}, u32[]{:S(2)}) collective-permute-start(f32[24,256]{1,0:T(8,128)S(1)} %get-tuple-element.48), channel_id=1, source_target_pairs={{0,8},{4,0},{1,9},{5,1},{2,10},{6,2},{3,11},{7,3},{8,16},{12,4},{9... | collective-permute-start | bytes 73736 | tf_op jit(solution)/shard_map/ppermute | solution.py:1163
  21.6 1.8 %collective-permute-done.4.refs_4_ = f32[24,256]{1,0:T(8,128)S(1)} collective-permute-done((f32[24,256]{1,0:T(8,128)S(1)}, f32[24,256]{1,0:T(8,128)S(1)}, u32[]{:S(2)}, u32[]{:S(2)}) %collective-permute-start.4) | collective-permute-done | bytes 24608 | tf_op jit(solution)/shard_map/ppermute | solution.py:1163
  23.4 1.6 %collective-permute-done.5.refs_5_ = f32[24,256]{1,0:T(8,128)S(1)} collective-permute-done((f32[24,256]{1,0:T(8,128)S(1)}, f32[24,256]{1,0:T(8,128)S(1)}, u32[]{:S(2)}, u32[]{:S(2)}) %collective-permute-start.5) | collective-permute-done | bytes 24608 | tf_op jit(solution)/shard_map/ppermute | solution.py:1163
  25.0 15.9 %shard_map.49 = (f32[8,24,24,256]{3,2,1,0:T(8,128)}, f32[8,24,256]{2,1,0:T(8,128)S(1)}, f32[9,24,256]{2,1,0:T(8,128)S(1)}, f32[9,24,256]{2,1,0:T(8,128)S(1)}, f32[9,24,256]{2,1,0:T(8,128)S(1)}) custom-call(f32[177]{0:T(256)S(1)} %copy-done.2, f32[8,24,24,256]{3,2,1,0:T(8,128)} %own.3, f32[8,24,256]{2,1,0:T(8,128)S(1)} %collective-permute-done.phlo.refs_0_, ...), custom_call_target="tpu_custom_call" | custom-call | flops 100000000 | bytes 16777216 | tf_op jit(solution)/shard_map/pallas_call | solution.py:1072
  41.5 1.6 %collective-permute-start.8 = (f32[9,24,256]{2,1,0:T(8,128)S(1)}, f32[9,24,256]{2,1,0:T(8,128)S(1)}, u32[]{:S(2)}, u32[]{:S(2)}) collective-permute-start(f32[9,24,256]{2,1,0:T(8,128)S(1)} %get-tuple-element.53), channel_id=1, source_target_pairs={{0,8},{4,0},{1,9},{5,1},{2,10},{6,2},{3,11},{7,3},{8,16},{12,4},{9... | collective-permute-start | bytes 663560 | tf_op jit(solution)/shard_map/ppermute | solution.py:1163
  43.5 3.7 %collective-permute-done.6.phlo.refs_0_ = f32[8,24,256]{2,1,0:T(8,128)S(1)} collective-permute-done((f32[8,24,256]{2,1,0:T(8,128)S(1)}, f32[8,24,256]{2,1,0:T(8,128)S(1)}, u32[]{:S(2)}, u32[]{:S(2)}) %collective-permute-start.6) | collective-permute-done | bytes 196640 | tf_op jit(solution)/shard_map/ppermute | solution.py:1166
  47.7 1.5 %collective-permute-start.10 = (f32[24,256]{1,0:T(8,128)S(1)}, f32[24,256]{1,0:T(8,128)S(1)}, u32[]{:S(2)}, u32[]{:S(2)}) collective-permute-start(f32[24,256]{1,0:T(8,128)S(1)} %get-tuple-element.55), channel_id=1, source_target_pairs={{0,8},{4,0},{1,9},{5,1},{2,10},{6,2},{3,11},{7,3},{8,16},{12,4},{9... | collective-permute-start | bytes 73736 | tf_op jit(solution)/shard_map/ppermute | solution.py:1163
  49.8 1.3 collective-permute-done.8.refs_2_
  51.6 1.4 %collective-permute-done.11.refs_5_ = f32[24,256]{1,0:T(8,128)S(1)} collective-permute-done((f32[24,256]{1,0:T(8,128)S(1)}, f32[24,256]{1,0:T(8,128)S(1)}, u32[]{:S(2)}, u32[]{:S(2)}) %collective-permute-start.11) | collective-permute-done | bytes 24608 | tf_op jit(solution)/shard_map/ppermute | solution.py:1163
  53.0 23.0 %shard_map.51 = (f32[8,24,24,256]{3,2,1,0:T(8,128)}, f32[8,24,256]{2,1,0:T(8,128)S(1)}, f32[9,24,256]{2,1,0:T(8,128)S(1)}, f32[10,24,256]{2,1,0:T(8,128)S(1)}, f32[10,24,256]{2,1,0:T(8,128)S(1)}) custom-call(f32[177]{0:T(256)S(1)} %copy-done.2, f32[8,24,24,256]{3,2,1,0:T(8,128)} %get-tuple-element.50.own, f32[8,24,24,256]{3,2,1,0:T(8,128)} %refs_7_.1, ...), custom_call_target="tpu_custom_call" | custom-call | flops 300000000 | bytes 16777216 | tf_op jit(solution)/shard_map/pallas_call | solution.py:1097
  76.1 1.6 %collective-permute-start.12 = (f32[10,24,256]{2,1,0:T(8,128)S(1)}, f32[10,24,256]{2,1,0:T(8,128)S(1)}, u32[]{:S(2)}, u32[]{:S(2)}) collective-permute-start(f32[10,24,256]{2,1,0:T(8,128)S(1)} %get-tuple-element.60), channel_id=1, source_target_pairs={{0,8},{4,0},{1,9},{5,1},{2,10},{6,2},{3,11},{7,3},{8,16},{12,4},{9... | collective-permute-start | bytes 737288 | tf_op jit(solution)/shard_map/ppermute | solution.py:1163
  78.2 2.6 %collective-permute-start.14 = (f32[8,24,256]{2,1,0:T(8,128)S(1)}, f32[8,24,256]{2,1,0:T(8,128)S(1)}, u32[]{:S(2)}, u32[]{:S(2)}) collective-permute-start(f32[8,24,256]{2,1,0:T(8,128)S(1)} %get-tuple-element.62), channel_id=1, source_target_pairs={{1,0},{2,1},{3,2},{4,3},{5,4},{6,5},{7,6},{0,7},{9,8},{10,9},{11,1... | collective-permute-start | bytes 589832 | tf_op jit(solution)/shard_map/ppermute | solution.py:1166
  80.8 2.4 %collective-permute-done.12.ahead.refs_8_ = f32[10,24,256]{2,1,0:T(8,128)S(1)} collective-permute-done((f32[10,24,256]{2,1,0:T(8,128)S(1)}, f32[10,24,256]{2,1,0:T(8,128)S(1)}, u32[]{:S(2)}, u32[]{:S(2)}) %collective-permute-start.12) | collective-permute-done | bytes 245792 | tf_op jit(solution)/shard_map/ppermute | solution.py:1163
  83.2 1.1 collective-permute-done.13.behind.refs_9_
  85.4 0.8 collective-permute-done.15.refs_11_
  86.4 2.9 %collective-permute-done.17.refs_13_ = f32[24,256]{1,0:T(8,128)S(1)} collective-permute-done((f32[24,256]{1,0:T(8,128)S(1)}, f32[24,256]{1,0:T(8,128)S(1)}, u32[]{:S(2)}, u32[]{:S(2)}) %collective-permute-start.17) | collective-permute-done | bytes 24608 | tf_op jit(solution)/shard_map/ppermute | solution.py:1166
  89.3 27.8 %shard_map.53 = (f32[8,24,24,256]{3,2,1,0:T(8,128)}, f32[8,24,256]{2,1,0:T(8,128)S(1)}, f32[9,24,256]{2,1,0:T(8,128)S(1)}, f32[10,24,256]{2,1,0:T(8,128)S(1)}, f32[10,24,256]{2,1,0:T(8,128)S(1)}) custom-call(f32[177]{0:T(256)S(1)} %copy-done.2, f32[8,24,24,256]{3,2,1,0:T(8,128)} %own.3, f32[8,24,24,256]{3,2,1,0:T(8,128)} %get-tuple-element.59.cot, ...), custom_call_target="tpu_custom_call" | custom-call | flops 300000000 | bytes 16777216 | tf_op jit(solution)/shard_map/pallas_call | solution.py:1097
  117.1 1.4 %collective-permute-start.18 = (f32[10,24,256]{2,1,0:T(8,128)S(1)}, f32[10,24,256]{2,1,0:T(8,128)S(1)}, u32[]{:S(2)}, u32[]{:S(2)}) collective-permute-start(f32[10,24,256]{2,1,0:T(8,128)S(1)} %get-tuple-element.67), channel_id=1, source_target_pairs={{0,8},{4,0},{1,9},{5,1},{2,10},{6,2},{3,11},{7,3},{8,16},{12,4},{9... | collective-permute-start | bytes 737288 | tf_op jit(solution)/shard_map/ppermute | solution.py:1163
  118.5 1.2 collective-permute-start.19
  119.7 2.6 %collective-permute-start.20 = (f32[8,24,256]{2,1,0:T(8,128)S(1)}, f32[8,24,256]{2,1,0:T(8,128)S(1)}, u32[]{:S(2)}, u32[]{:S(2)}) collective-permute-start(f32[8,24,256]{2,1,0:T(8,128)S(1)} %get-tuple-element.69), channel_id=1, source_target_pairs={{1,0},{2,1},{3,2},{4,3},{5,4},{6,5},{7,6},{0,7},{9,8},{10,9},{11,1... | collective-permute-start | bytes 589832 | tf_op jit(solution)/shard_map/ppermute | solution.py:1166
  122.3 1.8 %collective-permute-done.18.ahead = f32[10,24,256]{2,1,0:T(8,128)S(1)} collective-permute-done((f32[10,24,256]{2,1,0:T(8,128)S(1)}, f32[10,24,256]{2,1,0:T(8,128)S(1)}, u32[]{:S(2)}, u32[]{:S(2)}) %collective-permute-start.18) | collective-permute-done | bytes 245792 | tf_op jit(solution)/shard_map/ppermute | solution.py:1163
  125.2 4.5 %collective-permute-start.22 = (f32[24,256]{1,0:T(8,128)S(1)}, f32[24,256]{1,0:T(8,128)S(1)}, u32[]{:S(2)}, u32[]{:S(2)}) collective-permute-start(f32[24,256]{1,0:T(8,128)S(1)} %get-tuple-element.71), channel_id=1, source_target_pairs={{1,0},{2,1},{3,2},{4,3},{5,4},{6,5},{7,6},{0,7},{9,8},{10,9},{11,1... | collective-permute-start | bytes 73736 | tf_op jit(solution)/shard_map/ppermute | solution.py:1166
  129.8 1.5 %collective-permute-done.22.lines_right = f32[24,256]{1,0:T(8,128)S(1)} collective-permute-done((f32[24,256]{1,0:T(8,128)S(1)}, f32[24,256]{1,0:T(8,128)S(1)}, u32[]{:S(2)}, u32[]{:S(2)}) %collective-permute-start.22) | collective-permute-done | bytes 24608 | tf_op jit(solution)/shard_map/ppermute | solution.py:1166
  131.3 2.6 %collective-permute-done.23.lines_left = f32[24,256]{1,0:T(8,128)S(1)} collective-permute-done((f32[24,256]{1,0:T(8,128)S(1)}, f32[24,256]{1,0:T(8,128)S(1)}, u32[]{:S(2)}, u32[]{:S(2)}) %collective-permute-start.23) | collective-permute-done | bytes 24608 | tf_op jit(solution)/shard_map/ppermute | solution.py:1166
  133.9 4.5 %shard_map.55 = f32[8,24,24,256]{3,2,1,0:T(8,128)} custom-call(f32[177]{0:T(256)S(1)} %copy-done.2, f32[8,24,24,256]{3,2,1,0:T(8,128)} %get-tuple-element.66.part, f32[10,24,256]{2,1,0:T(8,128)S(1)} %collective-permute-done.18.ahead, f32[10,24,256]{2,1,0:T(8,128)S(1)} %collective-permute-done.19.behind, ...), custom_call_target="tpu_custom_call", output_to_operand_aliasing={{}: (1, {})} | custom-call | flops 1000000 | bytes 7340032 | tf_op jit(solution)/shard_map/pallas_call | solution.py:1132
  (36 shorter events, 7.2 us)
Async XLA Ops:
  0.8 10.5 %copy-start = (f32[8,24,24,256]{3,2,1,0:T(8,128)S(1)}, f32[8,24,24,256]{3,2,1,0:T(8,128)}, u32[]{:S(2)}) copy-start(f32[8,24,24,256]{3,2,1,0:T(8,128)} %refs_7_.1) | copy-start | bytes 14155780
  1.6 9.7 %copy-start.2 = (f32[177]{0:T(256)S(1)}, f32[177]{0:T(256)}, u32[]{:S(2)}) copy-start(f32[177]{0:T(256)} %pad_maximum_fusion.row_ref) | copy-start | bytes 2128
  5.9 13.1 %collective-permute-start.1 = (f32[9,24,256]{2,1,0:T(8,128)}, f32[9,24,256]{2,1,0:T(8,128)S(1)}, u32[]{:S(2)}, u32[]{:S(2)}) collective-permute-start(f32[9,24,256]{2,1,0:T(8,128)} %get-tuple-element.40), channel_id=1, source_target_pairs={{1,0},{2,1},{3,2},{4,3},{5,4},{6,5},{7,6},{0,7},{9,8},{10,9},{11,1... | collective-permute-start | bytes 663560 | tf_op jit(solution)/shard_map/ppermute | solution.py:1166
  9.3 9.7 %collective-permute-start = (f32[8,24,256]{2,1,0:T(8,128)}, f32[8,24,256]{2,1,0:T(8,128)S(1)}, u32[]{:S(2)}, u32[]{:S(2)}) collective-permute-start(f32[8,24,256]{2,1,0:T(8,128)} %get-tuple-element.39), channel_id=1, source_target_pairs={{0,1},{1,2},{2,3},{3,4},{4,5},{5,6},{6,7},{7,0},{8,9},{9,10},{10,1... | collective-permute-start | bytes 589832 | tf_op jit(solution)/shard_map/ppermute | solution.py:1166
  9.3 12.4 %collective-permute-start.2 = (f32[9,24,256]{2,1,0:T(8,128)}, f32[9,24,256]{2,1,0:T(8,128)S(1)}, u32[]{:S(2)}, u32[]{:S(2)}) collective-permute-start(f32[9,24,256]{2,1,0:T(8,128)} %get-tuple-element.46), channel_id=1, source_target_pairs={{0,8},{4,0},{1,9},{5,1},{2,10},{6,2},{3,11},{7,3},{8,16},{12,4},{9... | collective-permute-start | bytes 663560 | tf_op jit(solution)/shard_map/ppermute | solution.py:1163
  10.9 10.8 %collective-permute-start.3 = (f32[9,24,256]{2,1,0:T(8,128)}, f32[9,24,256]{2,1,0:T(8,128)S(1)}, u32[]{:S(2)}, u32[]{:S(2)}) collective-permute-start(f32[9,24,256]{2,1,0:T(8,128)} %get-tuple-element.47), channel_id=1, source_target_pairs={{8,0},{0,4},{9,1},{1,5},{10,2},{2,6},{11,3},{3,7},{16,8},{4,12},{1... | collective-permute-start | bytes 663560 | tf_op jit(solution)/shard_map/ppermute | solution.py:1163
  11.3 0.9 copy-start.1
  19.6 3.9 %collective-permute-start.4 = (f32[24,256]{1,0:T(8,128)S(1)}, f32[24,256]{1,0:T(8,128)S(1)}, u32[]{:S(2)}, u32[]{:S(2)}) collective-permute-start(f32[24,256]{1,0:T(8,128)S(1)} %get-tuple-element.48), channel_id=1, source_target_pairs={{0,8},{4,0},{1,9},{5,1},{2,10},{6,2},{3,11},{7,3},{8,16},{12,4},{9... | collective-permute-start | bytes 73736 | tf_op jit(solution)/shard_map/ppermute | solution.py:1163
  21.2 3.8 %collective-permute-start.5 = (f32[24,256]{1,0:T(8,128)S(1)}, f32[24,256]{1,0:T(8,128)S(1)}, u32[]{:S(2)}, u32[]{:S(2)}) collective-permute-start(f32[24,256]{1,0:T(8,128)S(1)} %get-tuple-element.49), channel_id=1, source_target_pairs={{8,0},{0,4},{9,1},{1,5},{10,2},{2,6},{11,3},{3,7},{16,8},{4,12},{1... | collective-permute-start | bytes 73736 | tf_op jit(solution)/shard_map/ppermute | solution.py:1163
  40.9 6.3 %collective-permute-start.7 = (f32[9,24,256]{2,1,0:T(8,128)S(1)}, f32[9,24,256]{2,1,0:T(8,128)S(1)}, u32[]{:S(2)}, u32[]{:S(2)}) collective-permute-start(f32[9,24,256]{2,1,0:T(8,128)S(1)} %get-tuple-element.52), channel_id=1, source_target_pairs={{1,0},{2,1},{3,2},{4,3},{5,4},{6,5},{7,6},{0,7},{9,8},{10,9},{11,1... | collective-permute-start | bytes 663560 | tf_op jit(solution)/shard_map/ppermute | solution.py:1166
  41.0 6.2 %collective-permute-start.6 = (f32[8,24,256]{2,1,0:T(8,128)S(1)}, f32[8,24,256]{2,1,0:T(8,128)S(1)}, u32[]{:S(2)}, u32[]{:S(2)}) collective-permute-start(f32[8,24,256]{2,1,0:T(8,128)S(1)} %get-tuple-element.51), channel_id=1, source_target_pairs={{0,1},{1,2},{2,3},{3,4},{4,5},{5,6},{6,7},{7,0},{8,9},{9,10},{10,1... | collective-permute-start | bytes 589832 | tf_op jit(solution)/shard_map/ppermute | solution.py:1166
  41.5 9.7 %collective-permute-start.8 = (f32[9,24,256]{2,1,0:T(8,128)S(1)}, f32[9,24,256]{2,1,0:T(8,128)S(1)}, u32[]{:S(2)}, u32[]{:S(2)}) collective-permute-start(f32[9,24,256]{2,1,0:T(8,128)S(1)} %get-tuple-element.53), channel_id=1, source_target_pairs={{0,8},{4,0},{1,9},{5,1},{2,10},{6,2},{3,11},{7,3},{8,16},{12,4},{9... | collective-permute-start | bytes 663560 | tf_op jit(solution)/shard_map/ppermute | solution.py:1163
  43.0 8.1 %collective-permute-start.9 = (f32[9,24,256]{2,1,0:T(8,128)S(1)}, f32[9,24,256]{2,1,0:T(8,128)S(1)}, u32[]{:S(2)}, u32[]{:S(2)}) collective-permute-start(f32[9,24,256]{2,1,0:T(8,128)S(1)} %get-tuple-element.54), channel_id=1, source_target_pairs={{8,0},{0,4},{9,1},{1,5},{10,2},{2,6},{11,3},{3,7},{16,8},{4,12},{1... | collective-permute-start | bytes 663560 | tf_op jit(solution)/shard_map/ppermute | solution.py:1163
  47.7 3.9 %collective-permute-start.10 = (f32[24,256]{1,0:T(8,128)S(1)}, f32[24,256]{1,0:T(8,128)S(1)}, u32[]{:S(2)}, u32[]{:S(2)}) collective-permute-start(f32[24,256]{1,0:T(8,128)S(1)} %get-tuple-element.55), channel_id=1, source_target_pairs={{0,8},{4,0},{1,9},{5,1},{2,10},{6,2},{3,11},{7,3},{8,16},{12,4},{9... | collective-permute-start | bytes 73736 | tf_op jit(solution)/shard_map/ppermute | solution.py:1163
  49.2 3.8 %collective-permute-start.11 = (f32[24,256]{1,0:T(8,128)S(1)}, f32[24,256]{1,0:T(8,128)S(1)}, u32[]{:S(2)}, u32[]{:S(2)}) collective-permute-start(f32[24,256]{1,0:T(8,128)S(1)} %get-tuple-element.56), channel_id=1, source_target_pairs={{8,0},{0,4},{9,1},{1,5},{10,2},{2,6},{11,3},{3,7},{16,8},{4,12},{1... | collective-permute-start | bytes 73736 | tf_op jit(solution)/shard_map/ppermute | solution.py:1163
  76.1 7.1 %collective-permute-start.12 = (f32[10,24,256]{2,1,0:T(8,128)S(1)}, f32[10,24,256]{2,1,0:T(8,128)S(1)}, u32[]{:S(2)}, u32[]{:S(2)}) collective-permute-start(f32[10,24,256]{2,1,0:T(8,128)S(1)} %get-tuple-element.60), channel_id=1, source_target_pairs={{0,8},{4,0},{1,9},{5,1},{2,10},{6,2},{3,11},{7,3},{8,16},{12,4},{9... | collective-permute-start | bytes 737288 | tf_op jit(solution)/shard_map/ppermute | solution.py:1163
  77.7 6.5 %collective-permute-start.13 = (f32[10,24,256]{2,1,0:T(8,128)S(1)}, f32[10,24,256]{2,1,0:T(8,128)S(1)}, u32[]{:S(2)}, u32[]{:S(2)}) collective-permute-start(f32[10,24,256]{2,1,0:T(8,128)S(1)} %get-tuple-element.61), channel_id=1, source_target_pairs={{8,0},{0,4},{9,1},{1,5},{10,2},{2,6},{11,3},{3,7},{16,8},{4,12},{1... | collective-permute-start | bytes 737288 | tf_op jit(solution)/shard_map/ppermute | solution.py:1163
  78.2 8.0 %collective-permute-start.15 = (f32[9,24,256]{2,1,0:T(8,128)S(1)}, f32[9,24,256]{2,1,0:T(8,128)S(1)}, u32[]{:S(2)}, u32[]{:S(2)}) collective-permute-start(f32[9,24,256]{2,1,0:T(8,128)S(1)} %get-tuple-element.63), channel_id=1, source_target_pairs={{0,1},{1,2},{2,3},{3,4},{4,5},{5,6},{6,7},{7,0},{8,9},{9,10},{10,1... | collective-permute-start | bytes 663560 | tf_op jit(solution)/shard_map/ppermute | solution.py:1166
  78.2 7.2 %collective-permute-start.14 = (f32[8,24,256]{2,1,0:T(8,128)S(1)}, f32[8,24,256]{2,1,0:T(8,128)S(1)}, u32[]{:S(2)}, u32[]{:S(2)}) collective-permute-start(f32[8,24,256]{2,1,0:T(8,128)S(1)} %get-tuple-element.62), channel_id=1, source_target_pairs={{1,0},{2,1},{3,2},{4,3},{5,4},{6,5},{7,6},{0,7},{9,8},{10,9},{11,1... | collective-permute-start | bytes 589832 | tf_op jit(solution)/shard_map/ppermute | solution.py:1166
  84.8 1.6 %collective-permute-start.16 = (f32[24,256]{1,0:T(8,128)S(1)}, f32[24,256]{1,0:T(8,128)S(1)}, u32[]{:S(2)}, u32[]{:S(2)}) collective-permute-start(f32[24,256]{1,0:T(8,128)S(1)} %get-tuple-element.64), channel_id=1, source_target_pairs={{1,0},{2,1},{3,2},{4,3},{5,4},{6,5},{7,6},{0,7},{9,8},{10,9},{11,1... | collective-permute-start | bytes 73736 | tf_op jit(solution)/shard_map/ppermute | solution.py:1166
  84.9 4.4 %collective-permute-start.17 = (f32[24,256]{1,0:T(8,128)S(1)}, f32[24,256]{1,0:T(8,128)S(1)}, u32[]{:S(2)}, u32[]{:S(2)}) collective-permute-start(f32[24,256]{1,0:T(8,128)S(1)} %get-tuple-element.65), channel_id=1, source_target_pairs={{0,1},{1,2},{2,3},{3,4},{4,5},{5,6},{6,7},{7,0},{8,9},{9,10},{10,1... | collective-permute-start | bytes 73736 | tf_op jit(solution)/shard_map/ppermute | solution.py:1166
  117.1 7.1 %collective-permute-start.18 = (f32[10,24,256]{2,1,0:T(8,128)S(1)}, f32[10,24,256]{2,1,0:T(8,128)S(1)}, u32[]{:S(2)}, u32[]{:S(2)}) collective-permute-start(f32[10,24,256]{2,1,0:T(8,128)S(1)} %get-tuple-element.67), channel_id=1, source_target_pairs={{0,8},{4,0},{1,9},{5,1},{2,10},{6,2},{3,11},{7,3},{8,16},{12,4},{9... | collective-permute-start | bytes 737288 | tf_op jit(solution)/shard_map/ppermute | solution.py:1163
  118.5 6.2 %collective-permute-start.19 = (f32[10,24,256]{2,1,0:T(8,128)S(1)}, f32[10,24,256]{2,1,0:T(8,128)S(1)}, u32[]{:S(2)}, u32[]{:S(2)}) collective-permute-start(f32[10,24,256]{2,1,0:T(8,128)S(1)} %get-tuple-element.68), channel_id=1, source_target_pairs={{8,0},{0,4},{9,1},{1,5},{10,2},{2,6},{11,3},{3,7},{16,8},{4,12},{1... | collective-permute-start | bytes 737288 | tf_op jit(solution)/shard_map/ppermute | solution.py:1163
  119.7 10.1 %collective-permute-start.21 = (f32[9,24,256]{2,1,0:T(8,128)S(1)}, f32[9,24,256]{2,1,0:T(8,128)S(1)}, u32[]{:S(2)}, u32[]{:S(2)}) collective-permute-start(f32[9,24,256]{2,1,0:T(8,128)S(1)} %get-tuple-element.70), channel_id=1, source_target_pairs={{0,1},{1,2},{2,3},{3,4},{4,5},{5,6},{6,7},{7,0},{8,9},{9,10},{10,1... | collective-permute-start | bytes 663560 | tf_op jit(solution)/shard_map/ppermute | solution.py:1166
  119.7 10.1 %collective-permute-start.20 = (f32[8,24,256]{2,1,0:T(8,128)S(1)}, f32[8,24,256]{2,1,0:T(8,128)S(1)}, u32[]{:S(2)}, u32[]{:S(2)}) collective-permute-start(f32[8,24,256]{2,1,0:T(8,128)S(1)} %get-tuple-element.69), channel_id=1, source_target_pairs={{1,0},{2,1},{3,2},{4,3},{5,4},{6,5},{7,6},{0,7},{9,8},{10,9},{11,1... | collective-permute-start | bytes 589832 | tf_op jit(solution)/shard_map/ppermute | solution.py:1166
  125.2 6.1 %collective-permute-start.22 = (f32[24,256]{1,0:T(8,128)S(1)}, f32[24,256]{1,0:T(8,128)S(1)}, u32[]{:S(2)}, u32[]{:S(2)}) collective-permute-start(f32[24,256]{1,0:T(8,128)S(1)} %get-tuple-element.71), channel_id=1, source_target_pairs={{1,0},{2,1},{3,2},{4,3},{5,4},{6,5},{7,6},{0,7},{9,8},{10,9},{11,1... | collective-permute-start | bytes 73736 | tf_op jit(solution)/shard_map/ppermute | solution.py:1166
  129.8 4.2 %collective-permute-start.23 = (f32[24,256]{1,0:T(8,128)S(1)}, f32[24,256]{1,0:T(8,128)S(1)}, u32[]{:S(2)}, u32[]{:S(2)}) collective-permute-start(f32[24,256]{1,0:T(8,128)S(1)} %get-tuple-element.72), channel_id=1, source_target_pairs={{0,1},{1,2},{2,3},{3,4},{4,5},{5,6},{6,7},{7,0},{8,9},{9,10},{10,1... | collective-permute-start | bytes 73736 | tf_op jit(solution)/shard_map/ppermute | solution.py:1166

commit v5 on v4

--- a/solution.py
+++ b/solution.py
@@ -464,18 +464,13 @@
     lax.fori_loop(0, g.rows, clear, 0)
 
 
-def edge_kernel(g, row_ref, cot, rc, ef_out, zf_out, cs, ef, zf, sem, sem_out):
+def edge_kernel(g, row_ref, cot, rc, ef, zf, cs, sem):
     for copy in row_copies(g, cot, cs, sem, parts=pl.ds(5, 3)):
         copy.start()
     clear_ghosts(g, cs, 3)
     for copy in row_copies(g, cot, cs, sem, parts=pl.ds(5, 3)):
         copy.wait()
     edge_pass(g, row_ref, rc, cs, 0, ef, zf)
-    leave = [pltpu.make_async_copy(ef, ef_out, sem_out.at[0]), pltpu.make_async_copy(zf, zf_out, sem_out.at[1])]
-    for copy in leave:
-        copy.start()
-    for copy in leave:
-        copy.wait()
 
 
 def cell_pull(load, plane, us, cf, p, fr_, ft_, fp_, ub, sb, sources, cot, e, first, ghost_e):
@@ -588,9 +583,13 @@
         base, *got = refs[:7]
         refs = refs[7:]
     else:
-        ef_in, zf_in = refs[:2]
-        refs = refs[2:]
-    out, gphlo, gphhi, go_ahead, go_behind, us, cs, cf, ef, zf, ft, fp, stage, line_lo, held, az_col, *refs = refs
+        ef, zf, *refs = refs
+    out, gphlo, gphhi, go_ahead, go_behind, *refs = refs
+    if received:
+        edge, left, right, *refs = refs
+    us, cs, cf, ft, fp, stage, line_lo, held, az_col, *refs = refs
+    if received:
+        ef, zf, *refs = refs
     sem, sem_cot, sem_out, sem_base = refs
     w, rows, cols = g.width, g.rows, g.cols
     load = loader(8)
@@ -607,13 +606,6 @@
             enter(j).start()
     zero = jnp.zeros((2, 8, LANES), jnp.float32)
     clear_ghosts(g, cs, 8)
-    if not received:
-        enter_edges = [
-            pltpu.make_async_copy(ef_in, ef, sem_base.at[0]),
-            pltpu.make_async_copy(zf_in, zf, sem_base.at[1]),
-        ]
-        for copy in enter_edges:
-            copy.start()
     fill_state(g, us, row_ref, halos)
     cell_pass(g, us, row_ref, own, sem, cf)
     for copy in row_copies(g, cot, cs, sem_cot):
@@ -651,9 +643,6 @@
 
     if received:
         edge_pass(g, row_ref, rc, cs, 5, ef, zf)
-    else:
-        for copy in enter_edges:
-            copy.wait()
 
     size = cols
     load = loader(size)
@@ -838,6 +827,18 @@
         return carry
 
     lax.fori_loop(0, rows, give, 0)
+    if received:
+        for e, j in enumerate((0, 1, 2, rows - 1)):
+            for c in range(8):
+                edge[c, e] = stage[c, j]
+
+        def strips(e, carry):
+            for c in range(8):
+                left[c, e] = stage[c, e + 3, 0:8, :]
+                right[c, e] = stage[c, e + 3, cols - 8 : cols, :]
+            return carry
+
+        lax.fori_loop(0, rows - 4, strips, 0)
     for ref, k in ((gphlo, -1), (gphhi, cols)):
         for c in range(6):
             ref[c] = join(column_of(g, us, c, k))
@@ -973,9 +974,9 @@
     to_right[10:20, :] = high(9, slice(9, 19))
 
 
-def finish_kernel(
-    g, row_ref, part, ahead, behind, from_right, from_left, lines_right, lines_left, out, edge, left, right, sem
-):
+def finish_kernel(g, row_ref, part, *refs):
+    given, refs = refs[:3], refs[3:]
+    ahead, behind, from_right, from_left, lines_right, lines_left, out, edge, left, right, sem = refs
     rows, cols = g.rows, g.cols
     inner = pl.ds(3, rows - 4)
     places = (
@@ -984,14 +985,11 @@
         ((slice(None), inner, pl.ds(0, 8)), left),
         ((slice(None), inner, pl.ds(cols - 8, 8)), right),
     )
-    enter = [pltpu.make_async_copy(part.at[at], ref, sem.at[i]) for i, (at, ref) in enumerate(places)]
-    leave = [pltpu.make_async_copy(ref, out.at[at], sem.at[4 + i]) for i, (at, ref) in enumerate(places)]
-    for copy in enter:
-        copy.start()
+    leave = [pltpu.make_async_copy(ref, out.at[at], sem.at[i]) for i, (at, ref) in enumerate(places)]
+    for c in range(8):
+        edge[c] = given[0][c]
     low, high = picker(g, row_ref, ahead, behind)
     bottom = row_ref[g.flags + BOTTOM]
-    for copy in enter[:2]:
-        copy.wait()
     for c in range(8):
         edge[c, 0] += 0.5 * low(c)
         edge[c, 3] += 0.5 * high(c)
@@ -1016,10 +1014,11 @@
         columns(edge, edge, e, j)
     for copy in leave[:2]:
         copy.start()
-    for copy in enter[2:]:
-        copy.wait()
 
     def step(e, carry):
+        for c in range(8):
+            left[c, e] = given[1][c, e]
+            right[c, e] = given[2][c, e]
         columns(left, right, e, e + 3)
         return carry
 
@@ -1052,6 +1051,11 @@
     return [pltpu.VMEM(s, jnp.float32) for s in shapes]
 
 
+def rim_shapes(g):
+    strip = (8, g.rows - 4, 8, g.rads)
+    return [(8, 4, g.cols, g.rads), strip, strip]
+
+
 def sizes(g):
     return (
         (8, g.rows, g.cols, g.rads),
@@ -1077,12 +1081,12 @@
     shape, sides, body, lines = sizes(g)
     message = (10, g.cols, g.rads)
     outs = [(ANY, shape)] + [(VMEM, s) for s in sides + [message, message]]
+    if received:
+        outs += [(VMEM, s) for s in rim_shapes(g)]
     scratch = buffers(
         (8, 2, n, LANES),
         (8, 2, n, LANES),
         (13, 2, n, LANES),
-        (3, 2, n, LANES),
-        (2, n, LANES),
         (11, 2, g.cols, LANES),
         (11, 2, 8 + g.cols, LANES),
         shape,
@@ -1090,18 +1094,19 @@
         (8, 2, g.rows, LANES),
         (g.rows, LANES),
     )
+    if received:
+        scratch += buffers((3, 2, n, LANES), (2, n, LANES))
     dma = pltpu.SemaphoreType.DMA
     scratch += [dma((g.rows, 2)), dma((g.rows, 2)), dma((g.rows,)), dma((g.rows,))]
-    ins = [ANY, ANY] + [VMEM] * 7 + ([ANY] + [VMEM] * 6 if received else [ANY, ANY])
+    ins = [ANY, ANY] + [VMEM] * 7 + ([ANY] + [VMEM] * 6 if received else [VMEM] * 2)
     run = call(functools.partial(adjoint_kernel, g, received), ins, outs, scratch, 3 * 10**8, 48, interpret)
     return run(table, own, cot, *halos, planes, *more)
 
 
 def edges_of(g, table, cot, planes):
     n = g.slots
-    outs = [(ANY, (3, 2, n, LANES)), (ANY, (2, n, LANES))]
-    scratch = buffers((3, 2, n, LANES), *[s for _, s in outs])
-    scratch += [pltpu.SemaphoreType.DMA((g.rows, 2)), pltpu.SemaphoreType.DMA((2,))]
+    outs = [(VMEM, (3, 2, n, LANES)), (VMEM, (2, n, LANES))]
+    scratch = buffers((3, 2, n, LANES)) + [pltpu.SemaphoreType.DMA((g.rows, 2))]
     return call(functools.partial(edge_kernel, g), [ANY, VMEM], outs, scratch, 10**8, 16)(table, cot, planes)
 
 
@@ -1127,18 +1132,17 @@
     )
 
 
-def finish(g, table, part, *received):
-    strip = (8, g.rows - 4, 8, g.rads)
+def finish(g, table, part, *more):
     return pl.pallas_call(
         functools.partial(finish_kernel, g),
         out_shape=jax.ShapeDtypeStruct(part.shape, jnp.float32),
-        in_specs=[SMEM, ANY] + [VMEM] * 6,
+        in_specs=[SMEM, ANY] + [VMEM] * 9,
         out_specs=ANY,
         input_output_aliases={1: 0},
-        scratch_shapes=buffers((8, 4, g.cols, g.rads), strip, strip) + [pltpu.SemaphoreType.DMA((8,))],
+        scratch_shapes=buffers(*rim_shapes(g)) + [pltpu.SemaphoreType.DMA((4,))],
         compiler_params=pltpu.CompilerParams(vmem_limit_bytes=44 << 20),
         cost_estimate=pl.CostEstimate(flops=10**6, bytes_accessed=7 << 20, transcendentals=0),
-    )(table, part, *received)
+    )(table, part, *more)
 
 
 class Place:
@@ -1170,9 +1174,14 @@
     place = Place()
     _, rows, cols, rads = state.shape
     g = Grid(rows, cols, rads, rows * place.n_th, cols * place.n_ph)
-    flags = jnp.stack([place.at_bottom, place.at_top, place.near]).astype(jnp.float32)
-    table = lax.dynamic_slice_in_dim(jnp.asarray(g.row_table()), place.th * rows, rows + 5, 0).reshape(-1)
-    table = jnp.concatenate([table, flags])
+    every = g.row_table()
+    tables = np.zeros((2 * place.n_th, g.flags + 3), np.float32)
+    for n in range(2 * place.n_th):
+        t = n // 2
+        tables[n, : g.flags] = every[t * rows : t * rows + rows + 5].reshape(-1)
+        tables[n, g.flags :] = (t == 0, t == place.n_th - 1, n % 2)
+    which = 2 * place.th + place.near.astype(jnp.int32)
+    table = lax.dynamic_index_in_dim(jnp.asarray(tables), which, 0, keepdims=False)
     planes = jnp.asarray(g.radial_planes())
 
     def halos_of(rims, beside=None):
@@ -1201,7 +1210,7 @@
     part, *ghosts = adjoint(g, table, moved, halos_one, cotangent, planes, edges, False)
     more = (cotangent,) + give_back(ghosts)
     part, *ghosts = adjoint(g, table, state, halos_zero, part, planes, more, True)
-    return finish(g, table, part, *give_back(ghosts))
+    return finish(g, table, part, *ghosts[4:], *give_back(ghosts[:4]))
 
 
 def solution(mesh):

time: 139 us -> 139 us (level)
  local copies, waits for them, and re-layouts: 1.74 us -> 3.66 us
    pallas_call x1, Pallas kernels: 4.54 us -> 2.9 us  [finish(): pl.pallas_call(functools.partial(finish_kernel, g), out_shape=jax.ShapeDt...]
where the time goes in v5:
time: 139 us
  Pallas kernels  83.5 us (60%)
  starting transfers between devices  27.2 us (20%)
  waiting for transfers between devices  24.1 us (17%)
  local copies, waits for them, and re-layouts  3.66 us (3%)
    pallas_call x2, Pallas kernels, adjoint(): return run(table, own, cot, *halos, planes, *more)  52.1 us
    pallas_call x1, Pallas kernels, forward(): return run(table, own, *halos, planes)  15.9 us
    ppermute x6, starting transfers between devices, sideways(): lax.ppermute(to_left, 'ph', self.left)  13.3 us
    ppermute x6, waiting for transfers between devices, sideways(): lax.ppermute(to_right, 'ph', self.right)  10 us
    ppermute x6, starting transfers between devices, polar(): lax.ppermute(ahead, both, self.round)  9.28 us
    ppermute x6, waiting for transfers between devices, polar(): lax.ppermute(ahead, both, self.round)  7.78 us
    pallas_call x1, Pallas kernels, edges_of(): call(functools.partial(edge_kernel, g), [ANY, VMEM], outs, scratch, 10 **...  6.08 us
    ppermute x6, waiting for transfers between devices, polar(): lax.ppermute(behind, both, self.back)  4.6 us
  transfers between devices with their start and end apart: 24, of which 15 were waited for; matrix products, arithmetic and copies ran while one was open for 0% of the time, Pallas kernels for 6%

profile of v5, /device:TPU:0, one launch (start us, length us, event | category | flops | bytes accessed | tf_op | source)
XLA Modules:
  0.0 138.7 jit_solution(10371845273719321055)
XLA Ops:
  0.0 1.4 %constant_dynamic-slice_fusion = f32[1,177]{1,0:T(1,128)} fusion(f32[8,177]{1,0:T(8,128)} %constant.22.clone, s32[]{:T(128)S(6)} %select_n.4), kind=kLoop, calls=%fused_computation | loop fusion | bytes 1420 | tf_op jit(solution)/shard_map/jit(dynamic_index_in_dim)/dynamic_slice | solution.py:1184
  1.4 4.2 %shard_map.46 = (f32[8,24,256]{2,1,0:T(8,128)}, f32[9,24,256]{2,1,0:T(8,128)}, f32[9,24,256]{2,1,0:T(8,128)}, f32[9,24,256]{2,1,0:T(8,128)}) custom-call(f32[177]{0:T(256)} %bitcast.1, f32[8,24,24,256]{3,2,1,0:T(8,128)} %own.3), custom_call_target="tpu_custom_call" | custom-call | flops 1000000 | bytes 16777216 | tf_op jit(solution)/shard_map/pallas_call | solution.py:1118
  5.7 3.4 %collective-permute-start.1 = (f32[9,24,256]{2,1,0:T(8,128)}, f32[9,24,256]{2,1,0:T(8,128)S(1)}, u32[]{:S(2)}, u32[]{:S(2)}) collective-permute-start(f32[9,24,256]{2,1,0:T(8,128)} %get-tuple-element.43), channel_id=1, source_target_pairs={{1,0},{2,1},{3,2},{4,3},{5,4},{6,5},{7,6},{0,7},{9,8},{10,9},{11,1... | collective-permute-start | bytes 663560 | tf_op jit(solution)/shard_map/ppermute | solution.py:1170
  9.1 1.6 %collective-permute-start.2 = (f32[9,24,256]{2,1,0:T(8,128)}, f32[9,24,256]{2,1,0:T(8,128)S(1)}, u32[]{:S(2)}, u32[]{:S(2)}) collective-permute-start(f32[9,24,256]{2,1,0:T(8,128)} %get-tuple-element.49), channel_id=1, source_target_pairs={{0,8},{4,0},{1,9},{5,1},{2,10},{6,2},{3,11},{7,3},{8,16},{12,4},{9... | collective-permute-start | bytes 663560 | tf_op jit(solution)/shard_map/ppermute | solution.py:1167
  11.1 0.9 copy-done.1
  12.0 6.1 %shard_map.47 = (f32[3,2,960,128]{3,2,1,0:T(8,128)S(1)}, f32[2,960,128]{2,1,0:T(8,128)S(1)}) custom-call(f32[177]{0:T(256)S(1)} %bitcast.2, f32[8,24,24,256]{3,2,1,0:T(8,128)S(1)} %copy-done, f32[13,2,8,128]{3,2,1,0:T(8,128)S(1)} %copy-done.1), custom_call_target="tpu_custom_call" | custom-call | flops 100000000 | bytes 16777216 | tf_op jit(solution)/shard_map/pallas_call | solution.py:1110
  18.7 1.6 %collective-permute-start.4 = (f32[24,256]{1,0:T(8,128)S(1)}, f32[24,256]{1,0:T(8,128)S(1)}, u32[]{:S(2)}, u32[]{:S(2)}) collective-permute-start(f32[24,256]{1,0:T(8,128)S(1)} %get-tuple-element.51), channel_id=1, source_target_pairs={{0,8},{4,0},{1,9},{5,1},{2,10},{6,2},{3,11},{7,3},{8,16},{12,4},{9... | collective-permute-start | bytes 73736 | tf_op jit(solution)/shard_map/ppermute | solution.py:1167
  20.8 1.8 %collective-permute-done.4.refs_4_ = f32[24,256]{1,0:T(8,128)S(1)} collective-permute-done((f32[24,256]{1,0:T(8,128)S(1)}, f32[24,256]{1,0:T(8,128)S(1)}, u32[]{:S(2)}, u32[]{:S(2)}) %collective-permute-start.4) | collective-permute-done | bytes 24608 | tf_op jit(solution)/shard_map/ppermute | solution.py:1167
  22.6 1.6 %collective-permute-done.5.refs_5_ = f32[24,256]{1,0:T(8,128)S(1)} collective-permute-done((f32[24,256]{1,0:T(8,128)S(1)}, f32[24,256]{1,0:T(8,128)S(1)}, u32[]{:S(2)}, u32[]{:S(2)}) %collective-permute-start.5) | collective-permute-done | bytes 24608 | tf_op jit(solution)/shard_map/ppermute | solution.py:1167
  24.1 15.9 %shard_map.49 = (f32[8,24,24,256]{3,2,1,0:T(8,128)}, f32[8,24,256]{2,1,0:T(8,128)S(1)}, f32[9,24,256]{2,1,0:T(8,128)S(1)}, f32[9,24,256]{2,1,0:T(8,128)S(1)}, f32[9,24,256]{2,1,0:T(8,128)S(1)}) custom-call(f32[177]{0:T(256)S(1)} %bitcast.4, f32[8,24,24,256]{3,2,1,0:T(8,128)} %own.3, f32[8,24,256]{2,1,0:T(8,128)S(1)} %collective-permute-done.phlo.refs_0_, ...), custom_call_target="tpu_custom_call" | custom-call | flops 100000000 | bytes 16777216 | tf_op jit(solution)/shard_map/pallas_call | solution.py:1076
  40.6 1.6 %collective-permute-start.8 = (f32[9,24,256]{2,1,0:T(8,128)S(1)}, f32[9,24,256]{2,1,0:T(8,128)S(1)}, u32[]{:S(2)}, u32[]{:S(2)}) collective-permute-start(f32[9,24,256]{2,1,0:T(8,128)S(1)} %get-tuple-element.56), channel_id=1, source_target_pairs={{0,8},{4,0},{1,9},{5,1},{2,10},{6,2},{3,11},{7,3},{8,16},{12,4},{9... | collective-permute-start | bytes 663560 | tf_op jit(solution)/shard_map/ppermute | solution.py:1167
  42.6 3.7 %collective-permute-done.6.phlo.refs_0_ = f32[8,24,256]{2,1,0:T(8,128)S(1)} collective-permute-done((f32[8,24,256]{2,1,0:T(8,128)S(1)}, f32[8,24,256]{2,1,0:T(8,128)S(1)}, u32[]{:S(2)}, u32[]{:S(2)}) %collective-permute-start.6) | collective-permute-done | bytes 196640 | tf_op jit(solution)/shard_map/ppermute | solution.py:1170
  46.9 1.5 %collective-permute-start.10 = (f32[24,256]{1,0:T(8,128)S(1)}, f32[24,256]{1,0:T(8,128)S(1)}, u32[]{:S(2)}, u32[]{:S(2)}) collective-permute-start(f32[24,256]{1,0:T(8,128)S(1)} %get-tuple-element.58), channel_id=1, source_target_pairs={{0,8},{4,0},{1,9},{5,1},{2,10},{6,2},{3,11},{7,3},{8,16},{12,4},{9... | collective-permute-start | bytes 73736 | tf_op jit(solution)/shard_map/ppermute | solution.py:1167
  49.0 1.3 collective-permute-done.8.refs_2_
  50.8 1.4 %collective-permute-done.11.refs_5_ = f32[24,256]{1,0:T(8,128)S(1)} collective-permute-done((f32[24,256]{1,0:T(8,128)S(1)}, f32[24,256]{1,0:T(8,128)S(1)}, u32[]{:S(2)}, u32[]{:S(2)}) %collective-permute-start.11) | collective-permute-done | bytes 24608 | tf_op jit(solution)/shard_map/ppermute | solution.py:1167
  52.2 22.9 %shard_map.51 = (f32[8,24,24,256]{3,2,1,0:T(8,128)}, f32[8,24,256]{2,1,0:T(8,128)S(1)}, f32[9,24,256]{2,1,0:T(8,128)S(1)}, f32[10,24,256]{2,1,0:T(8,128)S(1)}, f32[10,24,256]{2,1,0:T(8,128)S(1)}) custom-call(f32[177]{0:T(256)S(1)} %bitcast.6, f32[8,24,24,256]{3,2,1,0:T(8,128)} %get-tuple-element.53.own, f32[8,24,24,256]{3,2,1,0:T(8,128)} %refs_7_.1, ...), custom_call_target="tpu_custom_call" | custom-call | flops 300000000 | bytes 16777216 | tf_op jit(solution)/shard_map/pallas_call | solution.py:1103
  75.1 1.6 %collective-permute-start.12 = (f32[10,24,256]{2,1,0:T(8,128)S(1)}, f32[10,24,256]{2,1,0:T(8,128)S(1)}, u32[]{:S(2)}, u32[]{:S(2)}) collective-permute-start(f32[10,24,256]{2,1,0:T(8,128)S(1)} %get-tuple-element.63), channel_id=1, source_target_pairs={{0,8},{4,0},{1,9},{5,1},{2,10},{6,2},{3,11},{7,3},{8,16},{12,4},{9... | collective-permute-start | bytes 737288 | tf_op jit(solution)/shard_map/ppermute | solution.py:1167
  77.2 2.6 %collective-permute-start.14 = (f32[8,24,256]{2,1,0:T(8,128)S(1)}, f32[8,24,256]{2,1,0:T(8,128)S(1)}, u32[]{:S(2)}, u32[]{:S(2)}) collective-permute-start(f32[8,24,256]{2,1,0:T(8,128)S(1)} %get-tuple-element.65), channel_id=1, source_target_pairs={{1,0},{2,1},{3,2},{4,3},{5,4},{6,5},{7,6},{0,7},{9,8},{10,9},{11,1... | collective-permute-start | bytes 589832 | tf_op jit(solution)/shard_map/ppermute | solution.py:1170
  79.8 2.4 %collective-permute-done.12.ahead.refs_8_ = f32[10,24,256]{2,1,0:T(8,128)S(1)} collective-permute-done((f32[10,24,256]{2,1,0:T(8,128)S(1)}, f32[10,24,256]{2,1,0:T(8,128)S(1)}, u32[]{:S(2)}, u32[]{:S(2)}) %collective-permute-start.12) | collective-permute-done | bytes 245792 | tf_op jit(solution)/shard_map/ppermute | solution.py:1167
  82.2 1.1 collective-permute-done.13.behind.refs_9_
  84.4 0.8 collective-permute-done.15.refs_11_
  85.4 2.9 %collective-permute-done.17.refs_13_ = f32[24,256]{1,0:T(8,128)S(1)} collective-permute-done((f32[24,256]{1,0:T(8,128)S(1)}, f32[24,256]{1,0:T(8,128)S(1)}, u32[]{:S(2)}, u32[]{:S(2)}) %collective-permute-start.17) | collective-permute-done | bytes 24608 | tf_op jit(solution)/shard_map/ppermute | solution.py:1170
  88.3 29.2 %shard_map.53 = (f32[8,24,24,256]{3,2,1,0:T(8,128)}, f32[8,24,256]{2,1,0:T(8,128)S(1)}, f32[9,24,256]{2,1,0:T(8,128)S(1)}, f32[10,24,256]{2,1,0:T(8,128)S(1)}, f...) custom-call(f32[177]{0:T(256)S(1)} %bitcast.8, ...), custom_call_target="tpu_custom_call" | custom-call | flops 300000000 | bytes 16777216 | tf_op jit(solution)/shard_map/pallas_call | solution.py:1103
  117.5 1.4 %collective-permute-start.18 = (f32[10,24,256]{2,1,0:T(8,128)S(1)}, f32[10,24,256]{2,1,0:T(8,128)S(1)}, u32[]{:S(2)}, u32[]{:S(2)}) collective-permute-start(f32[10,24,256]{2,1,0:T(8,128)S(1)} %get-tuple-element.73), channel_id=1, source_target_pairs={{0,8},{4,0},{1,9},{5,1},{2,10},{6,2},{3,11},{7,3},{8,16},{12,4},{9... | collective-permute-start | bytes 737288 | tf_op jit(solution)/shard_map/ppermute | solution.py:1167
  118.9 1.2 collective-permute-start.19
  120.1 2.6 %collective-permute-start.20 = (f32[8,24,256]{2,1,0:T(8,128)S(1)}, f32[8,24,256]{2,1,0:T(8,128)S(1)}, u32[]{:S(2)}, u32[]{:S(2)}) collective-permute-start(f32[8,24,256]{2,1,0:T(8,128)S(1)} %get-tuple-element.75), channel_id=1, source_target_pairs={{1,0},{2,1},{3,2},{4,3},{5,4},{6,5},{7,6},{0,7},{9,8},{10,9},{11,1... | collective-permute-start | bytes 589832 | tf_op jit(solution)/shard_map/ppermute | solution.py:1170
  122.7 1.8 %collective-permute-done.18.ahead.refs_3_ = f32[10,24,256]{2,1,0:T(8,128)S(1)} collective-permute-done((f32[10,24,256]{2,1,0:T(8,128)S(1)}, f32[10,24,256]{2,1,0:T(8,128)S(1)}, u32[]{:S(2)}, u32[]{:S(2)}) %collective-permute-start.18) | collective-permute-done | bytes 245792 | tf_op jit(solution)/shard_map/ppermute | solution.py:1167
  125.6 4.5 %collective-permute-start.22 = (f32[24,256]{1,0:T(8,128)S(1)}, f32[24,256]{1,0:T(8,128)S(1)}, u32[]{:S(2)}, u32[]{:S(2)}) collective-permute-start(f32[24,256]{1,0:T(8,128)S(1)} %get-tuple-element.77), channel_id=1, source_target_pairs={{1,0},{2,1},{3,2},{4,3},{5,4},{6,5},{7,6},{0,7},{9,8},{10,9},{11,1... | collective-permute-start | bytes 73736 | tf_op jit(solution)/shard_map/ppermute | solution.py:1170
  130.2 1.5 %collective-permute-done.22.refs_7_ = f32[24,256]{1,0:T(8,128)S(1)} collective-permute-done((f32[24,256]{1,0:T(8,128)S(1)}, f32[24,256]{1,0:T(8,128)S(1)}, u32[]{:S(2)}, u32[]{:S(2)}) %collective-permute-start.22) | collective-permute-done | bytes 24608 | tf_op jit(solution)/shard_map/ppermute | solution.py:1170
  131.7 2.6 %collective-permute-done.23.refs_8_ = f32[24,256]{1,0:T(8,128)S(1)} collective-permute-done((f32[24,256]{1,0:T(8,128)S(1)}, f32[24,256]{1,0:T(8,128)S(1)}, u32[]{:S(2)}, u32[]{:S(2)}) %collective-permute-start.23) | collective-permute-done | bytes 24608 | tf_op jit(solution)/shard_map/ppermute | solution.py:1170
  134.3 1.3 copy-done.2
  135.6 2.9 %shard_map.55 = f32[8,24,24,256]{3,2,1,0:T(8,128)} custom-call(f32[177]{0:T(256)S(1)} %bitcast.10, f32[8,24,24,256]{3,2,1,0:T(8,128)} %get-tuple-element.69.part, f32[8,4,24,256]{3,2,1,0:T(8,128)S(1)} %get-tuple-element.70.refs_0_, f32[8,20,8,256]{3,2,1,0:T(8,128)S(1)} %get-tuple-element.71.refs_1_, ...), custom_call_target="tpu_custom_call", output_to_operand_aliasing={{}: (1, {})} | custom-call | flops 1000000 | bytes 7340032 | tf_op jit(solution)/shard_map/pallas_call | solution.py:1136
  (35 shorter events, 7.0 us)
Async XLA Ops:
  0.0 11.1 %copy-start = (f32[8,24,24,256]{3,2,1,0:T(8,128)S(1)}, f32[8,24,24,256]{3,2,1,0:T(8,128)}, u32[]{:S(2)}) copy-start(f32[8,24,24,256]{3,2,1,0:T(8,128)} %refs_7_.1) | copy-start | bytes 14155780
  1.4 9.6 %copy-start.3 = (f32[1,177]{1,0:T(1,128)S(1)}, f32[1,177]{1,0:T(1,128)}, u32[]{:S(2)}) copy-start(f32[1,177]{1,0:T(1,128)} %constant_dynamic-slice_fusion) | copy-start | bytes 2128
  5.7 12.4 %collective-permute-start.1 = (f32[9,24,256]{2,1,0:T(8,128)}, f32[9,24,256]{2,1,0:T(8,128)S(1)}, u32[]{:S(2)}, u32[]{:S(2)}) collective-permute-start(f32[9,24,256]{2,1,0:T(8,128)} %get-tuple-element.43), channel_id=1, source_target_pairs={{1,0},{2,1},{3,2},{4,3},{5,4},{6,5},{7,6},{0,7},{9,8},{10,9},{11,1... | collective-permute-start | bytes 663560 | tf_op jit(solution)/shard_map/ppermute | solution.py:1170
  9.0 9.0 %collective-permute-start = (f32[8,24,256]{2,1,0:T(8,128)}, f32[8,24,256]{2,1,0:T(8,128)S(1)}, u32[]{:S(2)}, u32[]{:S(2)}) collective-permute-start(f32[8,24,256]{2,1,0:T(8,128)} %get-tuple-element.42), channel_id=1, source_target_pairs={{0,1},{1,2},{2,3},{3,4},{4,5},{5,6},{6,7},{7,0},{8,9},{9,10},{10,1... | collective-permute-start | bytes 589832 | tf_op jit(solution)/shard_map/ppermute | solution.py:1170
  9.1 11.7 %collective-permute-start.2 = (f32[9,24,256]{2,1,0:T(8,128)}, f32[9,24,256]{2,1,0:T(8,128)S(1)}, u32[]{:S(2)}, u32[]{:S(2)}) collective-permute-start(f32[9,24,256]{2,1,0:T(8,128)} %get-tuple-element.49), channel_id=1, source_target_pairs={{0,8},{4,0},{1,9},{5,1},{2,10},{6,2},{3,11},{7,3},{8,16},{12,4},{9... | collective-permute-start | bytes 663560 | tf_op jit(solution)/shard_map/ppermute | solution.py:1167
  10.6 10.1 %collective-permute-start.3 = (f32[9,24,256]{2,1,0:T(8,128)}, f32[9,24,256]{2,1,0:T(8,128)S(1)}, u32[]{:S(2)}, u32[]{:S(2)}) collective-permute-start(f32[9,24,256]{2,1,0:T(8,128)} %get-tuple-element.50), channel_id=1, source_target_pairs={{8,0},{0,4},{9,1},{1,5},{10,2},{2,6},{11,3},{3,7},{16,8},{4,12},{1... | collective-permute-start | bytes 663560 | tf_op jit(solution)/shard_map/ppermute | solution.py:1167
  11.1 0.9 copy-start.1
  18.7 3.9 %collective-permute-start.4 = (f32[24,256]{1,0:T(8,128)S(1)}, f32[24,256]{1,0:T(8,128)S(1)}, u32[]{:S(2)}, u32[]{:S(2)}) collective-permute-start(f32[24,256]{1,0:T(8,128)S(1)} %get-tuple-element.51), channel_id=1, source_target_pairs={{0,8},{4,0},{1,9},{5,1},{2,10},{6,2},{3,11},{7,3},{8,16},{12,4},{9... | collective-permute-start | bytes 73736 | tf_op jit(solution)/shard_map/ppermute | solution.py:1167
  20.3 3.8 %collective-permute-start.5 = (f32[24,256]{1,0:T(8,128)S(1)}, f32[24,256]{1,0:T(8,128)S(1)}, u32[]{:S(2)}, u32[]{:S(2)}) collective-permute-start(f32[24,256]{1,0:T(8,128)S(1)} %get-tuple-element.52), channel_id=1, source_target_pairs={{8,0},{0,4},{9,1},{1,5},{10,2},{2,6},{11,3},{3,7},{16,8},{4,12},{1... | collective-permute-start | bytes 73736 | tf_op jit(solution)/shard_map/ppermute | solution.py:1167
  40.0 6.3 %collective-permute-start.7 = (f32[9,24,256]{2,1,0:T(8,128)S(1)}, f32[9,24,256]{2,1,0:T(8,128)S(1)}, u32[]{:S(2)}, u32[]{:S(2)}) collective-permute-start(f32[9,24,256]{2,1,0:T(8,128)S(1)} %get-tuple-element.55), channel_id=1, source_target_pairs={{1,0},{2,1},{3,2},{4,3},{5,4},{6,5},{7,6},{0,7},{9,8},{10,9},{11,1... | collective-permute-start | bytes 663560 | tf_op jit(solution)/shard_map/ppermute | solution.py:1170
  40.1 6.2 %collective-permute-start.6 = (f32[8,24,256]{2,1,0:T(8,128)S(1)}, f32[8,24,256]{2,1,0:T(8,128)S(1)}, u32[]{:S(2)}, u32[]{:S(2)}) collective-permute-start(f32[8,24,256]{2,1,0:T(8,128)S(1)} %get-tuple-element.54), channel_id=1, source_target_pairs={{0,1},{1,2},{2,3},{3,4},{4,5},{5,6},{6,7},{7,0},{8,9},{9,10},{10,1... | collective-permute-start | bytes 589832 | tf_op jit(solution)/shard_map/ppermute | solution.py:1170
  40.6 9.7 %collective-permute-start.8 = (f32[9,24,256]{2,1,0:T(8,128)S(1)}, f32[9,24,256]{2,1,0:T(8,128)S(1)}, u32[]{:S(2)}, u32[]{:S(2)}) collective-permute-start(f32[9,24,256]{2,1,0:T(8,128)S(1)} %get-tuple-element.56), channel_id=1, source_target_pairs={{0,8},{4,0},{1,9},{5,1},{2,10},{6,2},{3,11},{7,3},{8,16},{12,4},{9... | collective-permute-start | bytes 663560 | tf_op jit(solution)/shard_map/ppermute | solution.py:1167
  42.2 8.1 %collective-permute-start.9 = (f32[9,24,256]{2,1,0:T(8,128)S(1)}, f32[9,24,256]{2,1,0:T(8,128)S(1)}, u32[]{:S(2)}, u32[]{:S(2)}) collective-permute-start(f32[9,24,256]{2,1,0:T(8,128)S(1)} %get-tuple-element.57), channel_id=1, source_target_pairs={{8,0},{0,4},{9,1},{1,5},{10,2},{2,6},{11,3},{3,7},{16,8},{4,12},{1... | collective-permute-start | bytes 663560 | tf_op jit(solution)/shard_map/ppermute | solution.py:1167
  46.9 3.9 %collective-permute-start.10 = (f32[24,256]{1,0:T(8,128)S(1)}, f32[24,256]{1,0:T(8,128)S(1)}, u32[]{:S(2)}, u32[]{:S(2)}) collective-permute-start(f32[24,256]{1,0:T(8,128)S(1)} %get-tuple-element.58), channel_id=1, source_target_pairs={{0,8},{4,0},{1,9},{5,1},{2,10},{6,2},{3,11},{7,3},{8,16},{12,4},{9... | collective-permute-start | bytes 73736 | tf_op jit(solution)/shard_map/ppermute | solution.py:1167
  48.4 3.8 %collective-permute-start.11 = (f32[24,256]{1,0:T(8,128)S(1)}, f32[24,256]{1,0:T(8,128)S(1)}, u32[]{:S(2)}, u32[]{:S(2)}) collective-permute-start(f32[24,256]{1,0:T(8,128)S(1)} %get-tuple-element.59), channel_id=1, source_target_pairs={{8,0},{0,4},{9,1},{1,5},{10,2},{2,6},{11,3},{3,7},{16,8},{4,12},{1... | collective-permute-start | bytes 73736 | tf_op jit(solution)/shard_map/ppermute | solution.py:1167
  75.1 7.1 %collective-permute-start.12 = (f32[10,24,256]{2,1,0:T(8,128)S(1)}, f32[10,24,256]{2,1,0:T(8,128)S(1)}, u32[]{:S(2)}, u32[]{:S(2)}) collective-permute-start(f32[10,24,256]{2,1,0:T(8,128)S(1)} %get-tuple-element.63), channel_id=1, source_target_pairs={{0,8},{4,0},{1,9},{5,1},{2,10},{6,2},{3,11},{7,3},{8,16},{12,4},{9... | collective-permute-start | bytes 737288 | tf_op jit(solution)/shard_map/ppermute | solution.py:1167
  76.8 6.5 %collective-permute-start.13 = (f32[10,24,256]{2,1,0:T(8,128)S(1)}, f32[10,24,256]{2,1,0:T(8,128)S(1)}, u32[]{:S(2)}, u32[]{:S(2)}) collective-permute-start(f32[10,24,256]{2,1,0:T(8,128)S(1)} %get-tuple-element.64), channel_id=1, source_target_pairs={{8,0},{0,4},{9,1},{1,5},{10,2},{2,6},{11,3},{3,7},{16,8},{4,12},{1... | collective-permute-start | bytes 737288 | tf_op jit(solution)/shard_map/ppermute | solution.py:1167
  77.2 8.0 %collective-permute-start.15 = (f32[9,24,256]{2,1,0:T(8,128)S(1)}, f32[9,24,256]{2,1,0:T(8,128)S(1)}, u32[]{:S(2)}, u32[]{:S(2)}) collective-permute-start(f32[9,24,256]{2,1,0:T(8,128)S(1)} %get-tuple-element.66), channel_id=1, source_target_pairs={{0,1},{1,2},{2,3},{3,4},{4,5},{5,6},{6,7},{7,0},{8,9},{9,10},{10,1... | collective-permute-start | bytes 663560 | tf_op jit(solution)/shard_map/ppermute | solution.py:1170
  77.2 7.2 %collective-permute-start.14 = (f32[8,24,256]{2,1,0:T(8,128)S(1)}, f32[8,24,256]{2,1,0:T(8,128)S(1)}, u32[]{:S(2)}, u32[]{:S(2)}) collective-permute-start(f32[8,24,256]{2,1,0:T(8,128)S(1)} %get-tuple-element.65), channel_id=1, source_target_pairs={{1,0},{2,1},{3,2},{4,3},{5,4},{6,5},{7,6},{0,7},{9,8},{10,9},{11,1... | collective-permute-start | bytes 589832 | tf_op jit(solution)/shard_map/ppermute | solution.py:1170
  83.9 1.6 %collective-permute-start.16 = (f32[24,256]{1,0:T(8,128)S(1)}, f32[24,256]{1,0:T(8,128)S(1)}, u32[]{:S(2)}, u32[]{:S(2)}) collective-permute-start(f32[24,256]{1,0:T(8,128)S(1)} %get-tuple-element.67), channel_id=1, source_target_pairs={{1,0},{2,1},{3,2},{4,3},{5,4},{6,5},{7,6},{0,7},{9,8},{10,9},{11,1... | collective-permute-start | bytes 73736 | tf_op jit(solution)/shard_map/ppermute | solution.py:1170
  83.9 4.4 %collective-permute-start.17 = (f32[24,256]{1,0:T(8,128)S(1)}, f32[24,256]{1,0:T(8,128)S(1)}, u32[]{:S(2)}, u32[]{:S(2)}) collective-permute-start(f32[24,256]{1,0:T(8,128)S(1)} %get-tuple-element.68), channel_id=1, source_target_pairs={{0,1},{1,2},{2,3},{3,4},{4,5},{5,6},{6,7},{7,0},{8,9},{9,10},{10,1... | collective-permute-start | bytes 73736 | tf_op jit(solution)/shard_map/ppermute | solution.py:1170
  117.5 7.1 %collective-permute-start.18 = (f32[10,24,256]{2,1,0:T(8,128)S(1)}, f32[10,24,256]{2,1,0:T(8,128)S(1)}, u32[]{:S(2)}, u32[]{:S(2)}) collective-permute-start(f32[10,24,256]{2,1,0:T(8,128)S(1)} %get-tuple-element.73), channel_id=1, source_target_pairs={{0,8},{4,0},{1,9},{5,1},{2,10},{6,2},{3,11},{7,3},{8,16},{12,4},{9... | collective-permute-start | bytes 737288 | tf_op jit(solution)/shard_map/ppermute | solution.py:1167
  118.9 6.2 %collective-permute-start.19 = (f32[10,24,256]{2,1,0:T(8,128)S(1)}, f32[10,24,256]{2,1,0:T(8,128)S(1)}, u32[]{:S(2)}, u32[]{:S(2)}) collective-permute-start(f32[10,24,256]{2,1,0:T(8,128)S(1)} %get-tuple-element.74), channel_id=1, source_target_pairs={{8,0},{0,4},{9,1},{1,5},{10,2},{2,6},{11,3},{3,7},{16,8},{4,12},{1... | collective-permute-start | bytes 737288 | tf_op jit(solution)/shard_map/ppermute | solution.py:1167
  120.1 10.1 %collective-permute-start.21 = (f32[9,24,256]{2,1,0:T(8,128)S(1)}, f32[9,24,256]{2,1,0:T(8,128)S(1)}, u32[]{:S(2)}, u32[]{:S(2)}) collective-permute-start(f32[9,24,256]{2,1,0:T(8,128)S(1)} %get-tuple-element.76), channel_id=1, source_target_pairs={{0,1},{1,2},{2,3},{3,4},{4,5},{5,6},{6,7},{7,0},{8,9},{9,10},{10,1... | collective-permute-start | bytes 663560 | tf_op jit(solution)/shard_map/ppermute | solution.py:1170
  120.1 10.1 %collective-permute-start.20 = (f32[8,24,256]{2,1,0:T(8,128)S(1)}, f32[8,24,256]{2,1,0:T(8,128)S(1)}, u32[]{:S(2)}, u32[]{:S(2)}) collective-permute-start(f32[8,24,256]{2,1,0:T(8,128)S(1)} %get-tuple-element.75), channel_id=1, source_target_pairs={{1,0},{2,1},{3,2},{4,3},{5,4},{6,5},{7,6},{0,7},{9,8},{10,9},{11,1... | collective-permute-start | bytes 589832 | tf_op jit(solution)/shard_map/ppermute | solution.py:1170
  125.6 6.0 %collective-permute-start.22 = (f32[24,256]{1,0:T(8,128)S(1)}, f32[24,256]{1,0:T(8,128)S(1)}, u32[]{:S(2)}, u32[]{:S(2)}) collective-permute-start(f32[24,256]{1,0:T(8,128)S(1)} %get-tuple-element.77), channel_id=1, source_target_pairs={{1,0},{2,1},{3,2},{4,3},{5,4},{6,5},{7,6},{0,7},{9,8},{10,9},{11,1... | collective-permute-start | bytes 73736 | tf_op jit(solution)/shard_map/ppermute | solution.py:1170
  130.2 4.2 %collective-permute-start.23 = (f32[24,256]{1,0:T(8,128)S(1)}, f32[24,256]{1,0:T(8,128)S(1)}, u32[]{:S(2)}, u32[]{:S(2)}) collective-permute-start(f32[24,256]{1,0:T(8,128)S(1)} %get-tuple-element.78), channel_id=1, source_target_pairs={{0,1},{1,2},{2,3},{3,4},{4,5},{5,6},{6,7},{7,0},{8,9},{9,10},{10,1... | collective-permute-start | bytes 73736 | tf_op jit(solution)/shard_map/ppermute | solution.py:1170
  134.3 1.3 copy-start.2
